TPU v7x, 32 devices: a whole 2x2x4 slice. The times are simulated.
32 devices in a mesh: dp: 8 (over y, x, core), seq: 4 (over z).
Axes of the slice: x: 2, y: 2, z: 4, core: 2. Of those that a mesh axis runs over, the one named last changes fastest.
Arguments:
- patches: bfloat16 [16, 1024, 1152], P('dp', 'seq'), may hold values from -6 to 6
- picture_ids: int32 [16, 1024], P('dp'), may hold values from 0 to 11, as said below
- valid_mask: int32 [16, 1024], P('dp'), may hold values from 0 to 1, as said below
- ln1_gain: bfloat16 [1152], P('dp'), may hold values from 0.5 to 1.5
- ln1_bias: bfloat16 [1152], P('dp'), may hold values from -1.1953125 to 1.1953125
- w_qkv: bfloat16 [1152, 3456], P('dp'), may hold values from -0.1875 to 0.1875
- bias_qv: bfloat16 [2, 1152], P(None, 'dp'), may hold values from -1.1953125 to 1.1953125
- w_out: bfloat16 [1152, 1152], P('dp'), may hold values from -0.75 to 0.75
- b_out: bfloat16 [1152], P('dp'), may hold values from -1.1953125 to 1.1953125
- ln2_gain: bfloat16 [1152], P('dp'), may hold values from 0.5 to 1.5
- ln2_bias: bfloat16 [1152], P('dp'), may hold values from -1.1953125 to 1.1953125
- w_fc1: bfloat16 [1152, 4304], P('dp'), may hold values from -0.1875 to 0.1875
- b_fc1: bfloat16 [4304], P('dp'), may hold values from -1.1953125 to 1.1953125
- w_fc2: bfloat16 [4304, 1152], P(None, 'dp'), may hold values from -0.09375 to 0.09375
- b_fc2: bfloat16 [1152], P('dp'), may hold values from -1.1953125 to 1.1953125
- cotangent: bfloat16 [16, 1024, 1152], P('dp', 'seq'), may hold values from -6 to 6
Outputs:
- layer_out: bfloat16 [16, 1024, 1152], P('dp', 'seq')
- grad_patches: bfloat16 [16, 1024, 1152], P('dp', 'seq')
- grad_ln1_gain: float32 [1152], P('dp')
- grad_ln1_bias: float32 [1152], P('dp')
- grad_w_qkv: float32 [1152, 3456], P('dp')
- grad_bias_qv: float32 [2, 1152], P(None, 'dp')
- grad_w_out: float32 [1152, 1152], P('dp')
- grad_b_out: float32 [1152], P('dp')
- grad_ln2_gain: float32 [1152], P('dp')
- grad_ln2_bias: float32 [1152], P('dp')
- grad_w_fc1: float32 [1152, 4304], P('dp')
- grad_b_fc1: float32 [4304], P('dp')
- grad_w_fc2: float32 [4304, 1152], P(None, 'dp')
- grad_b_fc2: float32 [1152], P('dp')
Inputs may be any that keep to these rules, and one draw needn't show every extreme that they name: `picture_ids`: in each row the valid tokens form consecutive pictures of 100 to 512 tokens with ids 0, 1, 2 and so on in order; every row holds one picture of exactly 512 tokens; padding tokens follow the last picture and carry id 11. `valid_mask`: 1 on the tokens of pictures, 0 on the padding that ends a row.
All inputs are finite; a program needn't handle non-finite values.
Results may differ from a plain program's by a relative error of at most 0.017.
Values may be sent and summed in bfloat16 or wider, within the bound.
A program may use at most 256 MiB of HBM per device.

v0:
```python
import jax
import jax.numpy as jnp
from jax import lax
from jax.sharding import PartitionSpec as P

HEADS = 16
HD = 72


epsilon = 1e-06
big_negative = -1e30


def layer_norm(values, scales, offset):
    center = values - jnp.mean(values, axis=-1, keepdims=True)
    spread = jnp.mean(center * center, axis=-1, keepdims=True)
    return center * lax.rsqrt(spread + epsilon) * scales + offset


def gelu_tanh(values):
    return (
        0.5
        * values
        * (1.0 + jnp.tanh(0.7978845608028654 * (values + 0.044715 * values * values * values)))
    )


def contract_rows(left, right):
    return lax.dot_general(
        left, right, (((0,), (0,)), ((), ())), preferred_element_type=jnp.float32
    )


def contract_cols(left, right):
    return lax.dot_general(
        left, right, (((1,), (1,)), ((), ())), preferred_element_type=jnp.float32
    )


def gather_weights(
    ln1_gain, ln1_bias, w_qkv, bias_qv, w_out, b_out, ln2_gain, ln2_bias, w_fc1, b_fc1, w_fc2, b_fc2
):
    return (
        lax.all_gather(ln1_gain, "dp", axis=0, tiled=True),
        lax.all_gather(ln1_bias, "dp", axis=0, tiled=True),
        lax.all_gather(w_qkv, "dp", axis=0, tiled=True),
        lax.all_gather(bias_qv, "dp", axis=1, tiled=True),
        lax.all_gather(w_out, "dp", axis=0, tiled=True),
        lax.all_gather(b_out, "dp", axis=0, tiled=True),
        lax.all_gather(ln2_gain, "dp", axis=0, tiled=True),
        lax.all_gather(ln2_bias, "dp", axis=0, tiled=True),
        lax.all_gather(w_fc1, "dp", axis=0, tiled=True),
        lax.all_gather(b_fc1, "dp", axis=0, tiled=True),
        lax.all_gather(w_fc2, "dp", axis=1, tiled=True),
        lax.all_gather(b_fc2, "dp", axis=0, tiled=True),
    )


def block_scores(queries, key_vectors, picture_ids, valid_mask, first_row, block_rows):
    length = picture_ids.shape[1]
    query_block = lax.dynamic_slice_in_dim(queries, first_row, block_rows, 1)
    ids_block = lax.dynamic_slice_in_dim(picture_ids, first_row, block_rows, 1)
    same_picture = (ids_block[:, :, None] == picture_ids[:, None, :]) & (
        valid_mask[:, None, :] == 1
    )
    diagonal = (first_row + jnp.arange(block_rows))[:, None] == jnp.arange(length)[None, :]
    allowed = (same_picture | diagonal[None])[:, None]
    scaling = queries.shape[-1] ** (-0.5)
    scores = (
        jnp.einsum("rqhe,rkhe->rhqk", query_block, key_vectors, preferred_element_type=jnp.float32)
        * scaling
    )
    return (query_block, jnp.where(allowed, scores, big_negative))


def attention_forward(queries, key_vectors, value_vectors, picture_ids, valid_mask):
    row_count, length, head_count, head_size = queries.shape
    block_rows = min(512, length)

    def one_block(block_index):
        query_block, scores = block_scores(
            queries, key_vectors, picture_ids, valid_mask, block_index * block_rows, block_rows
        )
        row_max = jnp.max(scores, axis=-1, keepdims=True)
        exp_terms = jnp.exp(scores - row_max)
        totals = jnp.sum(exp_terms, axis=-1, keepdims=True)
        probs_low = (exp_terms / totals).astype(jnp.bfloat16)
        mixing = jnp.einsum(
            "rhqk,rkhe->rqhe", probs_low, value_vectors, preferred_element_type=jnp.float32
        )
        return (mixing.astype(jnp.bfloat16), (row_max + jnp.log(totals))[..., 0])

    outputs, log_sums = lax.map(one_block, jnp.arange(length // block_rows))
    outputs = jnp.moveaxis(outputs, 0, 1).reshape(row_count, length, head_count, head_size)
    log_sums = jnp.moveaxis(log_sums, 0, 2).reshape(row_count, head_count, length)
    return (outputs, log_sums)


def attention_backward(
    queries, key_vectors, value_vectors, log_sums, grad_heads, picture_ids, valid_mask
):
    row_count, length, head_count, head_size = queries.shape
    block_rows = min(512, length)
    scaling = head_size ** (-0.5)

    def one_block(running, block_index):
        grad_keys, grad_values = running
        first_row = block_index * block_rows
        query_block, scores = block_scores(
            queries, key_vectors, picture_ids, valid_mask, first_row, block_rows
        )
        lse_block = lax.dynamic_slice_in_dim(log_sums, first_row, block_rows, 2)
        attn_probs = jnp.exp(scores - lse_block[..., None])
        grad_block = lax.dynamic_slice_in_dim(grad_heads, first_row, block_rows, 1)
        grad_values = grad_values + jnp.einsum(
            "rhqk,rqhe->rkhe",
            attn_probs.astype(jnp.bfloat16),
            grad_block,
            preferred_element_type=jnp.float32,
        )
        grad_probs = jnp.einsum(
            "rqhe,rkhe->rhqk", grad_block, value_vectors, preferred_element_type=jnp.float32
        )
        inner = jnp.sum(attn_probs * grad_probs, axis=-1, keepdims=True)
        grad_scores = (attn_probs * (grad_probs - inner)).astype(jnp.bfloat16)
        grad_query = (
            jnp.einsum(
                "rhqk,rkhe->rqhe", grad_scores, key_vectors, preferred_element_type=jnp.float32
            )
            * scaling
        )
        grad_keys = (
            grad_keys
            + jnp.einsum(
                "rhqk,rqhe->rkhe", grad_scores, query_block, preferred_element_type=jnp.float32
            )
            * scaling
        )
        return ((grad_keys, grad_values), grad_query)

    zeros_start = jnp.zeros(queries.shape, jnp.float32)
    (grad_keys, grad_values), grad_queries = lax.scan(
        one_block, (zeros_start, zeros_start), jnp.arange(length // block_rows)
    )
    grad_queries = jnp.moveaxis(grad_queries, 0, 1).reshape(
        row_count, length, head_count, head_size
    )
    return (grad_queries, grad_keys, grad_values)


def forward_pass(patches, picture_ids, valid_mask, gathered):
    (
        ln1_gain,
        ln1_bias,
        w_qkv,
        bias_qv,
        w_out,
        b_out,
        ln2_gain,
        ln2_bias,
        w_fc1,
        b_fc1,
        w_fc2,
        b_fc2,
    ) = gathered
    row_count, local_len, model_width = patches.shape
    inputs = patches.astype(jnp.float32).reshape(row_count * local_len, model_width)
    normed = layer_norm(inputs, ln1_gain.astype(jnp.float32), ln1_bias.astype(jnp.float32)).astype(
        jnp.bfloat16
    )
    projected = jnp.dot(normed, w_qkv, preferred_element_type=jnp.float32)
    bias_full = jnp.concatenate([bias_qv[0], jnp.zeros_like(bias_qv[0]), bias_qv[1]]).astype(
        jnp.float32
    )
    projected = (
        (projected + bias_full).astype(jnp.bfloat16).reshape(row_count, local_len, 3, HEADS, HD)
    )
    by_heads = lax.all_to_all(projected, "seq", split_axis=3, concat_axis=1, tiled=True)
    queries = by_heads[:, :, 0]
    key_vectors = by_heads[:, :, 1]
    value_vectors = by_heads[:, :, 2]
    mixing, log_sums = attention_forward(
        queries, key_vectors, value_vectors, picture_ids, valid_mask
    )
    token_mixing = lax.all_to_all(mixing, "seq", split_axis=1, concat_axis=2, tiled=True)
    attended = token_mixing.reshape(row_count * local_len, model_width)
    middle = (
        inputs
        + jnp.dot(attended, w_out, preferred_element_type=jnp.float32)
        + b_out.astype(jnp.float32)
    )
    normed_two = layer_norm(
        middle, ln2_gain.astype(jnp.float32), ln2_bias.astype(jnp.float32)
    ).astype(jnp.bfloat16)
    hidden = jnp.dot(normed_two, w_fc1, preferred_element_type=jnp.float32) + b_fc1.astype(
        jnp.float32
    )
    active = gelu_tanh(hidden).astype(jnp.bfloat16)
    outputs = (
        middle
        + jnp.dot(active, w_fc2, preferred_element_type=jnp.float32)
        + b_fc2.astype(jnp.float32)
    )
    layer_out = outputs.astype(jnp.bfloat16).reshape(row_count, local_len, model_width)
    kept_values = (
        inputs,
        normed,
        queries,
        key_vectors,
        value_vectors,
        log_sums,
        attended,
        middle,
        normed_two,
        hidden,
        active,
    )
    return (layer_out, kept_values)


def backward_pass(cotangent, picture_ids, valid_mask, gathered, kept_values):
    (
        ln1_gain,
        ln1_bias,
        w_qkv,
        bias_qv,
        w_out,
        b_out,
        ln2_gain,
        ln2_bias,
        w_fc1,
        b_fc1,
        w_fc2,
        b_fc2,
    ) = gathered
    (
        inputs,
        normed,
        queries,
        key_vectors,
        value_vectors,
        log_sums,
        attended,
        middle,
        normed_two,
        hidden,
        active,
    ) = kept_values
    row_count, local_len, model_width = cotangent.shape
    grad_z = cotangent.reshape(row_count * local_len, model_width)
    grad_w_fc2 = contract_rows(active, grad_z)
    grad_b_fc2 = jnp.sum(grad_z.astype(jnp.float32), axis=0)
    grad_active = contract_cols(grad_z, w_fc2)
    grad_hidden = jax.vjp(gelu_tanh, hidden)[1](grad_active)[0].astype(jnp.bfloat16)
    grad_w_fc1 = contract_rows(normed_two, grad_hidden)
    grad_b_fc1 = jnp.sum(grad_hidden.astype(jnp.float32), axis=0)
    grad_normed_two = contract_cols(grad_hidden, w_fc1)
    norm_pull = jax.vjp(
        layer_norm, middle, ln2_gain.astype(jnp.float32), ln2_bias.astype(jnp.float32)
    )[1]
    grad_middle, grad_ln2_gain, grad_ln2_bias = norm_pull(grad_normed_two)
    grad_middle = grad_middle + grad_z.astype(jnp.float32)
    grad_branch = grad_middle.astype(jnp.bfloat16)
    grad_w_out = contract_rows(attended, grad_branch)
    grad_b_out = jnp.sum(grad_branch.astype(jnp.float32), axis=0)
    grad_attended = (
        contract_cols(grad_branch, w_out)
        .astype(jnp.bfloat16)
        .reshape(row_count, local_len, HEADS, HD)
    )
    grad_heads = lax.all_to_all(grad_attended, "seq", split_axis=2, concat_axis=1, tiled=True)
    grad_queries, grad_keys, grad_values = attention_backward(
        queries, key_vectors, value_vectors, log_sums, grad_heads, picture_ids, valid_mask
    )
    grad_proj = jnp.stack([grad_queries, grad_keys, grad_values], axis=2).astype(jnp.bfloat16)
    grad_tokens = lax.all_to_all(grad_proj, "seq", split_axis=1, concat_axis=3, tiled=True).reshape(
        row_count * local_len, 3 * model_width
    )
    grad_w_qkv = contract_rows(normed, grad_tokens)
    column_sums = jnp.sum(grad_tokens.astype(jnp.float32), axis=0)
    grad_bias_qv = jnp.stack([column_sums[:model_width], column_sums[2 * model_width :]])
    grad_normed = contract_cols(grad_tokens, w_qkv)
    first_pull = jax.vjp(
        layer_norm, inputs, ln1_gain.astype(jnp.float32), ln1_bias.astype(jnp.float32)
    )[1]
    grad_inputs, grad_ln1_gain, grad_ln1_bias = first_pull(grad_normed)
    grad_patches = (
        (grad_middle + grad_inputs).astype(jnp.bfloat16).reshape(row_count, local_len, model_width)
    )
    grads = (
        grad_ln1_gain,
        grad_ln1_bias,
        grad_w_qkv,
        grad_bias_qv,
        grad_w_out,
        grad_b_out,
        grad_ln2_gain,
        grad_ln2_bias,
        grad_w_fc1,
        grad_b_fc1,
        grad_w_fc2,
        grad_b_fc2,
    )
    return (grad_patches, grads)


def per_device(
    patches,
    picture_ids,
    valid_mask,
    ln1_gain,
    ln1_bias,
    w_qkv,
    bias_qv,
    w_out,
    b_out,
    ln2_gain,
    ln2_bias,
    w_fc1,
    b_fc1,
    w_fc2,
    b_fc2,
    cotangent,
):
    gathered = gather_weights(
        ln1_gain,
        ln1_bias,
        w_qkv,
        bias_qv,
        w_out,
        b_out,
        ln2_gain,
        ln2_bias,
        w_fc1,
        b_fc1,
        w_fc2,
        b_fc2,
    )
    layer_out, kept_values = forward_pass(patches, picture_ids, valid_mask, gathered)
    grad_patches, grads = backward_pass(cotangent, picture_ids, valid_mask, gathered, kept_values)
    (
        grad_ln1_gain,
        grad_ln1_bias,
        grad_w_qkv,
        grad_bias_qv,
        grad_w_out,
        grad_b_out,
        grad_ln2_gain,
        grad_ln2_bias,
        grad_w_fc1,
        grad_b_fc1,
        grad_w_fc2,
        grad_b_fc2,
    ) = grads
    owned = (
        lax.psum_scatter(
            grad_ln1_gain.astype(jnp.bfloat16), "dp", scatter_dimension=0, tiled=True
        ).astype(jnp.float32),
        lax.psum_scatter(
            grad_ln1_bias.astype(jnp.bfloat16), "dp", scatter_dimension=0, tiled=True
        ).astype(jnp.float32),
        lax.psum_scatter(
            grad_w_qkv.astype(jnp.bfloat16), "dp", scatter_dimension=0, tiled=True
        ).astype(jnp.float32),
        lax.psum_scatter(
            grad_bias_qv.astype(jnp.bfloat16), "dp", scatter_dimension=1, tiled=True
        ).astype(jnp.float32),
        lax.psum_scatter(
            grad_w_out.astype(jnp.bfloat16), "dp", scatter_dimension=0, tiled=True
        ).astype(jnp.float32),
        lax.psum_scatter(
            grad_b_out.astype(jnp.bfloat16), "dp", scatter_dimension=0, tiled=True
        ).astype(jnp.float32),
        lax.psum_scatter(
            grad_ln2_gain.astype(jnp.bfloat16), "dp", scatter_dimension=0, tiled=True
        ).astype(jnp.float32),
        lax.psum_scatter(
            grad_ln2_bias.astype(jnp.bfloat16), "dp", scatter_dimension=0, tiled=True
        ).astype(jnp.float32),
        lax.psum_scatter(
            grad_w_fc1.astype(jnp.bfloat16), "dp", scatter_dimension=0, tiled=True
        ).astype(jnp.float32),
        lax.psum_scatter(
            grad_b_fc1.astype(jnp.bfloat16), "dp", scatter_dimension=0, tiled=True
        ).astype(jnp.float32),
        lax.psum_scatter(
            grad_w_fc2.astype(jnp.bfloat16), "dp", scatter_dimension=1, tiled=True
        ).astype(jnp.float32),
        lax.psum_scatter(
            grad_b_fc2.astype(jnp.bfloat16), "dp", scatter_dimension=0, tiled=True
        ).astype(jnp.float32),
    )
    (
        part_ln1_gain,
        part_ln1_bias,
        part_w_qkv,
        part_bias_qv,
        part_w_out,
        part_b_out,
        part_ln2_gain,
        part_ln2_bias,
        part_w_fc1,
        part_b_fc1,
        part_w_fc2,
        part_b_fc2,
    ) = owned
    summed = (
        lax.psum(part_ln1_gain.astype(jnp.bfloat16), "seq").astype(jnp.float32),
        lax.psum(part_ln1_bias.astype(jnp.bfloat16), "seq").astype(jnp.float32),
        lax.psum(part_w_qkv.astype(jnp.bfloat16), "seq").astype(jnp.float32),
        lax.psum(part_bias_qv.astype(jnp.bfloat16), "seq").astype(jnp.float32),
        lax.psum(part_w_out.astype(jnp.bfloat16), "seq").astype(jnp.float32),
        lax.psum(part_b_out.astype(jnp.bfloat16), "seq").astype(jnp.float32),
        lax.psum(part_ln2_gain.astype(jnp.bfloat16), "seq").astype(jnp.float32),
        lax.psum(part_ln2_bias.astype(jnp.bfloat16), "seq").astype(jnp.float32),
        lax.psum(part_w_fc1.astype(jnp.bfloat16), "seq").astype(jnp.float32),
        lax.psum(part_b_fc1.astype(jnp.bfloat16), "seq").astype(jnp.float32),
        lax.psum(part_w_fc2.astype(jnp.bfloat16), "seq").astype(jnp.float32),
        lax.psum(part_b_fc2.astype(jnp.bfloat16), "seq").astype(jnp.float32),
    )
    (
        final_ln1_gain,
        final_ln1_bias,
        final_w_qkv,
        final_bias_qv,
        final_w_out,
        final_b_out,
        final_ln2_gain,
        final_ln2_bias,
        final_w_fc1,
        final_b_fc1,
        final_w_fc2,
        final_b_fc2,
    ) = summed
    return (
        layer_out,
        grad_patches,
        final_ln1_gain,
        final_ln1_bias,
        final_w_qkv,
        final_bias_qv,
        final_w_out,
        final_b_out,
        final_ln2_gain,
        final_ln2_bias,
        final_w_fc1,
        final_b_fc1,
        final_w_fc2,
        final_b_fc2,
    )


def solution(mesh):
    placed = (
        P("dp", "seq", None),
        P("dp", None),
        P("dp", None),
        P("dp"),
        P("dp"),
        P("dp", None),
        P(None, "dp"),
        P("dp", None),
        P("dp"),
        P("dp"),
        P("dp"),
        P("dp", None),
        P("dp"),
        P(None, "dp"),
        P("dp"),
        P("dp", "seq", None),
    )
    return jax.shard_map(
        per_device,
        mesh=mesh,
        in_specs=placed,
        out_specs=(
            P("dp", "seq", None),
            P("dp", "seq", None),
            P("dp"),
            P("dp"),
            P("dp", None),
            P(None, "dp"),
            P("dp", None),
            P("dp"),
            P("dp"),
            P("dp"),
            P("dp", None),
            P("dp"),
            P(None, "dp"),
            P("dp"),
        ),
        check_vma=False,
    )
```

profile of v0, /device:TPU:0, one launch (start us, length us, event | category | flops | bytes accessed | tf_op | source)
XLA Modules:
  0.0 1001.1 jit_solution(8663832701447037541)
XLA Ops:
  12.9 26.5 %all-reduce.15 = (bf16[1152]{0:T(1024)(128)(2,1)S(1)}, bf16[1152]{0:T(1024)(128)(2,1)S(1)}, bf16[1152]{0:T(1024)(128)(2,1)}, bf16[4304]{0:T(1024)(128)(2,1)}, bf...) all-reduce(bf16[1152]{0:T(1024)(128)(2,1)S(1)} %dynamic-update-slice.1, ...), channel_id=1, replica_groups=mesh['dp'=8,'seq'=4] {'dp'}, use_global_device_ids=true, to_apply=%add.1 | all-reduce | flops 10064 | bytes 40256
  41.3 7.9 all-gather
  50.9 14.6 %all-gather.6.cloned.1.call-done = bf16[1152,3456]{1,0:T(8,128)(2,1)} async-done(((bf16[144,3456]{1,0:T(8,128)(2,1)}), bf16[1152,3456]{1,0:T(8,128)(2,1)}) %all-gather.6.cloned.1.call-update) | async-done | bytes 7962640 | tf_op jit(solution)/shard_map/all_gather | solution.py:46
  65.5 8.5 add_convert_fusion
  74.0 12.0 %reshape.329 = bf16[2,256,3,16,72]{4,3,2,1,0:T(8,128)(2,1)} reshape(bf16[512,3456]{1,0:T(8,128)(2,1)S(1)} %add_convert_fusion) | data formatting | bytes 7077888 | tf_op jit(solution)/shard_map/reshape | solution.py:176
  86.0 11.5 %copy.45 = bf16[2,256,3,16,72]{1,0,4,2,3:T(2,128)(2,1)} copy(bf16[2,256,3,16,72]{4,3,2,1,0:T(8,128)(2,1)} %reshape.329) | data formatting | bytes 7077888 | tf_op jit(solution)/shard_map/reshape | solution.py:176
  102.5 78.9 %all-to-all-done = bf16[2,256,3,16,72]{1,0,4,2,3:T(2,128)(2,1)S(1)} async-done(((bf16[2,256,3,16,72]{1,0,4,2,3:T(2,128)(2,1)}), bf16[2,256,3,16,72]{1,0,4,2,3:T(2,128)(2,1)S(1)}, u32[]{:S(2)}, u32[]{:S(2)}) %all-to-all-start) | async-done | bytes 3538976 | tf_op jit(solution)/shard_map/all_to_all | solution.py:178
  197.3 39.2 %while.27 = (s32[]{:T(128)}, bf16[2,2,512,4,72]{2,4,3,1,0:T(8,128)(2,1)}, f32[2,2,4,512]{3,2,1,0:T(4,128)S(1)}, s32[2]{0:T(128)S(1)}, s32[2,1024]{1,0:T(2,128)S(...) while((s32[]{:T(128)}, ...), condition=%wide.region_5.6_spmd, body=%wide.region_2.5_spmd.sunk | while | flops 1262254592 | bytes 59282116 | solution.py:93
  245.8 48.2 %all-to-all-done.1 = bf16[2,1024,4,72]{3,2,0,1:T(4,128)(2,1)} async-done(((bf16[2,1024,4,72]{3,2,0,1:T(4,128)(2,1)}), bf16[2,1024,4,72]{3,2,0,1:T(4,128)(2,1)}, u32[]{:S(2)}, u32[]{:S(2)}) %all-to-all-start.1) | async-done | bytes 1179680 | tf_op jit(solution)/shard_map/all_to_all | solution.py:185
  308.9 12.4 %convolution_add_fusion = f32[512,4304]{0,1:T(8,128)} fusion(bf16[1152,4304]{1,0:T(8,128)(2,1)} %all-gather.10.cloned.1.call-done, f32[4304]{0:T(1024)S(1)} %convert_element_type.189, f32[512,1152]{1,0:T(8,128)} %copy-done.8, f32[1152]{0:T(1024)S(1)} %convert_element_type.187, f32[1152]{0:T(1024)S(1)} %convert_element_type.186, f32[512]{0:T(512)S(1)} %fusion.41, ...), kind=kOutput, calls=%fused_computation.63 | convolution fusion | flops 5082357760 | bytes 21120832 | tf_op jit(solution)/shard_map/dot_general | solution.py:195
  321.3 19.0 %fusion.47 = (bf16[4304]{0:T(1024)(128)(2,1)}, bf16[512,4304]{0,1:T(8,128)(2,1)S(1)}) fusion(f32[512,4304]{0,1:T(8,128)} %convolution_add_fusion, bf16[512,1152]{1,0:T(8,128)(2,1)S(1)} %bitcast.166, bf16[4304,1152]{0,1:T(8,128)(2,1)} %all-gather.12.cloned.1.call-done), kind=kOutput, calls=%fused_computation.114 | convolution fusion | flops 5132292096 | bytes 24326560 | tf_op jit(solution)/shard_map/dot_general | solution.py:35
  340.4 12.6 %multiply_reduce_fusion.1 = (bf16[1152]{0:T(1024)(128)(2,1)}, f32[512]{0:T(512)S(1)}, bf16[1152]{0:T(1024)(128)(2,1)}, f32[512,1152]{1,0:T(8,128)S(1)}) fusion(f32[512,1152]{1,0:T(8,128)S(1)} %copy-done.9, f32[512]{0:T(512)S(1)} %fusion.41, f32[512]{0:T(512)S(1)} %broadcast_multiply_fusion, f32[1152]{0:T(1024)S(1)} %convert_element_type.186, ...), kind=kOutput, calls=%fused_computation.77 | convolution fusion | flops 5081921024 | bytes 19057664 | tf_op jit(solution)/shard_map/dot_general | solution.py:35
  359.4 11.5 %convolution_convert_fusion.1 = bf16[1152,4304]{1,0:T(8,128)(2,1)} fusion(bf16[512,4304]{0,1:T(8,128)(2,1)} %copy-done.61, f32[512,1152]{1,0:T(8,128)} %copy-done.8, f32[1152]{0:T(1024)S(1)} %convert_element_type.187, f32[1152]{0:T(1024)S(1)} %convert_element_type.186, f32[512]{0:T(512)S(1)} %fusion.41, f32[512]{0:T(512)S(1)} %broadcast_multiply_fusion), kind=kOutput, calls=%fused_computation.50 | convolution fusion | flops 5085112320 | bytes 16696320 | tf_op jit(solution)/shard_map/dot_general | solution.py:29
  386.5 10.9 %convolution_convert_fusion = bf16[4304,1152]{0,1:T(8,128)(2,1)} fusion(bf16[512,1152]{1,0:T(8,128)(2,1)S(1)} %bitcast.167, f32[512,4304]{0,1:T(8,128)} %convolution_add_fusion), kind=kOutput, calls=%fused_computation.49 | convolution fusion | flops 5101996032 | bytes 19910656 | tf_op jit(solution)/shard_map/dot_general | solution.py:29
  397.3 17.1 %all-to-all-done.2 = bf16[2,256,16,72]{1,0,3,2:T(2,128)(2,1)} async-done(((bf16[2,256,16,72]{1,0,3,2:T(2,128)(2,1)}), bf16[2,256,16,72]{1,0,3,2:T(2,128)(2,1)}, u32[]{:S(2)}, u32[]{:S(2)}) %all-to-all-start.2) | async-done | bytes 1179680 | tf_op jit(solution)/shard_map/all_to_all | solution.py:271
  418.6 131.8 %while.28 = (s32[]{:T(128)}, f32[2,1024,4,72]{1,3,2,0:T(8,128)}, f32[2,1024,4,72]{1,3,2,0:T(8,128)}, bf16[2,2,512,4,72]{2,4,3,1,0:T(8,128)(2,1)}, s32[2]{0:T(128...) while((s32[]{:T(128)}, f32[2,1024,4,72]{1,3,2,0:T(8,128)}, ...), condition=%wide.region_12.13_spmd.clone, body=%wide.region_10.12_spmd.clone.sunk | while | flops 3089725952 | bytes 207508400 | solution.py:142
  421.6 9.5 fusion.112
  431.2 12.8 %multiply_reduce_fusion.8 = (f32[2,4,512]{2,1,0:T(4,128)S(1)}, f32[2,4,512,1024]{3,2,1,0:T(8,128)}) fusion(f32[2,4,512,1024]{3,2,1,0:T(8,128)} %fusion.112, f32[2,4,512]{2,1,0:T(4,128)S(1)} %constant_dynamic-slice_fusion.7, pred[2,512,1024]{2,1,0:T(8,128)(4,1)S(1)} %and_or_fusion.5, bf16[2,1024,4,72]{1,3,2,0:T(8,128)(2,1)S(1)} %copy-done.5, ...), kind=kOutput, calls=%fused_computation.21.clone.1 | convolution fusion | flops 624947200 | bytes 36405252 | tf_op jit(solution)/shard_map/while/body/eval_jaxpr/rqhe,rkhe->rhqk/dot_general | solution.py:121
  444.0 16.3 %multiply_convert_fusion.5 = bf16[2,4,512,1024]{3,2,1,0:T(8,128)(2,1)} fusion(f32[2,4,512,1024]{3,2,1,0:T(8,128)} %get-tuple-element.408, f32[2,4,512,1024]{3,2,1,0:T(8,128)} %fusion.112, f32[2,4,512]{2,1,0:T(4,128)S(1)} %get-tuple-element.409, f32[2,4,512]{2,1,0:T(4,128)S(1)} %constant_dynamic-slice_fusion.7, pred[2,512,1024]{2,1,0:T(8,128)(4,1)S(1)} %and_or_fusion.5), kind=kLoop, calls=%fused_computation.20.clone.1 | loop fusion | flops 25165824 | bytes 43024384 | tf_op jit(solution)/shard_map/while/body/eval_jaxpr/convert_element_type | solution.py:125
  484.7 10.0 fusion.112
  494.7 15.9 %multiply_reduce_fusion.8 = (f32[2,4,512]{2,1,0:T(4,128)S(1)}, f32[2,4,512,1024]{3,2,1,0:T(8,128)}) fusion(f32[2,4,512,1024]{3,2,1,0:T(8,128)} %fusion.112, f32[2,4,512]{2,1,0:T(4,128)S(1)} %constant_dynamic-slice_fusion.7, pred[2,512,1024]{2,1,0:T(8,128)(4,1)S(1)} %and_or_fusion.5, bf16[2,1024,4,72]{1,3,2,0:T(8,128)(2,1)S(1)} %copy-done.5, ...), kind=kOutput, calls=%fused_computation.21.clone.1 | convolution fusion | flops 624947200 | bytes 36405252 | tf_op jit(solution)/shard_map/while/body/eval_jaxpr/rqhe,rkhe->rhqk/dot_general | solution.py:121
  510.6 16.7 %multiply_convert_fusion.5 = bf16[2,4,512,1024]{3,2,1,0:T(8,128)(2,1)} fusion(f32[2,4,512,1024]{3,2,1,0:T(8,128)} %get-tuple-element.408, f32[2,4,512,1024]{3,2,1,0:T(8,128)} %fusion.112, f32[2,4,512]{2,1,0:T(4,128)S(1)} %get-tuple-element.409, f32[2,4,512]{2,1,0:T(4,128)S(1)} %constant_dynamic-slice_fusion.7, pred[2,512,1024]{2,1,0:T(8,128)(4,1)S(1)} %and_or_fusion.5), kind=kLoop, calls=%fused_computation.20.clone.1 | loop fusion | flops 25165824 | bytes 43024384 | tf_op jit(solution)/shard_map/while/body/eval_jaxpr/convert_element_type | solution.py:125
  527.3 7.8 bitcast_add_fusion.4
  570.8 137.3 %all-to-all-done.3 = bf16[2,1024,3,4,72]{4,3,0,2,1:T(4,128)(2,1)} async-done(((bf16[2,1024,3,4,72]{4,3,0,2,1:T(4,128)(2,1)}), bf16[2,1024,3,4,72]{4,3,0,2,1:T(4,128)(2,1)}, u32[]{:S(2)}, u32[]{:S(2)}) %all-to-all-start.3) | async-done | bytes 3538976 | tf_op jit(solution)/shard_map/all_to_all | solution.py:276
  708.2 16.5 %copy.55 = bf16[2,4,256,3,4,72]{2,0,5,4,1,3:T(2,128)(2,1)} copy(bf16[2,4,256,3,4,72]{5,4,0,3,2,1:T(4,128)(2,1)} %bitcast.27) | data formatting | bytes 7077888 | tf_op jit(solution)/shard_map/all_to_all | solution.py:276
  735.8 10.8 %bitcast_reduce_fusion = bf16[3,4,4,72]{3,2,1,0:T(4,128)(2,1)S(1)} fusion(bf16[2,4,256,3,4,72]{2,0,5,4,1,3:T(2,128)(2,1)} %copy.55), kind=kLoop, calls=%fused_computation.67 | loop fusion | flops 1766016 | bytes 3545856 | tf_op jit(solution)/shard_map/reduce_sum | solution.py:280
  750.5 52.7 %reduce-scatter.8.cloned.1.call-done = bf16[144,3456]{1,0:T(8,128)(2,1)} async-done(((bf16[1152,3456]{1,0:T(8,128)(2,1)}), bf16[144,3456]{1,0:T(8,128)(2,1)}) %reduce-scatter.8.cloned.1.call-update) | async-done | bytes 995344 | tf_op jit(solution)/shard_map/reduce_scatter | solution.py:362
  803.2 10.2 %fusion.46 = (bf16[1152]{0:T(1024)(128)(2,1)}, f32[512]{0:T(512)S(1)}, f32[512,1152]{1,0:T(8,128)S(1)}) fusion(f32[1152]{0:T(1024)S(1)} %copy-done.25, f32[512]{0:T(512)S(1)} %bitcast.182, bf16[2,256,1152]{2,1,0:T(8,128)(2,1)S(1)} %copy-done.3, bf16[512,3456]{0,1:T(8,128)(2,1)} %bitcast.173, bf16[1152,3456]{1,0:T(8,128)(2,1)} %all-gather.6.cloned.1.call-done), kind=kOutput, calls=%fused_computation.113 | convolution fusion | flops 4080400896 | bytes 15051520 | tf_op jit(solution)/shard_map/dot_general | solution.py:35
  816.4 24.8 %all-reduce.14 = (bf16[1152]{0:T(1024)(128)(2,1)}, bf16[1152]{0:T(1024)(128)(2,1)}, bf16[1152]{0:T(1024)(128)(2,1)}, bf16[1152]{0:T(1024)(128)(2,1)}, bf16[1152]...) all-reduce(bf16[1152]{0:T(1024)(128)(2,1)} %copy-done.39, ...), channel_id=1, replica_groups=mesh['dp'=8,'seq'=4] {'dp'}, use_global_device_ids=true, to_apply=%add.6 | all-reduce | flops 12368 | bytes 49472
  855.2 12.9 %fusion.39 = bf16[512,1152]{1,0:T(8,128)(2,1)} fusion(f32[512,1152]{1,0:T(8,128)S(1)} %copy-done.10, bf16[4304,1152]{0,1:T(8,128)(2,1)} %all-gather.12.cloned.1.call-done, f32[1152]{0:T(1024)S(1)} %convert_element_type.191, f32[512,4304]{0,1:T(8,128)} %convolution_add_fusion), kind=kOutput, calls=%fused_computation.75 | convolution fusion | flops 5098807296 | bytes 22274560 | tf_op jit(solution)/shard_map/dot_general | solution.py:201
  869.0 12.7 %all-reduce.16 = (bf16[144]{0:T(256)(128)(2,1)S(1)}, bf16[144]{0:T(256)(128)(2,1)S(1)}, bf16[2,144]{1,0:T(2,128)(2,1)S(1)}, bf16[144]{0:T(256)(128)(2,1)S(1)}, b...) all-reduce(bf16[144]{0:T(256)(128)(2,1)S(1)} %copy-done.54, ...), channel_id=1, replica_groups=mesh['dp'=8,'seq'=4] {'seq'}, use_global_device_ids=true, to_apply=%region_17.18 | all-reduce | flops 1690 | bytes 6760 | tf_op jit(solution)/shard_map/psum | solution.py:408
  886.3 100.8 %all-reduce.20.cloned.1.call-done = (bf16[144,3456]{1,0:T(8,128)(2,1)}, bf16[144,1152]{1,0:T(8,128)(2,1)}, bf16[144,4304]{1,0:T(8,128)(2,1)}, bf16[4304,144]{0,1:T(8,128)(2,1)}) async-done(((bf16[144,3456]{1,0:T(8,128)(2,1)}, bf16[144,1152]{1,0:T(8,128)(2,1)}, bf16[144,4304]{1,0:T(8,128)(2,1)}, bf16[4304,144]{0,1:T(8,128)(2,1)}), (bf16[144,3456]{1,0:T(8,128)(2,1)}, bf16[144,1152]{1,0:T(8,128)(2,1)}, ...) | async-done | bytes 3806224 | tf_op jit(solution)/shard_map/psum | solution.py:410
  (317 shorter events, 220.5 us)
Async XLA Ops:
  7.3 32.2 %copy-start.1 = (bf16[2,256,1152]{2,1,0:T(8,128)(2,1)S(1)}, bf16[2,256,1152]{2,1,0:T(8,128)(2,1)}, u32[]{:S(2)}) copy-start(bf16[2,256,1152]{2,1,0:T(8,128)(2,1)} %param.20) | copy-start | bytes 3538948
  7.3 34.0 %copy-start.48 = (bf16[2,144]{1,0:T(2,128)(2,1)S(1)}, bf16[2,144]{1,0:T(2,128)(2,1)}, u32[]{:S(2)}) copy-start(bf16[2,144]{1,0:T(2,128)(2,1)} %param.26) | copy-start | bytes 1732
  7.3 58.2 %all-gather.6.cloned.1.call-start = ((), (), s32[]{:S(2)}) async-start(), calls=%async_computation.9 | async-start | bytes 8957952 | tf_op jit(solution)/shard_map/all_gather | solution.py:46
  8.0 294.8 %all-gather.8.cloned.1.call-start = ((), (), s32[]{:S(2)}) async-start(), calls=%async_computation.10 | async-start | bytes 2985984 | tf_op jit(solution)/shard_map/all_gather | solution.py:48
  8.8 300.2 %all-gather.10.cloned.1.call-start = ((), (), s32[]{:S(2)}) async-start(), calls=%async_computation.11 | async-start | bytes 11280384 | tf_op jit(solution)/shard_map/all_gather | solution.py:52
  97.5 84.0 %all-to-all-start = ((bf16[2,256,3,16,72]{1,0,4,2,3:T(2,128)(2,1)}), bf16[2,256,3,16,72]{1,0,4,2,3:T(2,128)(2,1)S(1)}, u32[]{:S(2)}, u32[]{:S(2)}) async-start(bf16[2,256,3,16,72]{1,0,4,2,3:T(2,128)(2,1)} %copy.45), calls=%async_computation | async-start | bytes 7077888 | tf_op jit(solution)/shard_map/all_to_all | solution.py:178
  101.9 219.4 %all-gather.12.cloned.1.call-start = ((), (), s32[]{:S(2)}) async-start(), calls=%async_computation.12 | async-start | bytes 11280384 | tf_op jit(solution)/shard_map/all_gather | solution.py:54
  240.8 53.1 %all-to-all-start.1 = ((bf16[2,1024,4,72]{3,2,0,1:T(4,128)(2,1)}), bf16[2,1024,4,72]{3,2,0,1:T(4,128)(2,1)}, u32[]{:S(2)}, u32[]{:S(2)}) async-start(bf16[2,1024,4,72]{3,2,0,1:T(4,128)(2,1)} %bitcast.168), calls=%async_computation.1 | async-start | bytes 4194304 | tf_op jit(solution)/shard_map/all_to_all | solution.py:185
  245.4 505.0 %reduce-scatter.10.cloned.1.call-start = ((), (), s32[]{:S(2)}) async-start(), calls=%async_computation.14 | async-start | bytes 2985984 | tf_op jit(solution)/shard_map/reduce_scatter | solution.py:368
  321.3 19.0 %copy-start.9 = (f32[512,1152]{1,0:T(8,128)S(1)}, f32[512,1152]{1,0:T(8,128)}, u32[]{:S(2)}) copy-start(f32[512,1152]{1,0:T(8,128)} %copy-done.8) | copy-start | bytes 7077892
  359.3 391.1 %reduce-scatter.12.cloned.1.call-start = ((), (), s32[]{:S(2)}) async-start(), calls=%async_computation.15 | async-start | bytes 11280384 | tf_op jit(solution)/shard_map/reduce_scatter | solution.py:380
  382.1 32.4 %all-to-all-start.2 = ((bf16[2,256,16,72]{1,0,3,2:T(2,128)(2,1)}), bf16[2,256,16,72]{1,0,3,2:T(2,128)(2,1)}, u32[]{:S(2)}, u32[]{:S(2)}) async-start(bf16[2,256,16,72]{1,0,3,2:T(2,128)(2,1)} %reshape.289), calls=%async_computation.2 | async-start | bytes 2359296 | tf_op jit(solution)/shard_map/all_to_all | solution.py:271
  386.4 364.1 %reduce-scatter.14.cloned.1.call-start = ((), (), s32[]{:S(2)}) async-start(), calls=%async_computation.16 | async-start | bytes 11280384 | tf_op jit(solution)/shard_map/reduce_scatter | solution.py:386
  460.4 14.5 %slice-start = ((s8[16777216]{0:T(1024)(128)(4,1)}), s8[4194304]{0:T(1024)(128)(4,1)S(1)}, s32[]{:S(2)}) async-start(s8[16777216]{0:T(1024)(128)(4,1)} %bitcast.161), calls=%async_computation.19 | async-start | bytes 8388608 | tf_op jit(solution)/shard_map/while
  460.4 14.5 %slice-start.1 = ((s8[16777216]{0:T(1024)(128)(4,1)}), s8[4194304]{0:T(1024)(128)(4,1)S(1)}, s32[]{:S(2)}) async-start(s8[16777216]{0:T(1024)(128)(4,1)} %bitcast.161), calls=%async_computation.20 | async-start | bytes 8388608 | tf_op jit(solution)/shard_map/while
  460.4 14.5 %slice-start.2 = ((s8[16777216]{0:T(1024)(128)(4,1)}), s8[4194304]{0:T(1024)(128)(4,1)S(1)}, s32[]{:S(2)}) async-start(s8[16777216]{0:T(1024)(128)(4,1)} %bitcast.161), calls=%async_computation.21 | async-start | bytes 8388608 | tf_op jit(solution)/shard_map/while
  527.3 15.4 %slice-start = ((s8[16777216]{0:T(1024)(128)(4,1)}), s8[4194304]{0:T(1024)(128)(4,1)S(1)}, s32[]{:S(2)}) async-start(s8[16777216]{0:T(1024)(128)(4,1)} %bitcast.161), calls=%async_computation.19 | async-start | bytes 8388608 | tf_op jit(solution)/shard_map/while
  527.3 15.4 %slice-start.1 = ((s8[16777216]{0:T(1024)(128)(4,1)}), s8[4194304]{0:T(1024)(128)(4,1)S(1)}, s32[]{:S(2)}) async-start(s8[16777216]{0:T(1024)(128)(4,1)} %bitcast.161), calls=%async_computation.20 | async-start | bytes 8388608 | tf_op jit(solution)/shard_map/while
  527.3 15.4 %slice-start.2 = ((s8[16777216]{0:T(1024)(128)(4,1)}), s8[4194304]{0:T(1024)(128)(4,1)S(1)}, s32[]{:S(2)}) async-start(s8[16777216]{0:T(1024)(128)(4,1)} %bitcast.161), calls=%async_computation.21 | async-start | bytes 8388608 | tf_op jit(solution)/shard_map/while
  564.8 143.3 %all-to-all-start.3 = ((bf16[2,1024,3,4,72]{4,3,0,2,1:T(4,128)(2,1)}), bf16[2,1024,3,4,72]{4,3,0,2,1:T(4,128)(2,1)}, u32[]{:S(2)}, u32[]{:S(2)}) async-start(bf16[2,1024,3,4,72]{4,3,0,2,1:T(4,128)(2,1)} %copy.54), calls=%async_computation.3 | async-start | bytes 12582912 | tf_op jit(solution)/shard_map/all_to_all | solution.py:276
  570.2 232.9 %reduce-scatter.8.cloned.1.call-start = ((), (), s32[]{:S(2)}) async-start(), calls=%async_computation.13 | async-start | bytes 8957952 | tf_op jit(solution)/shard_map/reduce_scatter | solution.py:362
  735.7 14.4 %copy-start.60 = (bf16[144]{0:T(256)(128)(2,1)S(1)}, bf16[144]{0:T(256)(128)(2,1)}, u32[]{:S(2)}) copy-start(bf16[144]{0:T(256)(128)(2,1)} %param.34) | copy-start | bytes 868
  735.7 132.3 %reduce-scatter.16.cloned.1.call-start = ((), (), s32[]{:S(2)}) async-start(), calls=%async_computation.17 | async-start | bytes 331776
  747.8 55.4 %copy-start.31 = (f32[1,2,2,128]{3,1,2,0:T(2,128)S(1)}, f32[1,2,2,128]{3,1,2,0:T(2,128)}, u32[]{:S(2)}) copy-start(f32[1,2,2,128]{3,1,2,0:T(2,128)} %copy-done.30) | copy-start | bytes 6148
  747.8 239.3 %all-reduce.20.cloned.1.call-start = ((), (), s32[]{:S(2)}) async-start(), calls=%async_computation.18 | async-start | bytes 7667712 | tf_op jit(solution)/shard_map/psum | solution.py:410
  750.4 52.7 %copy-start.39 = (bf16[1152]{0:T(1024)(128)(2,1)}, bf16[1152]{0:T(1024)(128)(2,1)S(1)}, u32[]{:S(2)}) copy-start(bf16[1152]{0:T(1024)(128)(2,1)S(1)} %dynamic-update-slice.6) | copy-start | bytes 6916
  813.4 38.1 %copy-start.7 = (f32[512,1152]{1,0:T(8,128)S(1)}, f32[512,1152]{1,0:T(8,128)}, u32[]{:S(2)}) copy-start(f32[512,1152]{1,0:T(8,128)} %copy-done.6) | copy-start | bytes 7077892
  855.1 13.8 %copy-start.42 = (bf16[538]{0:T(1024)(128)(2,1)S(1)}, bf16[538]{0:T(1024)(128)(2,1)}, u32[]{:S(2)}) copy-start(bf16[538]{0:T(1024)(128)(2,1)} %dynamic-slice.18) | copy-start | bytes 3232
  855.2 13.8 %copy-start.49 = (bf16[144]{0:T(256)(128)(2,1)S(1)}, bf16[144]{0:T(256)(128)(2,1)}, u32[]{:S(2)}) copy-start(bf16[144]{0:T(256)(128)(2,1)} %dynamic-slice.10) | copy-start | bytes 868
  855.2 13.8 %copy-start.50 = (bf16[144]{0:T(256)(128)(2,1)S(1)}, bf16[144]{0:T(256)(128)(2,1)}, u32[]{:S(2)}) copy-start(bf16[144]{0:T(256)(128)(2,1)} %dynamic-slice.12) | copy-start | bytes 868
  855.2 13.8 %copy-start.51 = (bf16[144]{0:T(256)(128)(2,1)S(1)}, bf16[144]{0:T(256)(128)(2,1)}, u32[]{:S(2)}) copy-start(bf16[144]{0:T(256)(128)(2,1)} %dynamic-slice.14) | copy-start | bytes 868
  855.2 13.8 %copy-start.52 = (bf16[144]{0:T(256)(128)(2,1)S(1)}, bf16[144]{0:T(256)(128)(2,1)}, u32[]{:S(2)}) copy-start(bf16[144]{0:T(256)(128)(2,1)} %dynamic-slice.16) | copy-start | bytes 868
  (54 other events, 326.9 us)
Sparse Core Ops, SparseCore 0:
  10.0 55.4 all-gather.5
  67.4 30.2 all-gather.7
  99.5 61.3 all-gather.9
  162.6 61.3 all-gather.11
  359.4 41.8 reduce-scatter.9
  405.2 79.1 reduce-scatter.11
  488.0 79.1 reduce-scatter.13
  735.8 67.2 reduce-scatter.7
  806.8 32.8 reduce-scatter.15
  842.2 144.8 all-reduce.19
where the time goes:
time: 1010 us; the launch traced here: 1000 us
  waiting for transfers between devices  452 us (45%)
  matrix products  234 us (23%)
  local copies, waits for them, and re-layouts  116 us (11%)
  other arithmetic  86.2 us (9%)
  blocking collectives  71.9 us (7%)
  starting transfers between devices  19.7 us (2%)
  between operations  17.8 us (2%)
    all_to_all x1, waiting for transfers between devices, backward_pass(): lax.all_to_all(grad_proj, 'seq', split_axis=1, concat_axis=3, tiled=True)  137 us
    psum x1, waiting for transfers between devices, per_device(): lax.psum(part_w_qkv.astype(jnp.bfloat16), 'seq').astype(jnp.float32)  101 us
    all_to_all x1, waiting for transfers between devices, forward_pass(): lax.all_to_all(projected, 'seq', split_axis=3, concat_axis=1, tiled=True)  78.9 us
    reduce_scatter x1, waiting for transfers between devices, per_device(): lax.psum_scatter(grad_w_qkv.astype(jnp.bfloat16), 'dp', scatter_dimension...  52.7 us
    unnamed x2, blocking collectives  51.3 us
    all_to_all x1, waiting for transfers between devices, forward_pass(): lax.all_to_all(mixing, 'seq', split_axis=1, concat_axis=2, tiled=True)  48.2 us
    dot_general x4, matrix products, contract_cols(): lax.dot_general(left, right, (((1,), (1,)), ((), ())), preferred_element_...  46.8 us
    convert_element_type x2, other arithmetic, one_block(): grad_scores = (attn_probs * (grad_probs - inner)).astype(jnp.bfloat16)  33 us
  transfers between devices with their start and end apart: 14, of which 7 were waited for; matrix products, arithmetic and copies ran while one was open for 38% of the time, Pallas kernels for 0%

commit v1 on v0

--- a/solution.py
+++ b/solution.py
@@ -1,6 +1,10 @@
+import functools
+
 import jax
 import jax.numpy as jnp
 from jax import lax
+from jax.experimental import pallas as pl
+from jax.experimental.pallas import tpu as pltpu
 from jax.sharding import PartitionSpec as P
 
 HEADS = 16
@@ -450,6 +454,742 @@
     )
 
 
+WIN = 256
+ROWBLK = 64
+LOG2E = 1.4426950408889634
+ORDER = (0, 2, 4, 6, 1, 3, 5, 7)
+bf16 = jnp.bfloat16
+f32 = jnp.float32
+
+
+def nn(a, b):
+    return lax.dot_general(a, b, (((1,), (0,)), ((), ())), preferred_element_type=f32)
+
+
+def nt(a, b):
+    return lax.dot_general(a, b, (((1,), (1,)), ((), ())), preferred_element_type=f32)
+
+
+def tn(a, b):
+    return lax.dot_general(a, b, (((0,), (0,)), ((), ())), preferred_element_type=f32)
+
+
+VM = pl.BlockSpec(memory_space=pltpu.VMEM)
+ANY = pl.BlockSpec(memory_space=pl.ANY)
+
+
+def sds(shape, dtype):
+    return jax.ShapeDtypeStruct(shape, dtype)
+
+
+def row_loop(total, body):
+    @pl.loop(0, total // ROWBLK)
+    def _(r):
+        body(pl.ds(pl.multiple_of(r * ROWBLK, ROWBLK), ROWBLK))
+
+
+def unit_copies(pieces, half, cols, dst, sem):
+    d = lax.axis_index("dp")
+    own, c0, xr, cx, yr, cy, da, db, cda, cdb = pieces
+    six, seven = (da, cda) if half == 0 else (db, cdb)
+    rows = own.shape[1]
+    sources = (own, c0, xr, cx, yr, cy)
+    copies = []
+    for m in range(8):
+        if m < 6:
+            src = sources[m].at[half, :, cols]
+        else:
+            src = (six if m == 6 else seven).at[:, cols]
+        where = pl.ds(pl.multiple_of(jnp.bitwise_xor(d, m) * rows, rows), rows)
+        copies.append(pltpu.make_async_copy(src, dst.at[where, :], sem.at[m]))
+    return copies
+
+
+def norm_rows(v, gain, offset):
+    center = v - jnp.mean(v, axis=-1, keepdims=True)
+    spread = jnp.mean(center * center, axis=-1, keepdims=True)
+    return center * lax.rsqrt(spread + epsilon) * gain + offset
+
+
+def transpose_ordered(src, flipped, dst):
+    d = lax.axis_index("dp")
+    width = src.shape[1]
+    part = width // 8
+
+    @pl.loop(0, width // 128)
+    def _(j):
+        cols = pl.ds(pl.multiple_of(j * 128, 128), 128)
+        flipped[cols, :] = src[:, cols].T
+
+    for i, m in enumerate(ORDER):
+        where = pl.ds(pl.multiple_of(jnp.bitwise_xor(d, m) * part, part), part)
+        dst[i * part : (i + 1) * part, :] = flipped[where, :]
+
+
+def kv_kernel(x_ref, vec_ref, *rest):
+    pieces, (n_ref, kv_ref, w, sem) = rest[:10], rest[10:]
+    width = x_ref.shape[1]
+    copies = unit_copies(pieces, 1, pl.ds(0, 2 * width), w, sem)
+    for c in copies:
+        c.start()
+
+    def body(rows):
+        v = x_ref[rows, :].astype(f32)
+        n_ref[rows, :] = norm_rows(v, vec_ref[0:1, 0:width], vec_ref[1:2, 0:width]).astype(bf16)
+
+    row_loop(x_ref.shape[0], body)
+    for c in copies:
+        c.wait()
+
+    @pl.loop(0, 2 * width // 256)
+    def _(t):
+        cols = pl.ds(pl.multiple_of(t * 256, 256), 256)
+        kv_ref[:, cols] = (nn(n_ref[...], w[:, cols]) + vec_ref[8:9, cols]).astype(bf16)
+
+
+def column_tiles(width, body):
+    full = width // 256
+
+    @pl.loop(0, full)
+    def _(t):
+        body(pl.ds(pl.multiple_of(t * 256, 256), 256))
+
+    if width % 256:
+        body(pl.ds(full * 256, width % 256))
+
+
+def q_kernel(n_ref, vec_ref, *rest):
+    pieces, (q_ref, nt_ref, w, flipped, sem) = rest[:10], rest[10:]
+    width = n_ref.shape[1]
+    copies = unit_copies(pieces, 0, pl.ds(0, width), w, sem)
+    for c in copies:
+        c.start()
+    transpose_ordered(n_ref, flipped, nt_ref)
+    for c in copies:
+        c.wait()
+
+    def body(cols):
+        q_ref[:, cols] = (nn(n_ref[...], w[:, cols]) + vec_ref[2:3, cols]).astype(bf16)
+
+    column_tiles(width, body)
+
+
+def head_window(h, width):
+    w0 = pl.multiple_of(jnp.minimum((h * HD) // 128, (width - WIN) // 128) * 128, 128)
+    lane = lax.broadcasted_iota(jnp.int32, (1, WIN), 1)
+    off = h * HD - w0
+    return w0, (lane >= off) & (lane < off + HD)
+
+
+def attention_forward_kernel(q_ref, ko_ref, kx_ref, qid_ref, kid_ref, att_ref, lse_ref, bias, acc, lse_cols):
+    tokens, width = q_ref.shape
+    scale = HD**-0.5 * LOG2E
+    block = 256
+
+    @pl.loop(0, tokens // ROWBLK)
+    def _(r):
+        rows = pl.ds(pl.multiple_of(r * ROWBLK, ROWBLK), ROWBLK)
+        same = qid_ref[rows, 0:1] == kid_ref[0:1, :]
+        col = lax.broadcasted_iota(jnp.int32, (ROWBLK, 2 * tokens), 1)
+        row = lax.broadcasted_iota(jnp.int32, (ROWBLK, 2 * tokens), 0) + r * ROWBLK
+        bias[rows, :] = jnp.where(same | (col == row), 0.0, big_negative)
+        acc[rows, :] = jnp.zeros((ROWBLK, width), f32)
+        lse_cols[rows, :] = jnp.zeros((ROWBLK, 128), f32)
+
+    @pl.loop(0, HEADS)
+    def _(h):
+        w0, mask = head_window(h, width)
+        win, winv = pl.ds(w0, WIN), pl.ds(w0 + width, WIN)
+        zero = jnp.zeros((), bf16)
+        ko, kx = jnp.where(mask, ko_ref[:, win], zero), jnp.where(mask, kx_ref[:, win], zero)
+        vo, vx = jnp.where(mask, ko_ref[:, winv], zero), jnp.where(mask, kx_ref[:, winv], zero)
+        lane = lax.broadcasted_iota(jnp.int32, (1, 128), 1)
+        for qb in range(tokens // block):
+            rows = pl.ds(qb * block, block)
+            qw = q_ref[rows, win]
+            so = nt(qw, ko) * scale + bias[rows, 0:tokens]
+            sx = nt(qw, kx) * scale + bias[rows, tokens : 2 * tokens]
+            m = jnp.maximum(jnp.max(so, axis=1, keepdims=True), jnp.max(sx, axis=1, keepdims=True))
+            po, px = jnp.exp2(so - m), jnp.exp2(sx - m)
+            total = jnp.sum(po, axis=1, keepdims=True) + jnp.sum(px, axis=1, keepdims=True)
+            o = nn(po.astype(bf16), vo) + nn(px.astype(bf16), vx)
+            acc[rows, win] += o * (1.0 / total)
+            lse_cols[rows, :] = jnp.where(lane == h, m + jnp.log2(total), lse_cols[rows, :])
+
+    def body(rows):
+        att_ref[rows, :] = acc[rows, :].astype(bf16)
+
+    row_loop(tokens, body)
+    lse_ref[...] = lse_cols[...].T[:HEADS, :]
+
+
+def attention_backward_kernel(near, q_ref, kv_ref, go_ref, lse_ref, del_ref, kid_ref, qid_ref, dqp_ref, dq_ref, dkv_ref, bias, dqa, dka):
+    tokens, width = q_ref.shape
+    scale, unit = HD**-0.5 * LOG2E, HD**-0.5
+
+    @pl.loop(0, tokens // ROWBLK)
+    def _(r):
+        rows = pl.ds(pl.multiple_of(r * ROWBLK, ROWBLK), ROWBLK)
+        allowed = kid_ref[rows, 0:1] == qid_ref[0:1, :]
+        if near:
+            col = lax.broadcasted_iota(jnp.int32, (ROWBLK, tokens), 1)
+            row = lax.broadcasted_iota(jnp.int32, (ROWBLK, tokens), 0) + r * ROWBLK
+            allowed = allowed | (col == row)
+        bias[rows, :] = jnp.where(allowed, 0.0, big_negative)
+        dka[rows, :] = jnp.zeros((ROWBLK, 2 * width), f32)
+        dqa[rows, :] = dqp_ref[rows, :] if near else jnp.zeros((ROWBLK, width), f32)
+
+    @pl.loop(0, HEADS)
+    def _(h):
+        w0, mask = head_window(h, width)
+        win, winv = pl.ds(w0, WIN), pl.ds(w0 + width, WIN)
+        zero = jnp.zeros((), bf16)
+        qw = q_ref[:, win]
+        qm, gm = jnp.where(mask, qw, zero), jnp.where(mask, go_ref[:, win], zero)
+        lse, inner = lse_ref[pl.ds(h, 1), :], del_ref[pl.ds(h, 1), :]
+        km, vw = jnp.where(mask, kv_ref[:, win], zero), kv_ref[:, winv]
+        pt = jnp.exp2(nt(km, qw) * scale + bias[...] - lse)
+        dka[:, winv] += nn(pt.astype(bf16), gm)
+        ds = (pt * (nt(vw, gm) - inner)).astype(bf16)
+        dka[:, win] += nn(ds, qm)
+        dqa[:, win] += tn(ds, km)
+
+    @pl.loop(0, tokens // ROWBLK)
+    def _(r):
+        rows = pl.ds(pl.multiple_of(r * ROWBLK, ROWBLK), ROWBLK)
+        dq_ref[rows, :] = (dqa[rows, :] * unit).astype(bf16) if near else dqa[rows, :]
+        dkv_ref[rows, 0:width] = (dka[rows, 0:width] * unit).astype(dkv_ref.dtype)
+        dkv_ref[rows, width : 2 * width] = dka[rows, width : 2 * width].astype(dkv_ref.dtype)
+
+
+def middle_kernel(att_ref, x_ref, cot_ref, vec_ref, *rest):
+    pieces, (mid_ref, n2_ref, n2t_ref, cott_ref, attt_ref, w, flipped, sem) = rest[:10], rest[10:]
+    tokens, width = x_ref.shape
+    copies = unit_copies(pieces, 0, pl.ds(width, width), w, sem)
+    for c in copies:
+        c.start()
+    transpose_ordered(cot_ref, flipped, cott_ref)
+    transpose_ordered(att_ref, flipped, attt_ref)
+    for c in copies:
+        c.wait()
+
+    def body(cols):
+        mid_ref[:, cols] = nn(att_ref[...], w[:, cols]) + vec_ref[4:5, cols] + x_ref[:, cols].astype(f32)
+
+    column_tiles(width, body)
+
+    def norm(rows):
+        n2_ref[rows, :] = norm_rows(mid_ref[rows, :], vec_ref[5:6, 0:width], vec_ref[6:7, 0:width]).astype(bf16)
+
+    row_loop(tokens, norm)
+    transpose_ordered(n2_ref, flipped, n2t_ref)
+
+
+def mlp_kernel(first, last, n2_ref, cot_ref, n2t_ref, cott_ref, b1_ref, vec_ref, outp_ref, gnp_ref, *rest):
+    pieces = rest[:10]
+    out_ref, gn_ref, keep_ref, send_ref, gb1_ref, wbuf, acc, gacc, sem = rest[10:]
+    t, steps = pl.program_id(0), pl.num_programs(0)
+    width = n2_ref.shape[1]
+    tile = wbuf.shape[-1]
+    half = width // 2
+
+    def copies(step, slot):
+        cols = pl.ds(pl.multiple_of(step * tile, tile), tile)
+        return unit_copies(pieces, 0, cols, wbuf.at[slot, 0], sem.at[slot, 0]) + unit_copies(
+            pieces, 1, cols, wbuf.at[slot, 1], sem.at[slot, 1]
+        )
+
+    slot = lax.rem(t, 2)
+
+    @pl.when(t == 0)
+    def _():
+        for c in copies(0, 0):
+            c.start()
+
+        def init(rows):
+            acc[rows, :] = outp_ref[rows, :] + vec_ref[7:8, 0:width] if first else outp_ref[rows, :]
+            gacc[rows, :] = jnp.zeros((ROWBLK, width), f32) if first else gnp_ref[rows, :]
+
+        row_loop(n2_ref.shape[0], init)
+
+    @pl.when(t + 1 < steps)
+    def _():
+        for c in copies(t + 1, 1 - slot):
+            c.start()
+
+    for c in copies(t, slot):
+        c.wait()
+    w1, w2 = wbuf[slot, 0], wbuf[slot, 1]
+    u = nn(n2_ref[...], w1) + b1_ref[...]
+    c0 = 0.7978845608028654
+    th = jnp.tanh(c0 * (u + 0.044715 * u * u * u))
+    active = (0.5 * u * (1.0 + th)).astype(bf16)
+    slope = 0.5 * (1.0 + th) + 0.5 * u * (1.0 - th * th) * (c0 * (1.0 + 3 * 0.044715 * u * u))
+    gh = (nn(cot_ref[...], w2) * slope).astype(bf16)
+    gb1_ref[...] = jnp.sum(gh.astype(f32), axis=0, keepdims=True)
+    acc[...] += nt(active, w2)
+    gacc[...] += nt(gh, w1)
+    g1 = nn(n2t_ref[...], gh).astype(bf16)
+    keep_ref[0], send_ref[0] = g1[:half], g1[half:]
+    g2 = nn(cott_ref[...], active).astype(bf16)
+    keep_ref[1], send_ref[1] = g2[:half], g2[half:]
+
+    @pl.when(t == steps - 1)
+    def _():
+        out_ref[...] = acc[...].astype(out_ref.dtype)
+        gn_ref[...] = gacc[...]
+
+
+def mlp_call(first, last, n2, cot, n2t, cott, b1, vec, outp, gnp, pieces):
+    tokens, width = n2.shape
+    cols, tile = pieces[0].shape[2], 256
+    const = lambda a: pl.BlockSpec(a.shape, lambda t: (0,) * a.ndim, pipeline_mode=pl.Buffered(1))
+    out_type = bf16 if last else f32
+    return pl.pallas_call(
+        functools.partial(mlp_kernel, first, last),
+        grid=(cols // tile,),
+        in_specs=[const(n2), const(cot), const(n2t), const(cott), pl.BlockSpec((1, tile), lambda t: (0, t)), const(vec),
+                  const(outp), const(gnp)] + [ANY] * 10,
+        out_specs=(
+            pl.BlockSpec((tokens, width), lambda t: (0, 0)),
+            pl.BlockSpec((tokens, width), lambda t: (0, 0)),
+            pl.BlockSpec((2, width // 2, tile), lambda t: (0, 0, t)),
+            pl.BlockSpec((2, width // 2, tile), lambda t: (0, 0, t)),
+            pl.BlockSpec((1, tile), lambda t: (0, t)),
+        ),
+        out_shape=(
+            sds((tokens, width), out_type),
+            sds((tokens, width), f32),
+            sds((2, width // 2, cols), bf16),
+            sds((2, width // 2, cols), bf16),
+            sds((1, cols), f32),
+        ),
+        scratch_shapes=[
+            pltpu.VMEM((2, 2, width, tile), bf16),
+            pltpu.VMEM((tokens, width), f32),
+            pltpu.VMEM((tokens, width), f32),
+            pltpu.SemaphoreType.DMA((2, 2, 8)),
+        ],
+        cost_estimate=pl.CostEstimate(
+            flops=12 * tokens * width * cols, bytes_accessed=8 * width * cols + 12 * tokens * width, transcendentals=tokens * cols
+        ),
+        name="mlp_first" if first else "mlp_last",
+    )(n2, cot, n2t, cott, b1, vec, outp, gnp, *pieces)
+
+
+def norm_back(v, g, gain):
+    center = v - jnp.mean(v, axis=-1, keepdims=True)
+    rs = lax.rsqrt(jnp.mean(center * center, axis=-1, keepdims=True) + epsilon)
+    n = center * rs
+    e = g * gain
+    grad = rs * (e - jnp.mean(e, axis=-1, keepdims=True) - n * jnp.mean(e * n, axis=-1, keepdims=True))
+    return grad, g * n
+
+
+def branch_kernel(cot_ref, gn_ref, mid_ref, vec_ref, att_ref, attt_ref, *rest):
+    pieces, (gm_ref, ga_ref, keep_ref, send_ref, sums_ref, del_ref, w, gb, sem) = rest[:10], rest[10:]
+    tokens, width = cot_ref.shape
+    copies = unit_copies(pieces, 0, pl.ds(width, width), w, sem)
+    for c in copies:
+        c.start()
+    sums_ref[...] = jnp.zeros(sums_ref.shape, f32)
+
+    def body(rows):
+        cot = cot_ref[rows, :].astype(f32)
+        g = gn_ref[rows, :]
+        grad, gain_part = norm_back(mid_ref[rows, :], g, vec_ref[5:6, 0:width])
+        gm = cot + grad
+        gm_ref[rows, :] = gm
+        low = gm.astype(bf16)
+        gb[rows, :] = low
+        sums_ref[0:1, :] += jnp.sum(gain_part, axis=0, keepdims=True)
+        sums_ref[1:2, :] += jnp.sum(g, axis=0, keepdims=True)
+        sums_ref[2:3, :] += jnp.sum(low.astype(f32), axis=0, keepdims=True)
+        sums_ref[3:4, :] += jnp.sum(cot, axis=0, keepdims=True)
+
+    row_loop(tokens, body)
+    half, part = width // 2, keep_ref.shape[-1]
+    for i in range(2):
+        at = i * (width - part)
+        g = nn(attt_ref[...], gb[:, at : at + part]).astype(bf16)
+        keep_ref[i], send_ref[i] = g[:half], g[half:]
+    for c in copies:
+        c.wait()
+    column = lax.broadcasted_iota(jnp.int32, (HEADS, 128), 1)
+    first = lax.broadcasted_iota(jnp.int32, (HEADS, 128), 0) * HD
+    del_ref[...] = jnp.zeros(del_ref.shape, f32)
+
+    @pl.loop(0, width // 128)
+    def _(j):
+        cols = pl.ds(pl.multiple_of(j * 128, 128), 128)
+        ga = nt(gb[...], w[cols, :]).astype(bf16)
+        ga_ref[:, cols] = ga
+        prod = ga.astype(f32) * att_ref[:, cols].astype(f32)
+        high = prod.astype(bf16)
+        rest_low = (prod - high.astype(f32)).astype(bf16)
+        at = column + j * 128
+        chosen = jnp.where((at >= first) & (at < first + HD), 1.0, 0.0).astype(bf16)
+        del_ref[...] += nt(chosen, high) + nt(chosen, rest_low)
+
+
+def qkv_grad_kernel(nt_ref, dq_ref, dko_ref, dkr_ref, keep_ref, send_ref, dkv_ref, all_ref):
+    tokens, width = dq_ref.shape
+    half, part = width // 2, keep_ref.shape[-1]
+
+    def join(rows):
+        total = (dko_ref[rows, :] + dkr_ref[rows, :].astype(f32)).astype(bf16)
+        dkv_ref[rows, :] = total
+        all_ref[rows, 0:width] = dq_ref[rows, :]
+        all_ref[rows, width : 3 * width] = total
+
+    row_loop(tokens, join)
+    for i in range(2):
+
+        @pl.loop(0, part // 256)
+        def _(t):
+            cols = pl.ds(pl.multiple_of(t * 256, 256), 256)
+            at = pl.ds(pl.multiple_of(t * 256 + i * (3 * width - part), 128), 256)
+            g = nn(nt_ref[...], all_ref[:, at]).astype(bf16)
+            keep_ref[i, :, cols], send_ref[i, :, cols] = g[:half], g[half:]
+
+
+def input_grad_kernel(dq_ref, dkv_ref, x_ref, gm_ref, vec_ref, *rest):
+    pieces, (gx_ref, sums_ref, wq, wkv, gn, sem) = rest[:10], rest[10:]
+    tokens, width = x_ref.shape
+    copies = unit_copies(pieces, 0, pl.ds(0, width), wq, sem.at[0]) + unit_copies(
+        pieces, 1, pl.ds(0, 2 * width), wkv, sem.at[1]
+    )
+    for c in copies:
+        c.start()
+    sums_ref[...] = jnp.zeros(sums_ref.shape, f32)
+    for c in copies:
+        c.wait()
+
+    @pl.loop(0, width // 128)
+    def _(j):
+        rows = pl.ds(pl.multiple_of(j * 128, 128), 128)
+        gn[:, rows] = nt(dq_ref[...], wq[rows, :]) + nt(dkv_ref[...], wkv[rows, :])
+
+    def body(rows):
+        g = gn[rows, :]
+        grad, gain_part = norm_back(x_ref[rows, :].astype(f32), g, vec_ref[0:1, 0:width])
+        gx_ref[rows, :] = (gm_ref[rows, :] + grad).astype(bf16)
+        sums_ref[0:1, :] += jnp.sum(gain_part, axis=0, keepdims=True)
+        sums_ref[1:2, :] += jnp.sum(g, axis=0, keepdims=True)
+        sums_ref[2:3, :] += jnp.sum(dq_ref[rows, :].astype(f32), axis=0, keepdims=True)
+        sums_ref[3:4, :] += jnp.sum(dkv_ref[rows, width : 2 * width].astype(f32), axis=0, keepdims=True)
+
+    row_loop(tokens, body)
+
+
+def call(body, name, outs, scratch, flops, moved, *args, pieces=()):
+    return pl.pallas_call(
+        body,
+        out_shape=tuple(sds(s, t) for s, t in outs),
+        in_specs=[VM] * len(args) + [ANY] * len(pieces),
+        out_specs=tuple(VM for _ in outs),
+        scratch_shapes=scratch,
+        cost_estimate=pl.CostEstimate(flops=flops, bytes_accessed=moved, transcendentals=0),
+        name=name,
+    )(*args, *pieces)
+
+
+def swap(v, mask, size):
+    return lax.ppermute(v, "dp", [(i, i ^ mask) for i in range(size)])
+
+
+def after(v, *others):
+    return lax.optimization_barrier((v, *others))[0]
+
+
+def sums_kernel(shape, *refs):
+    terms, outs, at = refs[: sum(map(sum, shape))], refs[sum(map(sum, shape)) :], 0
+    for out, counts in zip(outs, shape):
+        for k, count in enumerate(counts):
+            total = terms[at][...].astype(f32)
+            for r in terms[at + 1 : at + count]:
+                total = total + r[...].astype(f32)
+            out[k] = total.astype(bf16)
+            at += count
+
+
+def add_blocks(name, *outs):
+    first = outs[0][0][0][0]
+    rows, cols = first.shape[-2:]
+    tile = max(t for t in range(128, 1025, 128) if cols % t == 0)
+    specs, args = [], []
+    for out in outs:
+        for terms in out:
+            for array, index in terms:
+                specs.append(pl.BlockSpec((None,) * len(index) + (rows, tile), lambda t, index=index: (*index, 0, t)))
+                args.append(array)
+    count = sum(len(out) for out in outs)
+    return pl.pallas_call(
+        functools.partial(sums_kernel, [[len(terms) for terms in out] for out in outs]),
+        grid=(cols // tile,),
+        in_specs=specs,
+        out_specs=tuple(pl.BlockSpec((len(out), rows, tile), lambda t: (0, 0, t)) for out in outs),
+        out_shape=tuple(sds((len(out), rows, cols), bf16) for out in outs),
+        cost_estimate=pl.CostEstimate(flops=len(args) * rows * cols, bytes_accessed=2 * (len(args) + count) * rows * cols, transcendentals=0),
+        name=name,
+    )(*args)
+
+
+def blocks(v):
+    return v.reshape(2, 4, v.shape[1] // 4, v.shape[2])
+
+
+def unit_first(name, keep, got, size):
+    k, g = blocks(keep), blocks(got)
+    sa, sb = add_blocks(
+        name, [[(k, (0, j)), (g, (0, j))] for j in (1, 3)], [[(k, (1, j)), (g, (1, j))] for j in (2, 3)]
+    )
+    return swap(sa, 2, size), swap(sb, 4, size)
+
+
+def unit_second(name, keep, got, ax, by, size):
+    k, g = blocks(keep), blocks(got)
+    ta, tb = add_blocks(name, [[(k, (0, 2)), (g, (0, 2)), (ax, (1,))]], [[(k, (1, 1)), (g, (1, 1)), (by, (1,))]])
+    return swap(ta, 4, size), swap(tb, 2, size)
+
+
+def unit_third(name, keep, got, ax, by, ay, bx):
+    k, g = blocks(keep), blocks(got)
+    return add_blocks(
+        name, [[(k, (0, 0)), (g, (0, 0)), (ax, (0,)), (ay, (0,))], [(k, (1, 0)), (g, (1, 0)), (by, (0,)), (bx, (0,))]]
+    )[0]
+
+
+def fold_in(own):
+    return lax.ppermute(own, "seq", [(0, 1), (3, 2)])
+
+
+def across(inner):
+    return lax.ppermute(inner, "seq", [(1, 2), (2, 1)])
+
+
+def fold_out(total):
+    return lax.ppermute(total, "seq", [(1, 0), (2, 3)])
+
+
+def pair_sum(name, a, b):
+    return add_blocks(name, [[(a, (i,)), (b, (i,))] for i in range(a.shape[0])])[0]
+
+
+def reduce_small(rows, size):
+    d = lax.axis_index("dp")
+    bit, left = 1, rows
+    while bit < size:
+        pairs = left.reshape(left.shape[0] // 2, 2, -1)
+        up = (d // bit) % 2 == 1
+        mine = jnp.where(up, pairs[:, 1], pairs[:, 0])
+        other = jnp.where(up, pairs[:, 0], pairs[:, 1])
+        left = mine + swap(other.astype(bf16), bit, size).astype(f32)
+        bit *= 2
+    for mask in (1, 2):
+        low = left.astype(bf16)
+        left = low.astype(f32) + lax.ppermute(low, "seq", [(i, i ^ mask) for i in range(4)]).astype(f32)
+    return left[0]
+
+
+def gather_small(row, size):
+    d = lax.axis_index("dp")
+    got, bit = row[None], 1
+    while bit < size:
+        other = swap(got, bit, size)
+        up = (d // bit) % 2 == 1
+        got = jnp.concatenate([jnp.where(up, other, got), jnp.where(up, got, other)], axis=0)
+        bit *= 2
+    return got
+
+
+def token_routes(size, depth):
+    routes = []
+    for s in range(2):
+        perm = []
+        for d in range(size):
+            for z in range(depth):
+                j = (z & 1) ^ s
+                to_d, to_z = (d & ~1) | (z >> 1), 2 * (d & 1) + j
+                perm.append((d * depth + z, to_d * depth + to_z))
+        routes.append(perm)
+    return routes
+
+
+def to_rows(v, routes):
+    odd = lax.axis_index("seq") % 2 == 1
+    first = jnp.where(odd, v[1], v[0])
+    second = jnp.where(odd, v[0], v[1])
+    r0 = lax.ppermute(first, ("dp", "seq"), routes[0])
+    r1 = lax.ppermute(second, ("dp", "seq"), routes[1])
+    return jnp.concatenate([jnp.where(odd, r1, r0), jnp.where(odd, r0, r1)], axis=0)
+
+
+def from_rows(v, routes):
+    odd = lax.axis_index("seq") % 2 == 1
+    half = v.shape[0] // 2
+    t0, t1 = v[:half], v[half:]
+    back = [[(b, a) for a, b in perm] for perm in routes]
+    r0 = lax.ppermute(jnp.where(odd, t1, t0), ("dp", "seq"), back[0])
+    r1 = lax.ppermute(jnp.where(odd, t0, t1), ("dp", "seq"), back[1])
+    return jnp.stack([jnp.where(odd, r1, r0), jnp.where(odd, r0, r1)])
+
+
+def by_rows(size, depth):
+    def step(patches, picture_ids, valid_mask, ln1_gain, ln1_bias, w_qkv, bias_qv, w_out, b_out, ln2_gain, ln2_bias,
+             w_fc1, b_fc1, w_fc2, b_fc2, cotangent):
+        width = patches.shape[-1]
+        ff = w_fc1.shape[1]
+        tokens = patches.shape[0] * patches.shape[1]
+        part = width // size
+        d, z = lax.axis_index("dp"), lax.axis_index("seq")
+        core = d % 2
+        routes = token_routes(size, depth)
+
+        unit0 = jnp.stack([jnp.concatenate([w_qkv[:, :width], w_out], axis=1), w_qkv[:, width:]])
+        extra = -ff % 256
+        w1 = jnp.pad(w_fc1, ((0, 0), (0, extra)))
+        w2 = jnp.pad(w_fc2.T, ((0, 0), (0, extra)))
+        cut = (ff + extra) // 512 * 256 + ((ff + extra) // 256 % 2) * 256
+        unit1 = jnp.stack([w1[:, :cut], w2[:, :cut]])
+        unit2 = jnp.stack([w1[:, cut:], w2[:, cut:]])
+        x = to_rows(patches, routes)
+        x0, y0, c0 = swap(unit0, 2, size), swap(unit0, 4, size), swap(unit0, 1, size)
+        da0, db0, cx0, cy0 = swap(y0[0], 2, size), swap(x0[1], 4, size), swap(x0, 1, size), swap(y0, 1, size)
+        unit1 = after(unit1, x0, y0)
+        x1, y1, c1 = swap(unit1, 2, size), swap(unit1, 4, size), swap(unit1, 1, size)
+        p0 = (unit0, c0, x0, cx0, y0, cy0, da0, db0, swap(da0, 1, size), swap(db0, 1, size))
+        cot = to_rows(after(cotangent, x), routes)
+
+        small = jnp.concatenate([ln1_gain, ln1_bias, bias_qv[0], bias_qv[1], b_out, ln2_gain, ln2_bias, b_fc2, b_fc1])
+        small = gather_small(small, size).astype(f32)
+        vec = jnp.moveaxis(small[:, : 8 * part].reshape(size, 8, part), 0, 1).reshape(8, width)
+        b1 = jnp.pad(small[:, 8 * part :].reshape(1, ff), ((0, 0), (0, extra)))
+        vec = jnp.concatenate([vec, jnp.zeros((8, width), f32)], axis=0)
+        kv_bias = jnp.concatenate([jnp.zeros((1, width), f32), vec[3:4]], axis=1)
+        vec = jnp.concatenate([jnp.pad(vec[:8], ((0, 0), (0, width))), jnp.pad(kv_bias, ((0, 7), (0, 0)))], axis=0)
+
+        ids = jnp.stack([picture_ids, jnp.where(valid_mask == 1, picture_ids, -1)])
+        far_ids = swap(ids, 1, size)
+        ids = jnp.where(z // 2 == core, ids, far_ids)
+        ids = jnp.where(z % 2 == 1, ids[:, 1], ids[:, 0]).reshape(2, 2, tokens)
+        near = jnp.where(core == 1, ids[:, 1], ids[:, 0])
+        far = jnp.where(core == 1, ids[:, 0], ids[:, 1])
+        keys = jnp.concatenate([near[1], far[1]])
+        qid_row, qid_col = jnp.broadcast_to(near[0][None], (8, tokens)), jnp.broadcast_to(near[0][:, None], (tokens, 128))
+        kid_row, kid_col = jnp.broadcast_to(keys[None], (8, 2 * tokens)), jnp.broadcast_to(keys[:, None], (2 * tokens, 128))
+
+        act = ((tokens, width), bf16)
+        flip = ((width, tokens), bf16)
+        vm = pltpu.VMEM
+        dma8 = pltpu.SemaphoreType.DMA((8,))
+        mm = 2 * tokens * width * width
+        n, kv = call(kv_kernel, "kv", [act, ((tokens, 2 * width), bf16)], [vm((width, 2 * width), bf16), dma8],
+                     2 * mm, 4 * width * width, x, vec, pieces=p0)
+        far_kv = swap(kv, 1, size)
+        q, nt_ = call(q_kernel, "q", [act, flip], [vm((width, width), bf16), vm((width, tokens), bf16), dma8],
+                      mm, 2 * width * width, n, vec, pieces=p0)
+        sc = 2 * tokens * 2 * tokens * WIN * HEADS
+        q, x1, y1 = lax.optimization_barrier((q, x1, y1))
+        da1, db1, cx1, cy1 = swap(y1[0], 2, size), swap(x1[1], 4, size), swap(x1, 1, size), swap(y1, 1, size)
+        unit2 = after(unit2, q, x1, y1)
+        x2, y2, c2 = swap(unit2, 2, size), swap(unit2, 4, size), swap(unit2, 1, size)
+        att, lse = call(
+            attention_forward_kernel, "attention_forward", [act, ((HEADS, tokens), f32)],
+            [vm((tokens, 2 * tokens), f32), vm((tokens, width), f32), vm((tokens, 128), f32)],
+            3 * sc, 8 * tokens * width, q, kv, far_kv, qid_col, kid_row)
+        da1, db1, att = lax.optimization_barrier((da1, db1, att))
+        p1 = (unit1, c1, x1, cx1, y1, cy1, da1, db1, swap(da1, 1, size), swap(db1, 1, size))
+        mid, n2, n2t, cott, attt = call(
+            middle_kernel, "middle", [((tokens, width), f32), act, flip, flip, flip],
+            [vm((width, width), bf16), vm((width, tokens), bf16), dma8], mm, 2 * width * width, att, x, cot, vec, pieces=p0)
+        n2, x2, y2 = lax.optimization_barrier((n2, x2, y2))
+        da2, db2, cx2, cy2 = swap(y2[0], 2, size), swap(x2[1], 4, size), swap(x2, 1, size), swap(y2, 1, size)
+        acc, gn, keep1, send1, gb1a = mlp_call(True, False, n2, cot, n2t, cott, b1[:, :cut], vec, mid, mid, p1)
+        acc, da2, db2 = lax.optimization_barrier((acc, da2, db2))
+        p2 = (unit2, c2, x2, cx2, y2, cy2, da2, db2, swap(da2, 1, size), swap(db2, 1, size))
+        got1 = swap(send1.reshape(2, width // 2, -1), 1, size)
+        out, gn, keep2, send2, gb1b = mlp_call(False, True, n2, cot, n2t, cott, b1[:, cut:], vec, acc, gn, p2)
+        keep1, got1, gn = lax.optimization_barrier((keep1, got1, gn))
+        ax1, by1 = unit_first("first1", keep1, got1, size)
+        got2 = swap(send2, 1, size)
+        layer_out = from_rows(out, routes)
+
+        part_o = (width // 256 + 1) * 128
+        stacked = ((2, width // 2, part_o), bf16)
+        gm, ga, keepo, sendo, sums2, inner = call(
+            branch_kernel, "branch", [((tokens, width), f32), act, stacked, stacked, ((8, width), f32), ((HEADS, tokens), f32)],
+            [vm((width, width), bf16), vm((tokens, width), bf16), dma8], 2 * mm, 4 * width * width,
+            cot, gn, mid, vec, att, attt, pieces=p0)
+        keep2, got2, ga = lax.optimization_barrier((keep2, got2, ga))
+        ax2, by2 = unit_first("first2", keep2, got2, size)
+        goto = swap(sendo, 1, size)
+
+        def attention_backward(near, kv_half, ids_half, dqp):
+            return call(
+                functools.partial(attention_backward_kernel, near), "attention_backward_near" if near else "attention_backward_far",
+                [((tokens, width), bf16 if near else f32), ((tokens, 2 * width), f32 if near else bf16)],
+                [vm((tokens, tokens), f32), vm((tokens, width), f32), vm((tokens, 2 * width), f32)],
+                3 * sc, 16 * tokens * width, q, kv_half, ga, lse, inner, ids_half, qid_row, dqp)
+
+        dqp, dkx = attention_backward(False, far_kv, kid_col[tokens:], gm)
+        dkr = swap(dkx, 1, size)
+        dqp, ax1, by1, goto = lax.optimization_barrier((dqp, ax1, by1, goto))
+        ay1, bx1 = unit_second("second1", keep1, got1, ax1, by1, size)
+        axo, byo = unit_first("firsto", keepo, goto, size)
+        dq, dko = attention_backward(True, kv, kid_col[:tokens], dqp)
+        dq, ax2, by2, ay1, bx1 = lax.optimization_barrier((dq, ax2, by2, ay1, bx1))
+        ay2, bx2 = unit_second("second2", keep2, got2, ax2, by2, size)
+        own1 = unit_third("third1", keep1, got1, ax1, by1, ay1, bx1)
+        in1 = fold_in(own1)
+        part_q = (3 * width // 256 + 1) * 128
+        stacked = ((2, width // 2, part_q), bf16)
+        keepq, sendq, dkv = call(
+            qkv_grad_kernel, "qkv_grad", [stacked, stacked, ((tokens, 2 * width), bf16)], [vm((tokens, 3 * width), bf16)],
+            3 * mm, 8 * width * width, nt_, dq, dko, dkr)
+        gotq = swap(sendq, 1, size)
+        dkv, axo, byo = lax.optimization_barrier((dkv, axo, byo))
+        ayo, bxo = unit_second("secondo", keepo, goto, axo, byo, size)
+        gx, sums1 = call(
+            input_grad_kernel, "input_grad", [act, ((8, width), f32)],
+            [vm((width, width), bf16), vm((width, 2 * width), bf16), vm((tokens, width), f32), pltpu.SemaphoreType.DMA((2, 8))],
+            3 * mm, 6 * width * width, dq, dkv, x, gm, vec, pieces=p0)
+        keepq, gotq, gx = lax.optimization_barrier((keepq, gotq, gx))
+        axq, byq = unit_first("firstq", keepq, gotq, size)
+        grad_patches = from_rows(gx, routes)
+
+        gb1 = jnp.concatenate([gb1a, gb1b], axis=1)[:, :ff].reshape(size, ff // size)
+        vecs = jnp.concatenate([sums1[:4], sums2[:4]]).reshape(8, size, part)
+        small = reduce_small(jnp.concatenate([jnp.moveaxis(vecs, 0, 1).reshape(size, 8 * part), gb1], axis=1), size)
+        mine, grad_b_fc1 = small[: 8 * part].reshape(8, part), small[8 * part :]
+
+        own2 = unit_third("third2", keep2, got2, ax2, by2, ay2, bx2)
+        owno = unit_third("thirdo", keepo, goto, axo, byo, ayo, bxo)
+        in2, ino = fold_in(own2), fold_in(owno)
+        mid1 = pair_sum("inner1", own1, in1)
+        tot1 = pair_sum("total1", mid1, across(mid1))
+        mid2, mido = pair_sum("inner2", own2, in2), pair_sum("innero", owno, ino)
+        tot2, toto = pair_sum("total2", mid2, across(mid2)), pair_sum("totalo", mido, across(mido))
+        ayq, bxq = unit_second("secondq", keepq, gotq, axq, byq, size)
+        ownq = unit_third("thirdq", keepq, gotq, axq, byq, ayq, bxq)
+        midq = pair_sum("innerq", ownq, fold_in(ownq))
+        totq = pair_sum("totalq", midq, across(midq))
+        inside = (z == 1) | (z == 2)
+        g1, g2, go, gq = [jnp.where(inside, t, fold_out(t)).astype(f32) for t in (tot1, tot2, toto, totq)]
+        n1, nk = cut, ff - cut
+        w1g = jnp.concatenate([g1[0], g2[0][:, :nk]], axis=1)
+        w2g = jnp.concatenate([g1[1], g2[1][:, :nk]], axis=1).T
+        wog = jnp.concatenate([go[0], go[1][:, 2 * part_o - width :]], axis=1)
+        wqg = jnp.concatenate([gq[0], gq[1][:, 2 * part_q - 3 * width :]], axis=1)
+        return (layer_out, grad_patches, mine[0], mine[1], wqg, mine[2:4], wog, mine[6], mine[4], mine[5], w1g, grad_b_fc1, w2g, mine[7])
+
+    return step
+
+
+def fits_rows(mesh, patches):
+    return mesh.shape["dp"] == 8 and mesh.shape["seq"] == 4
+
+
 def solution(mesh):
     placed = (
         P("dp", "seq", None),
@@ -470,7 +1210,7 @@
         P("dp", "seq", None),
     )
     return jax.shard_map(
-        per_device,
+        by_rows(mesh.shape["dp"], mesh.shape["seq"]) if fits_rows(mesh, None) else per_device,
         mesh=mesh,
         in_specs=placed,
         out_specs=(

time: 1010 us -> 644 us (0.64)
  Pallas kernels: 0 us -> 273 us
  waiting for transfers between devices: 452 us -> 205 us
  matrix products: 234 us -> 0 us
  local copies, waits for them, and re-layouts: 116 us -> 31.7 us
  starting transfers between devices: 19.7 us -> 96.9 us
  blocking collectives: 71.9 us -> 0 us
  other arithmetic: 86.2 us -> 32.3 us
  between operations: 17.8 us -> 1.78 us
    all_to_all x4 -> x0, waiting for transfers between devices: 282 us -> none  [the longest x1 137 us: backward_pass(): lax.all_to_all(grad_proj, 'seq', split_axis=1, concat_axis=3, tiled=True)]
    pallas_call x0 -> x31, Pallas kernels: none -> 273 us  [the longest x9 150 us: call(): pl.pallas_call(body, out_shape=tuple((sds(s, t) for s, t in outs)), in_sp...]
    dot_general x26 -> x0, matrix products: 234 us -> none  [the longest x4 46.8 us: contract_cols(): lax.dot_general(left, right, (((1,), (1,)), ((), ())), preferred_element_...]
    ppermute x0 -> x78, waiting for transfers between devices: none -> 205 us  [the longest x56 90.2 us: swap(): return lax.ppermute(v, 'dp', [(i, i ^ mask) for i in range(size)])]
    psum x1 -> x0, waiting for transfers between devices: 101 us -> none  [per_device(): lax.psum(part_w_qkv.astype(jnp.bfloat16), 'seq').astype(jnp.float32)]
    ppermute x0 -> x78, starting transfers between devices: none -> 96.9 us  [the longest x56 38.6 us: swap(): return lax.ppermute(v, 'dp', [(i, i ^ mask) for i in range(size)])]
    reduce_scatter x4 -> x0, waiting for transfers between devices: 52.7 us -> none  [the longest x1 52.7 us: per_device(): lax.psum_scatter(grad_w_qkv.astype(jnp.bfloat16), 'dp', scatter_dimension...]
    unnamed x2 -> x0, blocking collectives: 51.3 us -> none
  transfers between devices with their start and end apart: 14 -> 78, of which waited for: 7 -> 24; matrix products, arithmetic and copies ran while one was open for 38% -> 8% of each run, Pallas kernels for 0% -> 42%
where the time goes in v1:
time: 644 us; the launch traced here: 641 us
  Pallas kernels  273 us (42%)
  waiting for transfers between devices  205 us (32%)
  starting transfers between devices  96.9 us (15%)
  other arithmetic  32.3 us (5%)
  local copies, waits for them, and re-layouts  31.7 us (5%)
    pallas_call x9, Pallas kernels, call(): pl.pallas_call(body, out_shape=tuple((sds(s, t) for s, t in outs)), in_sp...  150 us
    ppermute x56, waiting for transfers between devices, swap(): return lax.ppermute(v, 'dp', [(i, i ^ mask) for i in range(size)])  90.2 us
    ppermute x4, waiting for transfers between devices, fold_out(): return lax.ppermute(total, 'seq', [(1, 0), (2, 3)])  88.8 us
    pallas_call x20, Pallas kernels, add_blocks(): pl.pallas_call(functools.partial(sums_kernel, [[len(terms) for terms in o...  62.4 us
    pallas_call x2, Pallas kernels, mlp_call(): pl.pallas_call(functools.partial(mlp_kernel, first, last), grid=(cols //...  60.4 us
    ppermute x56, starting transfers between devices, swap(): return lax.ppermute(v, 'dp', [(i, i ^ mask) for i in range(size)])  38.6 us
    ppermute x4, waiting for transfers between devices, fold_in(): return lax.ppermute(own, 'seq', [(0, 1), (3, 2)])  20.3 us
    ppermute x2, starting transfers between devices, reduce_small(): lax.ppermute(low, 'seq', [(i, i ^ mask) for i in range(4)]).astype(f32)  13.5 us
  transfers between devices with their start and end apart: 78, of which 24 were waited for; matrix products, arithmetic and copies ran while one was open for 8% of the time, Pallas kernels for 42%

profile of v1, /device:TPU:0, one launch (start us, length us, event | category | flops | bytes accessed | tf_op | source)
XLA Modules:
  0.0 641.3 jit_solution(2639255006363450131)
XLA Ops:
  17.2 19.8 %collective-permute-done.3 = bf16[2,1690]{1,0:T(2,128)(2,1)S(1)} collective-permute-done((bf16[2,1690]{1,0:T(2,128)(2,1)S(1)}, bf16[2,1690]{1,0:T(2,128)(2,1)S(1)}, u32[]{:S(2)}, u32[]{:S(2)}) %collective-permute-start.3) | collective-permute-done | bytes 6792 | tf_op jit(solution)/shard_map/ppermute | solution.py:898
  41.9 6.0 collective-permute-start.1
  53.9 10.7 %collective-permute-done.10.rest_6_ = bf16[144,2304]{1,0:T(8,128)(2,1)S(1)} collective-permute-done((bf16[144,2304]{1,0:T(8,128)(2,1)}, bf16[144,2304]{1,0:T(8,128)(2,1)S(1)}, u32[]{:S(2)}, u32[]{:S(2)}) %collective-permute-start.10) | collective-permute-done | bytes 663584 | tf_op jit(solution)/shard_map/ppermute | solution.py:898
  75.1 5.9 collective-permute-start.21
  81.0 9.8 %kv.1 = (bf16[512,1152]{1,0:T(8,128)(2,1)}, bf16[512,2304]{1,0:T(8,128)(2,1)}) custom-call(bf16[512,1152]{1,0:T(8,128)(2,1)} %pad_maximum_fusion.4.x_ref, f32[16,2304]{1,0:T(8,128)} %select_maximum_fusion.vec_ref, bf16[2,144,2304]{2,1,0:T(8,128)(2,1)} %copy-done.1, bf16[2,144,2304]{2,1,0:T(8,128)(2,1)} %collective-permute-done.5.rest_1_, ...), custom_call_target="tpu_custom_call" | custom-call | flops 2717908992 | bytes 5308416 | tf_op jit(solution)/shard_map/kv/pallas_call | solution.py:886
  91.0 6.6 %q.1 = (bf16[512,1152]{1,0:T(8,128)(2,1)}, bf16[1152,512]{1,0:T(8,128)(2,1)}) custom-call(bf16[512,1152]{1,0:T(8,128)(2,1)} %get-tuple-element.102.n_ref, f32[16,2304]{1,0:T(8,128)} %select_maximum_fusion.vec_ref, bf16[2,144,2304]{2,1,0:T(8,128)(2,1)} %copy-done.1, bf16[2,144,2304]{2,1,0:T(8,128)(2,1)} %collective-permute-done.5.rest_1_, ...), custom_call_target="tpu_custom_call" | custom-call | flops 1358954496 | bytes 2654208 | tf_op jit(solution)/shard_map/q/pallas_call | solution.py:886
  106.8 10.7 %collective-permute-done.16.rest_6_ = bf16[144,2304]{1,0:T(8,128)(2,1)} collective-permute-done((bf16[144,2304]{1,0:T(8,128)(2,1)S(1)}, bf16[144,2304]{1,0:T(8,128)(2,1)}, u32[]{:S(2)}, u32[]{:S(2)}) %collective-permute-start.16) | collective-permute-done | bytes 663584 | tf_op jit(solution)/shard_map/ppermute | solution.py:898
  120.1 25.6 %attention_forward.1 = (bf16[512,1152]{1,0:T(8,128)(2,1)}, f32[16,512]{1,0:T(8,128)}) custom-call(bf16[512,1152]{1,0:T(8,128)(2,1)} %get-tuple-element.107.q_ref, bf16[512,2304]{1,0:T(8,128)(2,1)} %get-tuple-element.108.ko_ref.kv_ref, bf16[512,2304]{1,0:T(8,128)(2,1)} %collective-permute-done.18.kx_ref.kv_ref, s32[512,128]{1,0:T(8,128)} %broadcast_in_dim.37.qid_ref, ...), custom_call_target="tpu_custom_call" | custom-call | flops 12884901888 | bytes 4718592 | tf_op jit(solution)/shard_map/attention_forward/pallas_call | solution.py:886
  145.7 12.0 %middle.1 = (f32[512,1152]{1,0:T(8,128)}, bf16[512,1152]{1,0:T(8,128)(2,1)}, bf16[1152,512]{1,0:T(8,128)(2,1)}, bf16[1152,512]{1,0:T(8,128)(2,1)}, bf16[1152,512]{1,0:T(8,128)(2,1)}) custom-call(bf16[512,1152]{1,0:T(8,128)(2,1)} %get-tuple-element.110.att_ref, bf16[512,1152]{1,0:T(8,128)(2,1)} %pad_maximum_fusion.4.x_ref, ...), custom_call_target="tpu_custom_call" | custom-call | flops 1358954496 | bytes 2654208 | tf_op jit(solution)/shard_map/middle/pallas_call | solution.py:886
  164.6 31.7 %mlp_first.1 = (f32[512,1152]{1,0:T(8,128)}, f32[512,1152]{1,0:T(8,128)}, bf16[2,576,2304]{2,1,0:T(8,128)(2,1)}, bf16[2,576,2304]{2,1,0:T(8,128)(2,1)}, f32[1,2304]{1,0:T(1,128)}) custom-call(bf16[512,1152]{1,0:T(8,128)(2,1)} %get-tuple-element.114.n2_ref, bf16[512,1152]{1,0:T(8,128)(2,1)} %pad_maximum_fusion.5.cot_ref, ...), custom_call_target="tpu_custom_call" | custom-call | flops 16307453952 | bytes 28311552 | tf_op jit(solution)/shard_map/mlp_first/pallas_call | solution.py:748
  199.6 28.7 %mlp_last.1 = (bf16[512,1152]{1,0:T(8,128)(2,1)}, f32[512,1152]{1,0:T(8,128)}, bf16[2,576,2048]{2,1,0:T(8,128)(2,1)}, bf16[2,576,2048]{2,1,0:T(8,128)(2,1)}, f32[1,2048]{1,0:T(1,128)}) custom-call(bf16[512,1152]{1,0:T(8,128)(2,1)} %get-tuple-element.114.n2_ref, bf16[512,1152]{1,0:T(8,128)(2,1)} %pad_maximum_fusion.5.cot_ref, ...), custom_call_target="tpu_custom_call" | custom-call | flops 14495514624 | bytes 25952256 | tf_op jit(solution)/shard_map/mlp_last/pallas_call | solution.py:748
  228.5 4.9 first1.1
  235.1 17.2 %branch.1 = (f32[512,1152]{1,0:T(8,128)}, bf16[512,1152]{1,0:T(8,128)(2,1)}, bf16[2,576,640]{2,1,0:T(8,128)(2,1)}, bf16[2,576,640]{2,1,0:T(8,128)(2,1)}, f32[8,1152]{1,0:T(8,128)}, /*index=5*/f32[16,512]{1,0:T(8,128)}) custom-call(bf16[512,1152]{1,0:T(8,128)(2,1)} %pad_maximum_fusion.5.cot_ref, f32[512,1152]{1,0:T(8,128)} %get-tuple-element.134.gn_ref, ...), custom_call_target="tpu_custom_call" | custom-call | flops 2717908992 | bytes 5308416 | tf_op jit(solution)/shard_map/branch/pallas_call | solution.py:886
  253.8 21.8 %attention_backward_far.1 = (f32[512,1152]{1,0:T(8,128)}, bf16[512,2304]{1,0:T(8,128)(2,1)}) custom-call(bf16[512,1152]{1,0:T(8,128)(2,1)} %get-tuple-element.107.q_ref, bf16[512,2304]{1,0:T(8,128)(2,1)} %collective-permute-done.18.kx_ref.kv_ref, bf16[512,1152]{1,0:T(8,128)(2,1)} %get-tuple-element.137.go_ref, f32[16,512]{1,0:T(8,128)} %get-tuple-element.138.lse_ref, ...), custom_call_target="tpu_custom_call" | custom-call | flops 12884901888 | bytes 9437184 | tf_op jit(solution)/shard_map/attention_backward_far/pallas_call | solution.py:886
  282.2 4.6 second1.1
  291.7 22.2 %attention_backward_near.1 = (bf16[512,1152]{1,0:T(8,128)(2,1)}, f32[512,2304]{1,0:T(8,128)}) custom-call(bf16[512,1152]{1,0:T(8,128)(2,1)} %get-tuple-element.107.q_ref, bf16[512,2304]{1,0:T(8,128)(2,1)} %get-tuple-element.108.ko_ref.kv_ref, bf16[512,1152]{1,0:T(8,128)(2,1)} %get-tuple-element.137.go_ref, f32[16,512]{1,0:T(8,128)} %get-tuple-element.138.lse_ref, ...), custom_call_target="tpu_custom_call" | custom-call | flops 12884901888 | bytes 9437184 | tf_op jit(solution)/shard_map/attention_backward_near/pallas_call | solution.py:886
  316.4 7.8 %collective-permute-done.45.refs_3_ = bf16[1,144,2304]{2,1,0:T(8,128)(2,1)S(1)} collective-permute-done((bf16[1,144,2304]{2,1,0:T(8,128)(2,1)}, bf16[1,144,2304]{2,1,0:T(8,128)(2,1)S(1)}, u32[]{:S(2)}, u32[]{:S(2)}) %collective-permute-start.45) | collective-permute-done | bytes 663584 | tf_op jit(solution)/shard_map/ppermute | solution.py:898
  325.3 4.6 third1.1.refs_0_.refs_2_
  329.9 3.9 collective-permute-start.70
  338.5 14.8 %qkv_grad.1 = (bf16[2,576,1792]{2,1,0:T(8,128)(2,1)}, bf16[2,576,1792]{2,1,0:T(8,128)(2,1)}, bf16[512,2304]{1,0:T(8,128)(2,1)}) custom-call(bf16[1152,512]{1,0:T(8,128)(2,1)} %get-tuple-element.128.nt_ref, bf16[512,1152]{1,0:T(8,128)(2,1)} %get-tuple-element.157.dq_ref, f32[512,2304]{1,0:T(8,128)} %get-tuple-element.158.dko_ref, ...), custom_call_target="tpu_custom_call" | custom-call | flops 4076863488 | bytes 10616832 | tf_op jit(solution)/shard_map/qkv_grad/pallas_call | solution.py:886
  353.4 20.4 %input_grad.1 = (bf16[512,1152]{1,0:T(8,128)(2,1)}, f32[8,1152]{1,0:T(8,128)}) custom-call(bf16[512,1152]{1,0:T(8,128)(2,1)} %get-tuple-element.157.dq_ref, bf16[512,2304]{1,0:T(8,128)(2,1)} %get-tuple-element.167.dkv_ref, bf16[512,1152]{1,0:T(8,128)(2,1)} %pad_maximum_fusion.4.x_ref, f32[512,1152]{1,0:T(8,128)} %get-tuple-element.140.dqp_ref.gm_ref, ...), custom_call_target="tpu_custom_call" | custom-call | flops 4076863488 | bytes 7962624 | tf_op jit(solution)/shard_map/input_grad/pallas_call | solution.py:886
  386.6 3.8 inner1.1.refs_0_.refs_2_
  395.6 4.3 collective-permute-done.36
  413.2 11.3 %collective-permute-start.57 = (bf16[1,1690]{1,0:T(2,128)(2,1)S(1)}, bf16[1,1690]{1,0:T(2,128)(2,1)S(1)}, u32[]{:S(2)}, u32[]{:S(2)}) collective-permute-start(bf16[1,1690]{1,0:T(2,128)(2,1)S(1)} %add_convert_fusion), channel_id=1, source_target_pairs={{0,2},{1,3},{2,0},{3,1},{4,6},{5,7},{6,4},{7,5},{8,10},{9,11},{10,... | collective-permute-start | bytes 10148 | tf_op jit(solution)/shard_map/ppermute | solution.py:991
  432.9 3.8 total1.1
  448.5 42.0 %collective-permute-done.69 = bf16[2,144,640]{2,1,0:T(8,128)(2,1)S(1)} collective-permute-done((bf16[2,144,640]{2,1,0:T(8,128)(2,1)}, bf16[2,144,640]{2,1,0:T(8,128)(2,1)S(1)}, u32[]{:S(2)}, u32[]{:S(2)}) %collective-permute-start.69) | collective-permute-done | bytes 368672 | tf_op jit(solution)/shard_map/ppermute | solution.py:972
  503.0 16.5 %collective-permute-done.58.refs_2_ = bf16[2,144,1792]{2,1,0:T(8,128)(2,1)} collective-permute-done((bf16[2,144,1792]{2,1,0:T(8,128)(2,1)}, bf16[2,144,1792]{2,1,0:T(8,128)(2,1)}, u32[]{:S(2)}, u32[]{:S(2)}) %collective-permute-start.58) | collective-permute-done | bytes 1032224 | tf_op jit(solution)/shard_map/ppermute | solution.py:898
  526.5 9.4 %collective-permute-done.60.refs_3_ = bf16[1,144,1792]{2,1,0:T(8,128)(2,1)S(1)} collective-permute-done((bf16[1,144,1792]{2,1,0:T(8,128)(2,1)}, bf16[1,144,1792]{2,1,0:T(8,128)(2,1)S(1)}, u32[]{:S(2)}, u32[]{:S(2)}) %collective-permute-start.60) | collective-permute-done | bytes 516128 | tf_op jit(solution)/shard_map/ppermute | solution.py:898
  545.1 18.6 %collective-permute-done.62.refs_1_.refs_3_ = bf16[2,144,1792]{2,1,0:T(8,128)(2,1)S(1)} collective-permute-done((bf16[2,144,1792]{2,1,0:T(8,128)(2,1)}, bf16[2,144,1792]{2,1,0:T(8,128)(2,1)S(1)}, u32[]{:S(2)}, u32[]{:S(2)}) %collective-permute-start.62) | collective-permute-done | bytes 1032224 | tf_op jit(solution)/shard_map/ppermute | solution.py:964
  572.1 3.9 collective-permute-start.51
  576.0 6.1 collective-permute-start.52
  592.6 46.9 %collective-permute-done.64 = bf16[2,144,1792]{2,1,0:T(8,128)(2,1)S(1)} collective-permute-done((bf16[2,144,1792]{2,1,0:T(8,128)(2,1)}, bf16[2,144,1792]{2,1,0:T(8,128)(2,1)S(1)}, u32[]{:S(2)}, u32[]{:S(2)}) %collective-permute-start.64) | collective-permute-done | bytes 1032224 | tf_op jit(solution)/shard_map/ppermute | solution.py:972
  (365 shorter events, 183.4 us)
Async XLA Ops:
  3.2 44.7 %collective-permute-start.8 = (bf16[2,144,2304]{2,1,0:T(8,128)(2,1)S(1)}, bf16[2,144,2304]{2,1,0:T(8,128)(2,1)S(1)}, u32[]{:S(2)}, u32[]{:S(2)}) collective-permute-start(bf16[2,144,2304]{2,1,0:T(8,128)(2,1)S(1)} %pad_maximum_fusion.2.rest_0_), channel_id=1, source_target_pairs={{0,16},{4,20},{8,24},{12,28},{16,0},{20,4},{24,8},{28,12},{1,17},{... | collective-permute-start | bytes 3981320 | tf_op jit(solution)/shard_map/ppermute | solution.py:898
  6.2 44.1 %collective-permute-start.6 = (bf16[2,144,2304]{2,1,0:T(8,128)(2,1)S(1)}, bf16[2,144,2304]{2,1,0:T(8,128)(2,1)}, u32[]{:S(2)}, u32[]{:S(2)}) collective-permute-start(bf16[2,144,2304]{2,1,0:T(8,128)(2,1)S(1)} %pad_maximum_fusion.2.rest_0_), channel_id=1, source_target_pairs={{0,8},{4,12},{8,0},{12,4},{16,24},{20,28},{24,16},{28,20},{1,9},{5... | collective-permute-start | bytes 3981320 | tf_op jit(solution)/shard_map/ppermute | solution.py:898
  7.7 59.6 %collective-permute-start.5 = (bf16[2,144,2304]{2,1,0:T(8,128)(2,1)S(1)}, bf16[2,144,2304]{2,1,0:T(8,128)(2,1)}, u32[]{:S(2)}, u32[]{:S(2)}) collective-permute-start(bf16[2,144,2304]{2,1,0:T(8,128)(2,1)S(1)} %pad_maximum_fusion.2.rest_0_), channel_id=1, source_target_pairs={{0,4},{4,0},{8,12},{12,8},{16,20},{20,16},{24,28},{28,24},{1,5},{5... | collective-permute-start | bytes 3981320 | tf_op jit(solution)/shard_map/ppermute | solution.py:898
  11.0 54.4 %collective-permute-start = (bf16[256,1152]{1,0:T(8,128)(2,1)}, bf16[256,1152]{1,0:T(8,128)(2,1)}, u32[]{:S(2)}, u32[]{:S(2)}) collective-permute-start(bf16[256,1152]{1,0:T(8,128)(2,1)} %get-tuple-element.212), channel_id=1, source_target_pairs={{0,1},{1,0},{2,5},{3,4},{4,3},{5,2},{6,7},{7,6},{8,9},{9,8},{10,13... | collective-permute-start | bytes 1769480 | tf_op jit(solution)/shard_map/ppermute | solution.py:1024
  105.1 56.2 %collective-permute-start.24 = (bf16[2,144,2304]{2,1,0:T(8,128)(2,1)S(1)}, bf16[2,144,2304]{2,1,0:T(8,128)(2,1)}, u32[]{:S(2)}, u32[]{:S(2)}) collective-permute-start(bf16[2,144,2304]{2,1,0:T(8,128)(2,1)S(1)} %copy-done.24), channel_id=1, source_target_pairs={{0,4},{4,0},{8,12},{12,8},{16,20},{20,16},{24,28},{28,24},{1,5},{5... | collective-permute-start | bytes 3981320 | tf_op jit(solution)/shard_map/ppermute | solution.py:898
  106.2 51.4 %collective-permute-start.22 = (bf16[2,144,2048]{2,1,0:T(8,128)(2,1)S(1)}, bf16[2,144,2048]{2,1,0:T(8,128)(2,1)}, u32[]{:S(2)}, u32[]{:S(2)}) collective-permute-start(bf16[2,144,2048]{2,1,0:T(8,128)(2,1)S(1)} %copy-done.28), channel_id=1, source_target_pairs={{0,8},{4,12},{8,0},{12,4},{16,24},{20,28},{24,16},{28,20},{1,9},{5... | collective-permute-start | bytes 3538952 | tf_op jit(solution)/shard_map/ppermute | solution.py:898
  117.5 40.2 %collective-permute-start.23 = (bf16[2,144,2048]{2,1,0:T(8,128)(2,1)S(1)}, bf16[2,144,2048]{2,1,0:T(8,128)(2,1)}, u32[]{:S(2)}, u32[]{:S(2)}) collective-permute-start(bf16[2,144,2048]{2,1,0:T(8,128)(2,1)S(1)} %copy-done.28), channel_id=1, source_target_pairs={{0,16},{4,20},{8,24},{12,28},{16,0},{20,4},{24,8},{28,12},{1,17},{... | collective-permute-start | bytes 3538952 | tf_op jit(solution)/shard_map/ppermute | solution.py:898
  118.1 43.3 %collective-permute-start.25 = (bf16[2,144,2304]{2,1,0:T(8,128)(2,1)}, bf16[2,144,2304]{2,1,0:T(8,128)(2,1)}, u32[]{:S(2)}, u32[]{:S(2)}) collective-permute-start(bf16[2,144,2304]{2,1,0:T(8,128)(2,1)} %collective-permute-done.14.rest_2_), channel_id=1, source_target_pairs={{0,4},{4,0},{8,12},{12,8},{16,20},{20,16},{24,28},{28,24},{1,5},{5... | collective-permute-start | bytes 3981320 | tf_op jit(solution)/shard_map/ppermute | solution.py:898
  118.1 43.8 %collective-permute-start.26 = (bf16[2,144,2304]{2,1,0:T(8,128)(2,1)}, bf16[2,144,2304]{2,1,0:T(8,128)(2,1)}, u32[]{:S(2)}, u32[]{:S(2)}) collective-permute-start(bf16[2,144,2304]{2,1,0:T(8,128)(2,1)} %collective-permute-done.15.rest_4_), channel_id=1, source_target_pairs={{0,4},{4,0},{8,12},{12,8},{16,20},{20,16},{24,28},{28,24},{1,5},{5... | collective-permute-start | bytes 3981320 | tf_op jit(solution)/shard_map/ppermute | solution.py:898
  161.3 36.2 %collective-permute-start.31 = (bf16[2,144,2048]{2,1,0:T(8,128)(2,1)S(1)}, bf16[2,144,2048]{2,1,0:T(8,128)(2,1)S(1)}, u32[]{:S(2)}, u32[]{:S(2)}) collective-permute-start(bf16[2,144,2048]{2,1,0:T(8,128)(2,1)S(1)} %copy-done.28), channel_id=1, source_target_pairs={{0,4},{4,0},{8,12},{12,8},{16,20},{20,16},{24,28},{28,24},{1,5},{5... | collective-permute-start | bytes 3538952 | tf_op jit(solution)/shard_map/ppermute | solution.py:898
  161.5 36.1 %collective-permute-start.32 = (bf16[2,144,2048]{2,1,0:T(8,128)(2,1)}, bf16[2,144,2048]{2,1,0:T(8,128)(2,1)}, u32[]{:S(2)}, u32[]{:S(2)}) collective-permute-start(bf16[2,144,2048]{2,1,0:T(8,128)(2,1)} %collective-permute-done.22.rest_2_), channel_id=1, source_target_pairs={{0,4},{4,0},{8,12},{12,8},{16,20},{20,16},{24,28},{28,24},{1,5},{5... | collective-permute-start | bytes 3538952 | tf_op jit(solution)/shard_map/ppermute | solution.py:898
  161.9 35.7 %collective-permute-start.33 = (bf16[2,144,2048]{2,1,0:T(8,128)(2,1)}, bf16[2,144,2048]{2,1,0:T(8,128)(2,1)}, u32[]{:S(2)}, u32[]{:S(2)}) collective-permute-start(bf16[2,144,2048]{2,1,0:T(8,128)(2,1)} %collective-permute-done.23.rest_4_), channel_id=1, source_target_pairs={{0,4},{4,0},{8,12},{12,8},{16,20},{20,16},{24,28},{28,24},{1,5},{5... | collective-permute-start | bytes 3538952 | tf_op jit(solution)/shard_map/ppermute | solution.py:898
  162.0 34.3 %collective-permute-start.29 = (bf16[144,2048]{1,0:T(8,128)(2,1)}, bf16[144,2048]{1,0:T(8,128)(2,1)}, u32[]{:S(2)}, u32[]{:S(2)}) collective-permute-start(bf16[144,2048]{1,0:T(8,128)(2,1)} %slice_bitcast_fusion.14), channel_id=1, source_target_pairs={{0,8},{4,12},{8,0},{12,4},{16,24},{20,28},{24,16},{28,20},{1,9},{5... | collective-permute-start | bytes 1769480 | tf_op jit(solution)/shard_map/ppermute | solution.py:898
  233.4 47.5 %collective-permute-start.40 = (bf16[2,144,2304]{2,1,0:T(8,128)(2,1)}, bf16[2,144,2304]{2,1,0:T(8,128)(2,1)S(1)}, u32[]{:S(2)}, u32[]{:S(2)}) collective-permute-start(bf16[2,144,2304]{2,1,0:T(8,128)(2,1)} %get-tuple-element.144), channel_id=1, source_target_pairs={{0,8},{4,12},{8,0},{12,4},{16,24},{20,28},{24,16},{28,20},{1,9},{5... | collective-permute-start | bytes 3981320 | tf_op jit(solution)/shard_map/ppermute | solution.py:898
  234.3 47.9 %collective-permute-start.41 = (bf16[2,144,2304]{2,1,0:T(8,128)(2,1)}, bf16[2,144,2304]{2,1,0:T(8,128)(2,1)}, u32[]{:S(2)}, u32[]{:S(2)}) collective-permute-start(bf16[2,144,2304]{2,1,0:T(8,128)(2,1)} %get-tuple-element.145), channel_id=1, source_target_pairs={{0,16},{4,20},{8,24},{12,28},{16,0},{20,4},{24,8},{28,12},{1,17},{... | collective-permute-start | bytes 3981320 | tf_op jit(solution)/shard_map/ppermute | solution.py:898
  275.6 62.0 %collective-permute-start.47 = (bf16[512,2304]{1,0:T(8,128)(2,1)}, bf16[512,2304]{1,0:T(8,128)(2,1)}, u32[]{:S(2)}, u32[]{:S(2)}) collective-permute-start(bf16[512,2304]{1,0:T(8,128)(2,1)} %get-tuple-element.159), channel_id=1, source_target_pairs={{0,4},{4,0},{8,12},{12,8},{16,20},{20,16},{24,28},{28,24},{1,5},{5... | collective-permute-start | bytes 7077896 | tf_op jit(solution)/shard_map/ppermute | solution.py:898
  280.9 34.2 %collective-permute-start.44 = (bf16[2,144,2048]{2,1,0:T(8,128)(2,1)}, bf16[2,144,2048]{2,1,0:T(8,128)(2,1)}, u32[]{:S(2)}, u32[]{:S(2)}) collective-permute-start(bf16[2,144,2048]{2,1,0:T(8,128)(2,1)} %get-tuple-element.152), channel_id=1, source_target_pairs={{0,16},{4,20},{8,24},{12,28},{16,0},{20,4},{24,8},{28,12},{1,17},{... | collective-permute-start | bytes 3538952 | tf_op jit(solution)/shard_map/ppermute | solution.py:898
  286.8 37.5 %collective-permute-start.45 = (bf16[1,144,2304]{2,1,0:T(8,128)(2,1)}, bf16[1,144,2304]{2,1,0:T(8,128)(2,1)S(1)}, u32[]{:S(2)}, u32[]{:S(2)}) collective-permute-start(bf16[1,144,2304]{2,1,0:T(8,128)(2,1)} %get-tuple-element.155), channel_id=1, source_target_pairs={{0,16},{4,20},{8,24},{12,28},{16,0},{20,4},{24,8},{28,12},{1,17},{... | collective-permute-start | bytes 1990664 | tf_op jit(solution)/shard_map/ppermute | solution.py:898
  287.6 36.6 %collective-permute-start.46 = (bf16[1,144,2304]{2,1,0:T(8,128)(2,1)}, bf16[1,144,2304]{2,1,0:T(8,128)(2,1)S(1)}, u32[]{:S(2)}, u32[]{:S(2)}) collective-permute-start(bf16[1,144,2304]{2,1,0:T(8,128)(2,1)} %get-tuple-element.156), channel_id=1, source_target_pairs={{0,8},{4,12},{8,0},{12,4},{16,24},{20,28},{24,16},{28,20},{1,9},{5... | collective-permute-start | bytes 1990664 | tf_op jit(solution)/shard_map/ppermute | solution.py:898
  313.9 39.4 %collective-permute-start.49 = (bf16[2,144,640]{2,1,0:T(8,128)(2,1)S(1)}, bf16[2,144,640]{2,1,0:T(8,128)(2,1)S(1)}, u32[]{:S(2)}, u32[]{:S(2)}) collective-permute-start(bf16[2,144,640]{2,1,0:T(8,128)(2,1)S(1)} %copy-done.53), channel_id=1, source_target_pairs={{0,8},{4,12},{8,0},{12,4},{16,24},{20,28},{24,16},{28,20},{1,9},{5... | collective-permute-start | bytes 1105928 | tf_op jit(solution)/shard_map/ppermute | solution.py:898
  315.2 38.2 %collective-permute-start.50 = (bf16[2,144,640]{2,1,0:T(8,128)(2,1)S(1)}, bf16[2,144,640]{2,1,0:T(8,128)(2,1)S(1)}, u32[]{:S(2)}, u32[]{:S(2)}) collective-permute-start(bf16[2,144,640]{2,1,0:T(8,128)(2,1)S(1)} %copy-done.52), channel_id=1, source_target_pairs={{0,16},{4,20},{8,24},{12,28},{16,0},{20,4},{24,8},{28,12},{1,17},{... | collective-permute-start | bytes 1105928 | tf_op jit(solution)/shard_map/ppermute | solution.py:898
  329.9 53.9 %collective-permute-start.70 = (bf16[2,144,2304]{2,1,0:T(8,128)(2,1)}, bf16[2,144,2304]{2,1,0:T(8,128)(2,1)S(1)}, u32[]{:S(2)}, u32[]{:S(2)}) collective-permute-start(bf16[2,144,2304]{2,1,0:T(8,128)(2,1)} %third1.1.refs_0_.refs_2_), channel_id=1, source_target_pairs={{0,1},{3,2},{4,5},{7,6},{8,9},{11,10},{12,13},{15,14},{16,17},{19,... | collective-permute-start | bytes 3981320 | tf_op jit(solution)/shard_map/ppermute | solution.py:964
  336.7 53.7 %collective-permute-start.73 = (bf16[1,144,2048]{2,1,0:T(8,128)(2,1)}, bf16[1,144,2048]{2,1,0:T(8,128)(2,1)}, u32[]{:S(2)}, u32[]{:S(2)}) collective-permute-start(bf16[1,144,2048]{2,1,0:T(8,128)(2,1)} %get-tuple-element.188), channel_id=1, source_target_pairs={{0,16},{4,20},{8,24},{12,28},{16,0},{20,4},{24,8},{28,12},{1,17},{... | collective-permute-start | bytes 1769480 | tf_op jit(solution)/shard_map/ppermute | solution.py:898
  337.5 53.8 %collective-permute-start.74 = (bf16[1,144,2048]{2,1,0:T(8,128)(2,1)}, bf16[1,144,2048]{2,1,0:T(8,128)(2,1)}, u32[]{:S(2)}, u32[]{:S(2)}) collective-permute-start(bf16[1,144,2048]{2,1,0:T(8,128)(2,1)} %get-tuple-element.189), channel_id=1, source_target_pairs={{0,8},{4,12},{8,0},{12,4},{16,24},{20,28},{24,16},{28,20},{1,9},{5... | collective-permute-start | bytes 1769480 | tf_op jit(solution)/shard_map/ppermute | solution.py:898
  375.1 115.5 %collective-permute-start.48 = (bf16[2,576,1792]{2,1,0:T(8,128)(2,1)}, bf16[2,576,1792]{2,1,0:T(8,128)(2,1)}, u32[]{:S(2)}, u32[]{:S(2)}) collective-permute-start(bf16[2,576,1792]{2,1,0:T(8,128)(2,1)} %get-tuple-element.161), channel_id=1, source_target_pairs={{0,4},{4,0},{8,12},{12,8},{16,20},{20,16},{24,28},{28,24},{1,5},{5... | collective-permute-start | bytes 12386312 | tf_op jit(solution)/shard_map/ppermute | solution.py:898
  391.4 40.5 %collective-permute-start.71 = (bf16[2,144,2304]{2,1,0:T(8,128)(2,1)}, bf16[2,144,2304]{2,1,0:T(8,128)(2,1)S(1)}, u32[]{:S(2)}, u32[]{:S(2)}) collective-permute-start(bf16[2,144,2304]{2,1,0:T(8,128)(2,1)} %inner1.1.refs_0_.refs_2_), channel_id=1, source_target_pairs={{1,2},{2,1},{5,6},{6,5},{9,10},{10,9},{13,14},{14,13},{17,18},{18,... | collective-permute-start | bytes 3981320 | tf_op jit(solution)/shard_map/ppermute | solution.py:968
  403.8 38.4 %collective-permute-start.75 = (bf16[2,144,2048]{2,1,0:T(8,128)(2,1)}, bf16[2,144,2048]{2,1,0:T(8,128)(2,1)S(1)}, u32[]{:S(2)}, u32[]{:S(2)}) collective-permute-start(bf16[2,144,2048]{2,1,0:T(8,128)(2,1)} %third2.1.refs_0_.refs_2_), channel_id=1, source_target_pairs={{0,1},{3,2},{4,5},{7,6},{8,9},{11,10},{12,13},{15,14},{16,17},{19,... | collective-permute-start | bytes 3538952 | tf_op jit(solution)/shard_map/ppermute | solution.py:964
  436.6 64.8 %collective-permute-start.72 = (bf16[2,144,2304]{2,1,0:T(8,128)(2,1)}, bf16[2,144,2304]{2,1,0:T(8,128)(2,1)}, u32[]{:S(2)}, u32[]{:S(2)}) collective-permute-start(bf16[2,144,2304]{2,1,0:T(8,128)(2,1)} %total1.1), channel_id=1, source_target_pairs={{1,0},{2,3},{5,4},{6,7},{9,8},{10,11},{13,12},{14,15},{17,16},{18,... | collective-permute-start | bytes 3981320 | tf_op jit(solution)/shard_map/ppermute | solution.py:972
  440.7 49.7 %collective-permute-start.69 = (bf16[2,144,640]{2,1,0:T(8,128)(2,1)}, bf16[2,144,640]{2,1,0:T(8,128)(2,1)S(1)}, u32[]{:S(2)}, u32[]{:S(2)}) collective-permute-start(bf16[2,144,640]{2,1,0:T(8,128)(2,1)} %totalo.1), channel_id=1, source_target_pairs={{1,0},{2,3},{5,4},{6,7},{9,8},{10,11},{13,12},{14,15},{17,16},{18,... | collective-permute-start | bytes 1105928 | tf_op jit(solution)/shard_map/ppermute | solution.py:972
  445.7 50.8 %collective-permute-start.76 = (bf16[2,144,2048]{2,1,0:T(8,128)(2,1)}, bf16[2,144,2048]{2,1,0:T(8,128)(2,1)S(1)}, u32[]{:S(2)}, u32[]{:S(2)}) collective-permute-start(bf16[2,144,2048]{2,1,0:T(8,128)(2,1)} %inner2.1.refs_0_.refs_2_), channel_id=1, source_target_pairs={{1,2},{2,1},{5,6},{6,5},{9,10},{10,9},{13,14},{14,13},{17,18},{18,... | collective-permute-start | bytes 3538952 | tf_op jit(solution)/shard_map/ppermute | solution.py:968
  500.2 42.3 %collective-permute-start.77 = (bf16[2,144,2048]{2,1,0:T(8,128)(2,1)}, bf16[2,144,2048]{2,1,0:T(8,128)(2,1)}, u32[]{:S(2)}, u32[]{:S(2)}) collective-permute-start(bf16[2,144,2048]{2,1,0:T(8,128)(2,1)} %total2.1), channel_id=1, source_target_pairs={{1,0},{2,3},{5,4},{6,7},{9,8},{10,11},{13,12},{14,15},{17,16},{18,... | collective-permute-start | bytes 3538952 | tf_op jit(solution)/shard_map/ppermute | solution.py:972
  585.6 53.8 %collective-permute-start.64 = (bf16[2,144,1792]{2,1,0:T(8,128)(2,1)}, bf16[2,144,1792]{2,1,0:T(8,128)(2,1)S(1)}, u32[]{:S(2)}, u32[]{:S(2)}) collective-permute-start(bf16[2,144,1792]{2,1,0:T(8,128)(2,1)} %totalq.1), channel_id=1, source_target_pairs={{1,0},{2,3},{5,4},{6,7},{9,8},{10,11},{13,12},{14,15},{17,16},{18,... | collective-permute-start | bytes 3096584 | tf_op jit(solution)/shard_map/ppermute | solution.py:972
  (101 other events, 1205.4 us)

commit v2 on v1

--- a/solution.py
+++ b/solution.py
@@ -488,21 +488,56 @@
         body(pl.ds(pl.multiple_of(r * ROWBLK, ROWBLK), ROWBLK))
 
 
-def unit_copies(pieces, half, cols, dst, sem):
+MESH = pl.DeviceIdType.MESH
+
+
+def flipped_index(d, mask):
+    for bit in (1, 2, 4):
+        if mask & bit:
+            d = d + bit - 2 * bit * lax.rem(lax.div(d, bit), 2)
+    return d
+
+
+def sibling():
+    return flipped_index(lax.axis_index("dp"), 1), lax.axis_index("seq")
+
+
+def meet_sibling():
+    barrier = pltpu.get_barrier_semaphore()
+    pl.semaphore_signal(barrier, inc=1, device_id=sibling(), device_id_type=MESH)
+    pl.semaphore_wait(barrier, 1)
+
+
+def to_sibling(src, dst, sem, i):
+    return pltpu.make_async_remote_copy(
+        src_ref=src, dst_ref=dst, send_sem=sem.at[1, i], recv_sem=sem.at[2, i], device_id=sibling(), device_id_type=MESH
+    )
+
+
+def unit_copies(pieces, half, rows, cols, place, sem):
     d = lax.axis_index("dp")
-    own, c0, xr, cx, yr, cy, da, db, cda, cdb = pieces
-    six, seven = (da, cda) if half == 0 else (db, cdb)
-    rows = own.shape[1]
-    sources = (own, c0, xr, cx, yr, cy)
+    own, xr, yr, da, db = pieces
     copies = []
-    for m in range(8):
-        if m < 6:
-            src = sources[m].at[half, :, cols]
-        else:
-            src = (six if m == 6 else seven).at[:, cols]
-        where = pl.ds(pl.multiple_of(jnp.bitwise_xor(d, m) * rows, rows), rows)
-        copies.append(pltpu.make_async_copy(src, dst.at[where, :], sem.at[m]))
+    for i, piece in enumerate((own, xr, yr, da if half == 0 else db)):
+        src = piece.at[half, rows, cols] if i < 3 else piece.at[rows, cols]
+        dst = place(flipped_index(d, 2 * i))
+        copies.append(pltpu.make_async_copy(src, dst, sem.at[0, i]))
+        copies.append(to_sibling(src, dst, sem, i))
     return copies
+
+
+def shard_rows(ref, count):
+    return lambda j: ref.at[pl.ds(pl.multiple_of(j * count, count), count), :]
+
+
+def start_all(copies):
+    for c in copies:
+        c.start()
+
+
+def wait_all(copies):
+    for c in copies:
+        c.wait()
 
 
 def norm_rows(v, gain, offset):
@@ -522,29 +557,60 @@
         flipped[cols, :] = src[:, cols].T
 
     for i, m in enumerate(ORDER):
-        where = pl.ds(pl.multiple_of(jnp.bitwise_xor(d, m) * part, part), part)
+        where = pl.ds(pl.multiple_of(flipped_index(d, m) * part, part), part)
         dst[i * part : (i + 1) * part, :] = flipped[where, :]
 
 
-def kv_kernel(x_ref, vec_ref, *rest):
-    pieces, (n_ref, kv_ref, w, sem) = rest[:10], rest[10:]
+def spread(buf, out_ref, part, span):
+    inside = (part + 127) // 128 * 128
+
+    @pl.loop(0, 8)
+    def _(j):
+        at = pl.multiple_of(jnp.minimum(j * part // 128, (out_ref.shape[1] - span) // 128) * 128, 128)
+        r = lax.broadcasted_iota(jnp.int32, (inside, span), 0)
+        c = lax.broadcasted_iota(jnp.int32, (inside, span), 1)
+        place = jnp.where((c == r + (j * part - at)) & (r < part), 1.0, 0.0).astype(bf16)
+        out_ref[0:16, pl.ds(at, span)] += nn(buf[j][:, 0:inside], place)
+
+
+def kv_kernel(ff, x_ref, *rest):
+    pieces, (n_ref, kv_ref, vec_ref, b1_ref, wkv_ref, w, buf, sem, out_sem) = rest[:5], rest[5:]
     width = x_ref.shape[1]
-    copies = unit_copies(pieces, 1, pl.ds(0, 2 * width), w, sem)
-    for c in copies:
-        c.start()
+    part = width // 8
+    every = pl.ds(0, width)
+    meet_sibling()
+    vectors, weights = [], []
+    for half in range(2):
+        vectors += unit_copies(pieces, half, pl.ds(part, 16), every, lambda j, half=half: buf.at[half, j], sem.at[2 + half])
+    for half in range(2):
+        weights += unit_copies(pieces, half, pl.ds(0, part), every, shard_rows(w.at[half], part), sem.at[half])
+    start_all(vectors + weights)
+    vec_ref[...] = jnp.zeros(vec_ref.shape, f32)
+    b1_ref[...] = jnp.zeros(b1_ref.shape, f32)
+    wait_all(vectors)
+    spread(buf.at[0], vec_ref, part, 512)
 
     def body(rows):
         v = x_ref[rows, :].astype(f32)
-        n_ref[rows, :] = norm_rows(v, vec_ref[0:1, 0:width], vec_ref[1:2, 0:width]).astype(bf16)
+        n_ref[rows, :] = norm_rows(v, vec_ref[0:1, :], vec_ref[1:2, :]).astype(bf16)
 
     row_loop(x_ref.shape[0], body)
-    for c in copies:
-        c.wait()
-
-    @pl.loop(0, 2 * width // 256)
-    def _(t):
-        cols = pl.ds(pl.multiple_of(t * 256, 256), 256)
-        kv_ref[:, cols] = (nn(n_ref[...], w[:, cols]) + vec_ref[8:9, cols]).astype(bf16)
+    wait_all(weights)
+    store = pltpu.make_async_copy(w, wkv_ref, out_sem)
+    store.start()
+
+    def keys(cols):
+        kv_ref[:, cols] = nn(n_ref[...], w[0, :, cols]).astype(bf16)
+
+    column_tiles(width, keys)
+
+    def values(cols):
+        total = nn(n_ref[...], w[1, :, cols]) + vec_ref[3:4, cols]
+        kv_ref[:, pl.ds(pl.multiple_of(cols.start + width, 128), cols.size)] = total.astype(bf16)
+
+    column_tiles(width, values)
+    spread(buf.at[1], b1_ref, ff // 8, 768)
+    store.wait()
 
 
 def column_tiles(width, body):
@@ -559,19 +625,25 @@
 
 
 def q_kernel(n_ref, vec_ref, *rest):
-    pieces, (q_ref, nt_ref, w, flipped, sem) = rest[:10], rest[10:]
+    pieces, (q_ref, nt_ref, wq_ref, wo_ref, w, flipped, sem, out_sem) = rest[:5], rest[5:]
     width = n_ref.shape[1]
-    copies = unit_copies(pieces, 0, pl.ds(0, width), w, sem)
-    for c in copies:
-        c.start()
+    part = width // 8
+    meet_sibling()
+    halves = [
+        unit_copies(pieces, half, pl.ds(0, part), pl.ds(0, width), shard_rows(w.at[half], part), sem.at[half]) for half in range(2)
+    ]
+    start_all(halves[0] + halves[1])
     transpose_ordered(n_ref, flipped, nt_ref)
-    for c in copies:
-        c.wait()
+    wait_all(halves[0])
 
     def body(cols):
-        q_ref[:, cols] = (nn(n_ref[...], w[:, cols]) + vec_ref[2:3, cols]).astype(bf16)
+        q_ref[:, cols] = (nn(n_ref[...], w[0, :, cols]) + vec_ref[2:3, cols]).astype(bf16)
 
     column_tiles(width, body)
+    wait_all(halves[1])
+    stores = [pltpu.make_async_copy(w.at[i], out, out_sem.at[i]) for i, out in ((0, wq_ref), (1, wo_ref))]
+    start_all(stores)
+    wait_all(stores)
 
 
 def head_window(h, width):
@@ -623,55 +695,71 @@
     lse_ref[...] = lse_cols[...].T[:HEADS, :]
 
 
-def attention_backward_kernel(near, q_ref, kv_ref, go_ref, lse_ref, del_ref, kid_ref, qid_ref, dqp_ref, dq_ref, dkv_ref, bias, dqa, dka):
+def attention_backward_kernel(
+    h0, h1, base, done, q_ref, kn_ref, kf_ref, go_ref, lse_ref, del_ref, kid_ref, qid_ref, cin_ref,
+    dq_ref, dkn_ref, dkf_ref, cout_ref, bias, acc
+):
     tokens, width = q_ref.shape
+    span = acc.shape[2]
     scale, unit = HD**-0.5 * LOG2E, HD**-0.5
+
+    @pl.loop(0, 2 * tokens // ROWBLK)
+    def _(r):
+        rows = pl.ds(pl.multiple_of(r * ROWBLK, ROWBLK), ROWBLK)
+        col = lax.broadcasted_iota(jnp.int32, (ROWBLK, tokens), 1)
+        row = lax.broadcasted_iota(jnp.int32, (ROWBLK, tokens), 0) + r * ROWBLK
+        allowed = (kid_ref[rows, 0:1] == qid_ref[0:1, :]) | (col == row)
+        bias[rows, :] = jnp.where(allowed, 0.0, big_negative)
 
     @pl.loop(0, tokens // ROWBLK)
     def _(r):
         rows = pl.ds(pl.multiple_of(r * ROWBLK, ROWBLK), ROWBLK)
-        allowed = kid_ref[rows, 0:1] == qid_ref[0:1, :]
-        if near:
-            col = lax.broadcasted_iota(jnp.int32, (ROWBLK, tokens), 1)
-            row = lax.broadcasted_iota(jnp.int32, (ROWBLK, tokens), 0) + r * ROWBLK
-            allowed = allowed | (col == row)
-        bias[rows, :] = jnp.where(allowed, 0.0, big_negative)
-        dka[rows, :] = jnp.zeros((ROWBLK, 2 * width), f32)
-        dqa[rows, :] = dqp_ref[rows, :] if near else jnp.zeros((ROWBLK, width), f32)
-
-    @pl.loop(0, HEADS)
+        for i in range(5):
+            if base == 0:
+                acc[i, rows, :] = jnp.zeros((ROWBLK, span), f32)
+            else:
+                acc[i, rows, 0:128] = cin_ref[i, rows, :]
+                acc[i, rows, 128:span] = jnp.zeros((ROWBLK, span - 128), f32)
+
+    @pl.loop(h0, h1)
     def _(h):
         w0, mask = head_window(h, width)
         win, winv = pl.ds(w0, WIN), pl.ds(w0 + width, WIN)
+        at = pl.ds(pl.multiple_of(w0 - base, 128), WIN)
         zero = jnp.zeros((), bf16)
         qw = q_ref[:, win]
         qm, gm = jnp.where(mask, qw, zero), jnp.where(mask, go_ref[:, win], zero)
         lse, inner = lse_ref[pl.ds(h, 1), :], del_ref[pl.ds(h, 1), :]
-        km, vw = jnp.where(mask, kv_ref[:, win], zero), kv_ref[:, winv]
-        pt = jnp.exp2(nt(km, qw) * scale + bias[...] - lse)
-        dka[:, winv] += nn(pt.astype(bf16), gm)
-        ds = (pt * (nt(vw, gm) - inner)).astype(bf16)
-        dka[:, win] += nn(ds, qm)
-        dqa[:, win] += tn(ds, km)
+        dq = None
+        for b, kref in ((0, kn_ref), (1, kf_ref)):
+            km, vw = jnp.where(mask, kref[:, win], zero), kref[:, winv]
+            pt = jnp.exp2(nt(km, qw) * scale + bias[b * tokens : (b + 1) * tokens, :] - lse)
+            acc[2 + 2 * b, :, at] += nn(pt.astype(bf16), gm)
+            ds = (pt * (nt(vw, gm) - inner)).astype(bf16)
+            acc[1 + 2 * b, :, at] += nn(ds, qm)
+            part = tn(ds, km)
+            dq = part if dq is None else dq + part
+        acc[0, :, at] += dq
+
+    if span == done:
+        cout_ref[...] = jnp.zeros(cout_ref.shape, f32)
 
     @pl.loop(0, tokens // ROWBLK)
     def _(r):
         rows = pl.ds(pl.multiple_of(r * ROWBLK, ROWBLK), ROWBLK)
-        dq_ref[rows, :] = (dqa[rows, :] * unit).astype(bf16) if near else dqa[rows, :]
-        dkv_ref[rows, 0:width] = (dka[rows, 0:width] * unit).astype(dkv_ref.dtype)
-        dkv_ref[rows, width : 2 * width] = dka[rows, width : 2 * width].astype(dkv_ref.dtype)
-
-
-def middle_kernel(att_ref, x_ref, cot_ref, vec_ref, *rest):
-    pieces, (mid_ref, n2_ref, n2t_ref, cott_ref, attt_ref, w, flipped, sem) = rest[:10], rest[10:]
+        dq_ref[rows, :] = (acc[0, rows, 0:done] * unit).astype(bf16)
+        for b, out in ((0, dkn_ref), (1, dkf_ref)):
+            out[rows, 0:done] = (acc[1 + 2 * b, rows, 0:done] * unit).astype(out.dtype)
+            out[rows, done : 2 * done] = acc[2 + 2 * b, rows, 0:done].astype(out.dtype)
+        for i in range(5):
+            if span > done:
+                cout_ref[i, rows, :] = acc[i, rows, done : done + 128]
+
+
+def middle_kernel(att_ref, x_ref, cot_ref, vec_ref, w, mid_ref, n2_ref, n2t_ref, cott_ref, attt_ref, flipped):
     tokens, width = x_ref.shape
-    copies = unit_copies(pieces, 0, pl.ds(width, width), w, sem)
-    for c in copies:
-        c.start()
     transpose_ordered(cot_ref, flipped, cott_ref)
     transpose_ordered(att_ref, flipped, attt_ref)
-    for c in copies:
-        c.wait()
 
     def body(cols):
         mid_ref[:, cols] = nn(att_ref[...], w[:, cols]) + vec_ref[4:5, cols] + x_ref[:, cols].astype(f32)
@@ -685,26 +773,39 @@
     transpose_ordered(n2_ref, flipped, n2t_ref)
 
 
-def mlp_kernel(first, last, n2_ref, cot_ref, n2t_ref, cott_ref, b1_ref, vec_ref, outp_ref, gnp_ref, *rest):
-    pieces = rest[:10]
-    out_ref, gn_ref, keep_ref, send_ref, gb1_ref, wbuf, acc, gacc, sem = rest[10:]
-    t, steps = pl.program_id(0), pl.num_programs(0)
+def store_blocks(half, total, part, keep, send, cols):
+    kept = (0, 2) if half == 0 else (0, 1)
+    sent = (1, 3) if half == 0 else (2, 3)
+    for i in range(2):
+        keep[i, :, cols] = total[kept[i] * part : (kept[i] + 1) * part]
+        send[i, :, cols] = total[sent[i] * part : (sent[i] + 1) * part]
+
+
+def mlp_kernel(first, last, aliased, n2_ref, cot_ref, n2t_ref, cott_ref, b1_ref, vec_ref, outp_ref, gnp_ref, *rest):
+    pieces = rest[:5]
+    out_ref, gn_ref, ka_ref, sa_ref, kb_ref, sb_ref, gb1_ref, wbuf, acc, gacc, mine, theirs, came, sem, gsem, credit = (
+        rest[9 if aliased else 5 :])
+    t, steps = pl.program_id(0), pl.num_programs(0) - 1
     width = n2_ref.shape[1]
-    tile = wbuf.shape[-1]
+    tile, part = wbuf.shape[-1], width // 8
     half = width // 2
-
-    def copies(step, slot):
+    slot = lax.rem(t, 2)
+    before = 1 - slot
+
+    def copies(step, to):
         cols = pl.ds(pl.multiple_of(step * tile, tile), tile)
-        return unit_copies(pieces, 0, cols, wbuf.at[slot, 0], sem.at[slot, 0]) + unit_copies(
-            pieces, 1, cols, wbuf.at[slot, 1], sem.at[slot, 1]
-        )
-
-    slot = lax.rem(t, 2)
+        every = []
+        for h in range(2):
+            every += unit_copies(pieces, h, pl.ds(0, part), cols, shard_rows(wbuf.at[to, h], part), sem.at[to, h])
+        return every
+
+    def exchange(at, h):
+        return to_sibling(theirs.at[at, h], came.at[at, h], gsem.at[at], h)
 
     @pl.when(t == 0)
     def _():
-        for c in copies(0, 0):
-            c.start()
+        meet_sibling()
+        start_all(copies(0, 0))
 
         def init(rows):
             acc[rows, :] = outp_ref[rows, :] + vec_ref[7:8, 0:width] if first else outp_ref[rows, :]
@@ -712,69 +813,102 @@
 
         row_loop(n2_ref.shape[0], init)
 
+    @pl.when((t > 0) & (t < steps))
+    def _():
+        pl.semaphore_wait(credit, 1)
+
     @pl.when(t + 1 < steps)
     def _():
-        for c in copies(t + 1, 1 - slot):
-            c.start()
-
-    for c in copies(t, slot):
-        c.wait()
-    w1, w2 = wbuf[slot, 0], wbuf[slot, 1]
-    u = nn(n2_ref[...], w1) + b1_ref[...]
-    c0 = 0.7978845608028654
-    th = jnp.tanh(c0 * (u + 0.044715 * u * u * u))
-    active = (0.5 * u * (1.0 + th)).astype(bf16)
-    slope = 0.5 * (1.0 + th) + 0.5 * u * (1.0 - th * th) * (c0 * (1.0 + 3 * 0.044715 * u * u))
-    gh = (nn(cot_ref[...], w2) * slope).astype(bf16)
-    gb1_ref[...] = jnp.sum(gh.astype(f32), axis=0, keepdims=True)
-    acc[...] += nt(active, w2)
-    gacc[...] += nt(gh, w1)
-    g1 = nn(n2t_ref[...], gh).astype(bf16)
-    keep_ref[0], send_ref[0] = g1[:half], g1[half:]
-    g2 = nn(cott_ref[...], active).astype(bf16)
-    keep_ref[1], send_ref[1] = g2[:half], g2[half:]
-
-    @pl.when(t == steps - 1)
+        start_all(copies(t + 1, before))
+
+    @pl.when(t < steps)
+    def _():
+        wait_all(copies(t, slot))
+        w1, w2 = wbuf[slot, 0], wbuf[slot, 1]
+        u = nn(n2_ref[...], w1) + b1_ref[0:1, :]
+        c0 = 0.7978845608028654
+        th = jnp.tanh(c0 * (u + 0.044715 * u * u * u))
+        active = (0.5 * u * (1.0 + th)).astype(bf16)
+        slope = 0.5 * (1.0 + th) + 0.5 * u * (1.0 - th * th) * (c0 * (1.0 + 3 * 0.044715 * u * u))
+        gh = (nn(cot_ref[...], w2) * slope).astype(bf16)
+        gb1_ref[...] = jnp.sum(gh.astype(f32), axis=0, keepdims=True)
+        g1 = nn(n2t_ref[...], gh).astype(bf16)
+        mine[slot, 0], theirs[slot, 0] = g1[:half], g1[half:]
+        exchange(slot, 0).start()
+        g2 = nn(cott_ref[...], active).astype(bf16)
+        mine[slot, 1], theirs[slot, 1] = g2[:half], g2[half:]
+        exchange(slot, 1).start()
+        acc[...] += nt(active, w2)
+        gacc[...] += nt(gh, w1)
+
+    @pl.when(t > 0)
+    def _():
+        for h, keep, send in ((0, ka_ref, sa_ref), (1, kb_ref, sb_ref)):
+            exchange(before, h).wait()
+            total = (mine[before, h].astype(f32) + came[before, h].astype(f32)).astype(bf16)
+            store_blocks(h, total, part, keep, send, slice(None))
+
+    @pl.when(t < steps - 1)
+    def _():
+        pl.semaphore_signal(credit, inc=1, device_id=sibling(), device_id_type=MESH)
+
+    @pl.when(t == steps)
     def _():
         out_ref[...] = acc[...].astype(out_ref.dtype)
         gn_ref[...] = gacc[...]
 
 
-def mlp_call(first, last, n2, cot, n2t, cott, b1, vec, outp, gnp, pieces):
+def mlp_call(name, first, last, n2, cot, n2t, cott, b1, vec, outp, gnp, pieces, begin, total, into=None, collective=0):
     tokens, width = n2.shape
     cols, tile = pieces[0].shape[2], 256
+    steps = cols // tile
     const = lambda a: pl.BlockSpec(a.shape, lambda t: (0,) * a.ndim, pipeline_mode=pl.Buffered(1))
-    out_type = bf16 if last else f32
+    skip = 0 if into is None else (total - cols) // tile
+    grads = pl.BlockSpec((2, width // 8, tile), lambda t: (0, 0, jnp.maximum(t - 1, 0) + skip))
+    hidden = lambda t: jnp.minimum(t, steps - 1)
+    args = (n2, cot, n2t, cott, b1, vec, outp, gnp, *pieces)
+    grad = sds((2, width // 8, total), bf16)
     return pl.pallas_call(
-        functools.partial(mlp_kernel, first, last),
-        grid=(cols // tile,),
-        in_specs=[const(n2), const(cot), const(n2t), const(cott), pl.BlockSpec((1, tile), lambda t: (0, t)), const(vec),
-                  const(outp), const(gnp)] + [ANY] * 10,
+        functools.partial(mlp_kernel, first, last, into is not None),
+        grid=(steps + 1,),
+        in_specs=[const(n2), const(cot), const(n2t), const(cott), pl.BlockSpec((8, tile), lambda t: (0, hidden(t) + begin // tile)),
+                  const(vec), const(outp), const(gnp)] + [ANY] * (5 if into is None else 9),
         out_specs=(
             pl.BlockSpec((tokens, width), lambda t: (0, 0)),
             pl.BlockSpec((tokens, width), lambda t: (0, 0)),
-            pl.BlockSpec((2, width // 2, tile), lambda t: (0, 0, t)),
-            pl.BlockSpec((2, width // 2, tile), lambda t: (0, 0, t)),
-            pl.BlockSpec((1, tile), lambda t: (0, t)),
+            grads,
+            grads,
+            grads,
+            grads,
+            pl.BlockSpec((1, tile), lambda t: (0, hidden(t))),
         ),
         out_shape=(
-            sds((tokens, width), out_type),
+            sds((tokens, width), bf16 if last else f32),
             sds((tokens, width), f32),
-            sds((2, width // 2, cols), bf16),
-            sds((2, width // 2, cols), bf16),
+            grad,
+            grad,
+            grad,
+            grad,
             sds((1, cols), f32),
         ),
+        input_output_aliases={} if into is None else {len(args) + i: 2 + i for i in range(4)},
         scratch_shapes=[
             pltpu.VMEM((2, 2, width, tile), bf16),
             pltpu.VMEM((tokens, width), f32),
             pltpu.VMEM((tokens, width), f32),
-            pltpu.SemaphoreType.DMA((2, 2, 8)),
+            pltpu.VMEM((2, 2, width // 2, tile), bf16),
+            pltpu.VMEM((2, 2, width // 2, tile), bf16),
+            pltpu.VMEM((2, 2, width // 2, tile), bf16),
+            pltpu.SemaphoreType.DMA((2, 2, 3, 4)),
+            pltpu.SemaphoreType.DMA((2, 3, 2)),
+            pltpu.SemaphoreType.REGULAR,
         ],
+        compiler_params=pltpu.CompilerParams(collective_id=collective, has_side_effects=True),
         cost_estimate=pl.CostEstimate(
             flops=12 * tokens * width * cols, bytes_accessed=8 * width * cols + 12 * tokens * width, transcendentals=tokens * cols
         ),
-        name="mlp_first" if first else "mlp_last",
-    )(n2, cot, n2t, cott, b1, vec, outp, gnp, *pieces)
+        name=name,
+    )(*args, *(() if into is None else into))
 
 
 def norm_back(v, g, gain):
@@ -786,12 +920,10 @@
     return grad, g * n
 
 
-def branch_kernel(cot_ref, gn_ref, mid_ref, vec_ref, att_ref, attt_ref, *rest):
-    pieces, (gm_ref, ga_ref, keep_ref, send_ref, sums_ref, del_ref, w, gb, sem) = rest[:10], rest[10:]
+def branch_kernel(cot_ref, gn_ref, mid_ref, vec_ref, att_ref, attt_ref, w, gm_ref, ga_ref, sums_ref, del_ref,
+                  ka_ref, sa_ref, kb_ref, sb_ref, gb, mine, theirs, came, sem):
     tokens, width = cot_ref.shape
-    copies = unit_copies(pieces, 0, pl.ds(width, width), w, sem)
-    for c in copies:
-        c.start()
+    meet_sibling()
     sums_ref[...] = jnp.zeros(sums_ref.shape, f32)
 
     def body(rows):
@@ -808,13 +940,13 @@
         sums_ref[3:4, :] += jnp.sum(cot, axis=0, keepdims=True)
 
     row_loop(tokens, body)
-    half, part = width // 2, keep_ref.shape[-1]
+    half, part = width // 2, mine.shape[-1]
+    exchanges = [to_sibling(theirs.at[i], came.at[i], sem, i) for i in range(2)]
     for i in range(2):
         at = i * (width - part)
         g = nn(attt_ref[...], gb[:, at : at + part]).astype(bf16)
-        keep_ref[i], send_ref[i] = g[:half], g[half:]
-    for c in copies:
-        c.wait()
+        mine[i], theirs[i] = g[:half], g[half:]
+        exchanges[i].start()
     column = lax.broadcasted_iota(jnp.int32, (HEADS, 128), 1)
     first = lax.broadcasted_iota(jnp.int32, (HEADS, 128), 0) * HD
     del_ref[...] = jnp.zeros(del_ref.shape, f32)
@@ -831,18 +963,22 @@
         chosen = jnp.where((at >= first) & (at < first + HD), 1.0, 0.0).astype(bf16)
         del_ref[...] += nt(chosen, high) + nt(chosen, rest_low)
 
-
-def qkv_grad_kernel(nt_ref, dq_ref, dko_ref, dkr_ref, keep_ref, send_ref, dkv_ref, all_ref):
+    for i, keep, send in ((0, ka_ref, sa_ref), (1, kb_ref, sb_ref)):
+        exchanges[i].wait()
+        store_blocks(i, (mine[i].astype(f32) + came[i].astype(f32)).astype(bf16), width // 8, keep, send, slice(None))
+
+
+def qkv_grad_kernel(nt_ref, dq_ref, dko_ref, dkr_ref, all_ref, ka_ref, sa_ref, kb_ref, sb_ref, mine, theirs, came, sem):
     tokens, width = dq_ref.shape
-    half, part = width // 2, keep_ref.shape[-1]
+    half, part = nt_ref.shape[0] // 2, mine.shape[-1]
+    meet_sibling()
 
     def join(rows):
-        total = (dko_ref[rows, :] + dkr_ref[rows, :].astype(f32)).astype(bf16)
-        dkv_ref[rows, :] = total
         all_ref[rows, 0:width] = dq_ref[rows, :]
-        all_ref[rows, width : 3 * width] = total
+        all_ref[rows, width : 3 * width] = (dko_ref[rows, :] + dkr_ref[rows, :].astype(f32)).astype(bf16)
 
     row_loop(tokens, join)
+    exchanges = [to_sibling(theirs.at[i], came.at[i], sem, i) for i in range(2)]
     for i in range(2):
 
         @pl.loop(0, part // 256)
@@ -850,44 +986,69 @@
             cols = pl.ds(pl.multiple_of(t * 256, 256), 256)
             at = pl.ds(pl.multiple_of(t * 256 + i * (3 * width - part), 128), 256)
             g = nn(nt_ref[...], all_ref[:, at]).astype(bf16)
-            keep_ref[i, :, cols], send_ref[i, :, cols] = g[:half], g[half:]
-
-
-def input_grad_kernel(dq_ref, dkv_ref, x_ref, gm_ref, vec_ref, *rest):
-    pieces, (gx_ref, sums_ref, wq, wkv, gn, sem) = rest[:10], rest[10:]
-    tokens, width = x_ref.shape
-    copies = unit_copies(pieces, 0, pl.ds(0, width), wq, sem.at[0]) + unit_copies(
-        pieces, 1, pl.ds(0, 2 * width), wkv, sem.at[1]
-    )
-    for c in copies:
-        c.start()
+            mine[i, :, cols], theirs[i, :, cols] = g[:half], g[half:]
+
+        exchanges[i].start()
+
+    for i, keep, send in ((0, ka_ref, sa_ref), (1, kb_ref, sb_ref)):
+        exchanges[i].wait()
+
+        @pl.loop(0, part // 256)
+        def _(t):
+            cols = pl.ds(pl.multiple_of(t * 256, 256), 256)
+            total = (mine[i, :, cols].astype(f32) + came[i, :, cols].astype(f32)).astype(bf16)
+            store_blocks(i, total, half // 4, keep, send, cols)
+
+
+def normed_grad_kernel(g1_ref, g2_ref, wq_ref, wkv_ref, gn_ref, sums_ref, w, sem):
+    tokens, width = gn_ref.shape
+    a, b = g1_ref.shape[1] // 3, g2_ref.shape[1] // 3
+    copies = [pltpu.make_async_copy(wq_ref, w.at[0], sem.at[0]), pltpu.make_async_copy(wkv_ref, w.at[pl.ds(1, 2)], sem.at[1])]
+    start_all(copies)
     sums_ref[...] = jnp.zeros(sums_ref.shape, f32)
+
+    def body(rows):
+        for i, j in ((0, 0), (1, 2)):
+            sums_ref[i : i + 1, 0:a] += jnp.sum(g1_ref[rows, j * a : (j + 1) * a].astype(f32), axis=0, keepdims=True)
+            sums_ref[i : i + 1, a:width] += jnp.sum(g2_ref[rows, j * b : (j + 1) * b].astype(f32), axis=0, keepdims=True)
+
+    row_loop(tokens, body)
     for c in copies:
         c.wait()
 
-    @pl.loop(0, width // 128)
-    def _(j):
-        rows = pl.ds(pl.multiple_of(j * 128, 128), 128)
-        gn[:, rows] = nt(dq_ref[...], wq[rows, :]) + nt(dkv_ref[...], wkv[rows, :])
+    def columns(cols):
+        total = None
+        for i in range(3):
+            for g, lo, hi in ((g1_ref, 0, a), (g2_ref, a, width)):
+                term = nt(g[:, i * (hi - lo) : (i + 1) * (hi - lo)], w[i, cols, lo:hi])
+                total = term if total is None else total + term
+        gn_ref[:, cols] = total
+
+    column_tiles(width, columns)
+
+
+def input_grad_kernel(gn_ref, x_ref, gm_ref, vec_ref, gx_ref, sums_ref):
+    tokens, width = x_ref.shape
+    sums_ref[...] = jnp.zeros(sums_ref.shape, f32)
 
     def body(rows):
-        g = gn[rows, :]
+        g = gn_ref[rows, :]
         grad, gain_part = norm_back(x_ref[rows, :].astype(f32), g, vec_ref[0:1, 0:width])
         gx_ref[rows, :] = (gm_ref[rows, :] + grad).astype(bf16)
         sums_ref[0:1, :] += jnp.sum(gain_part, axis=0, keepdims=True)
         sums_ref[1:2, :] += jnp.sum(g, axis=0, keepdims=True)
-        sums_ref[2:3, :] += jnp.sum(dq_ref[rows, :].astype(f32), axis=0, keepdims=True)
-        sums_ref[3:4, :] += jnp.sum(dkv_ref[rows, width : 2 * width].astype(f32), axis=0, keepdims=True)
 
     row_loop(tokens, body)
 
 
-def call(body, name, outs, scratch, flops, moved, *args, pieces=()):
+def call(body, name, outs, scratch, flops, moved, *args, pieces=(), collective=None, far_outs=0):
+    params = {} if collective is None else {"collective_id": collective, "has_side_effects": True}
     return pl.pallas_call(
         body,
         out_shape=tuple(sds(s, t) for s, t in outs),
         in_specs=[VM] * len(args) + [ANY] * len(pieces),
-        out_specs=tuple(VM for _ in outs),
+        out_specs=(VM,) * (len(outs) - far_outs) + (ANY,) * far_outs,
+        compiler_params=pltpu.CompilerParams(**params),
         scratch_shapes=scratch,
         cost_estimate=pl.CostEstimate(flops=flops, bytes_accessed=moved, transcendentals=0),
         name=name,
@@ -935,47 +1096,6 @@
     )(*args)
 
 
-def blocks(v):
-    return v.reshape(2, 4, v.shape[1] // 4, v.shape[2])
-
-
-def unit_first(name, keep, got, size):
-    k, g = blocks(keep), blocks(got)
-    sa, sb = add_blocks(
-        name, [[(k, (0, j)), (g, (0, j))] for j in (1, 3)], [[(k, (1, j)), (g, (1, j))] for j in (2, 3)]
-    )
-    return swap(sa, 2, size), swap(sb, 4, size)
-
-
-def unit_second(name, keep, got, ax, by, size):
-    k, g = blocks(keep), blocks(got)
-    ta, tb = add_blocks(name, [[(k, (0, 2)), (g, (0, 2)), (ax, (1,))]], [[(k, (1, 1)), (g, (1, 1)), (by, (1,))]])
-    return swap(ta, 4, size), swap(tb, 2, size)
-
-
-def unit_third(name, keep, got, ax, by, ay, bx):
-    k, g = blocks(keep), blocks(got)
-    return add_blocks(
-        name, [[(k, (0, 0)), (g, (0, 0)), (ax, (0,)), (ay, (0,))], [(k, (1, 0)), (g, (1, 0)), (by, (0,)), (bx, (0,))]]
-    )[0]
-
-
-def fold_in(own):
-    return lax.ppermute(own, "seq", [(0, 1), (3, 2)])
-
-
-def across(inner):
-    return lax.ppermute(inner, "seq", [(1, 2), (2, 1)])
-
-
-def fold_out(total):
-    return lax.ppermute(total, "seq", [(1, 0), (2, 3)])
-
-
-def pair_sum(name, a, b):
-    return add_blocks(name, [[(a, (i,)), (b, (i,))] for i in range(a.shape[0])])[0]
-
-
 def reduce_small(rows, size):
     d = lax.axis_index("dp")
     bit, left = 1, rows
@@ -992,17 +1112,6 @@
     return left[0]
 
 
-def gather_small(row, size):
-    d = lax.axis_index("dp")
-    got, bit = row[None], 1
-    while bit < size:
-        other = swap(got, bit, size)
-        up = (d // bit) % 2 == 1
-        got = jnp.concatenate([jnp.where(up, other, got), jnp.where(up, got, other)], axis=0)
-        bit *= 2
-    return got
-
-
 def token_routes(size, depth):
     routes = []
     for s in range(2):
@@ -1035,6 +1144,68 @@
     return jnp.stack([jnp.where(odd, r1, r0), jnp.where(odd, r0, r1)])
 
 
+class Order:
+    def __init__(self):
+        self.tail, self.meetings = None, 0
+
+    def gate(self, v):
+        return v if self.tail is None else after(v, self.tail)
+
+    def call(self, body, name, outs, scratch, flops, moved, first, *args, pieces=(), meets=False, far_outs=0):
+        self.meetings += meets
+        got = call(body, name, outs, scratch, flops, moved, self.gate(first), *args, pieces=pieces,
+                   collective=self.meetings if meets else None, far_outs=far_outs)
+        self.tail = got[0]
+        return got
+
+    def mlp(self, name, first, last, n2, *args, **named):
+        self.meetings += 1
+        got = mlp_call(name, first, last, self.gate(n2), *args, collective=self.meetings, **named)
+        self.tail = got[2]
+        return got
+
+    def add(self, name, *outs):
+        (array, index), *terms = outs[0][0]
+        outs = ([[(self.gate(array), index), *terms], *outs[0][1:]], *outs[1:])
+        got = add_blocks(name, *outs)
+        self.tail = got[0]
+        return got
+
+
+class Reduction:
+    def __init__(self, name, order, size, keep_a, send_a, keep_b, send_b):
+        self.name, self.order, self.size = name, order, size
+        self.a, self.b = keep_a, keep_b
+        self.ax, self.by = swap(send_a, 2, size), swap(send_b, 4, size)
+
+    def second(self):
+        ta, tb = self.order.add(
+            "second" + self.name, [[(self.a, (1,)), (self.ax, (1,))]], [[(self.b, (1,)), (self.by, (1,))]]
+        )
+        self.ay, self.bx = swap(ta, 4, self.size), swap(tb, 2, self.size)
+
+    def third(self):
+        a = [(self.a, (0,)), (self.ax, (0,)), (self.ay, (0,))]
+        b = [(self.b, (0,)), (self.by, (0,)), (self.bx, (0,))]
+        self.own = self.order.add("third" + self.name, [a, b])[0]
+        self.inner = lax.ppermute(self.own, "seq", [(0, 1), (3, 2)])
+
+    def add_pair(self, name, a, b):
+        return self.order.add(name + self.name, [[(a, (i,)), (b, (i,))] for i in range(2)])[0]
+
+    def fourth(self):
+        self.half = self.add_pair("inner", self.own, self.inner)
+        self.across = lax.ppermute(self.half, "seq", [(1, 2), (2, 1)])
+
+    def fifth(self):
+        self.total = self.add_pair("total", self.half, self.across)
+        self.outer = lax.ppermute(self.total, "seq", [(1, 0), (2, 3)])
+
+    def result(self):
+        z = lax.axis_index("seq")
+        return jnp.where((z == 1) | (z == 2), self.total, self.order.gate(self.outer)).astype(f32)
+
+
 def by_rows(size, depth):
     def step(patches, picture_ids, valid_mask, ln1_gain, ln1_bias, w_qkv, bias_qv, w_out, b_out, ln2_gain, ln2_bias,
              w_fc1, b_fc1, w_fc2, b_fc2, cotangent):
@@ -1042,32 +1213,38 @@
         ff = w_fc1.shape[1]
         tokens = patches.shape[0] * patches.shape[1]
         part = width // size
-        d, z = lax.axis_index("dp"), lax.axis_index("seq")
-        core = d % 2
+        z, core = lax.axis_index("seq"), lax.axis_index("dp") % 2
         routes = token_routes(size, depth)
-
-        unit0 = jnp.stack([jnp.concatenate([w_qkv[:, :width], w_out], axis=1), w_qkv[:, width:]])
+        order = Order()
+        vm = pltpu.VMEM
+        act, flip = ((tokens, width), bf16), ((width, tokens), bf16)
+        act32 = ((tokens, width), f32)
+        mm = 2 * tokens * width * width
+
+        small = jnp.stack([ln1_gain, ln1_bias, bias_qv[0], bias_qv[1], b_out, ln2_gain, ln2_bias, b_fc2])
+        small = jnp.pad(small, ((0, 8), (0, width - part)))
+        bias = jnp.pad(b_fc1[None], ((0, 15), (0, width - ff // size)))
+        unit0 = jnp.stack([
+            jnp.concatenate([w_qkv[:, width : 2 * width], small]), jnp.concatenate([w_qkv[:, 2 * width :], bias])])
+        unit1 = jnp.stack([w_qkv[:, :width], w_out])
         extra = -ff % 256
+        tiles = (ff + extra) // 256
+        ends = [0, tiles // 2 * 256, (tiles - tiles // 5) * 256, tiles * 256]
         w1 = jnp.pad(w_fc1, ((0, 0), (0, extra)))
         w2 = jnp.pad(w_fc2.T, ((0, 0), (0, extra)))
-        cut = (ff + extra) // 512 * 256 + ((ff + extra) // 256 % 2) * 256
-        unit1 = jnp.stack([w1[:, :cut], w2[:, :cut]])
-        unit2 = jnp.stack([w1[:, cut:], w2[:, cut:]])
+        hidden_units = [jnp.stack([w1[:, a:b], w2[:, a:b]]) for a, b in zip(ends, ends[1:])]
+
+        def straight(unit):
+            return swap(unit, 2, size), swap(unit, 4, size)
+
+        def corner(x, y):
+            return swap(y[0], 2, size), swap(x[1], 4, size)
+
+        x0, y0 = straight(unit0)
         x = to_rows(patches, routes)
-        x0, y0, c0 = swap(unit0, 2, size), swap(unit0, 4, size), swap(unit0, 1, size)
-        da0, db0, cx0, cy0 = swap(y0[0], 2, size), swap(x0[1], 4, size), swap(x0, 1, size), swap(y0, 1, size)
-        unit1 = after(unit1, x0, y0)
-        x1, y1, c1 = swap(unit1, 2, size), swap(unit1, 4, size), swap(unit1, 1, size)
-        p0 = (unit0, c0, x0, cx0, y0, cy0, da0, db0, swap(da0, 1, size), swap(db0, 1, size))
-        cot = to_rows(after(cotangent, x), routes)
-
-        small = jnp.concatenate([ln1_gain, ln1_bias, bias_qv[0], bias_qv[1], b_out, ln2_gain, ln2_bias, b_fc2, b_fc1])
-        small = gather_small(small, size).astype(f32)
-        vec = jnp.moveaxis(small[:, : 8 * part].reshape(size, 8, part), 0, 1).reshape(8, width)
-        b1 = jnp.pad(small[:, 8 * part :].reshape(1, ff), ((0, 0), (0, extra)))
-        vec = jnp.concatenate([vec, jnp.zeros((8, width), f32)], axis=0)
-        kv_bias = jnp.concatenate([jnp.zeros((1, width), f32), vec[3:4]], axis=1)
-        vec = jnp.concatenate([jnp.pad(vec[:8], ((0, 0), (0, width))), jnp.pad(kv_bias, ((0, 7), (0, 0)))], axis=0)
+        unit1, y0a, x0b = lax.optimization_barrier((unit1, y0[0], x0[1]))
+        p0 = (unit0, x0, y0, swap(y0a, 2, size), swap(x0b, 4, size))
+        x1, y1 = straight(unit1)
 
         ids = jnp.stack([picture_ids, jnp.where(valid_mask == 1, picture_ids, -1)])
         far_ids = swap(ids, 1, size)
@@ -1079,108 +1256,135 @@
         qid_row, qid_col = jnp.broadcast_to(near[0][None], (8, tokens)), jnp.broadcast_to(near[0][:, None], (tokens, 128))
         kid_row, kid_col = jnp.broadcast_to(keys[None], (8, 2 * tokens)), jnp.broadcast_to(keys[:, None], (2 * tokens, 128))
 
-        act = ((tokens, width), bf16)
-        flip = ((width, tokens), bf16)
-        vm = pltpu.VMEM
-        dma8 = pltpu.SemaphoreType.DMA((8,))
-        mm = 2 * tokens * width * width
-        n, kv = call(kv_kernel, "kv", [act, ((tokens, 2 * width), bf16)], [vm((width, 2 * width), bf16), dma8],
-                     2 * mm, 4 * width * width, x, vec, pieces=p0)
+        dma = pltpu.SemaphoreType.DMA
+        n, kv, vec, b1, w_kv = order.call(
+            functools.partial(kv_kernel, ff), "kv",
+            [act, ((tokens, 2 * width), bf16), ((16, width), f32), ((16, ff + extra), f32), ((2, width, width), bf16)],
+            [vm((2, width, width), bf16), vm((2, 8, 16, width), bf16), dma((4, 3, 4)), dma],
+            2 * mm, 4 * width * width, x, pieces=p0, meets=True, far_outs=1)
         far_kv = swap(kv, 1, size)
-        q, nt_ = call(q_kernel, "q", [act, flip], [vm((width, width), bf16), vm((width, tokens), bf16), dma8],
-                      mm, 2 * width * width, n, vec, pieces=p0)
+        x1, y1 = order.gate(x1), order.gate(y1)
+        p1 = (unit1, x1, y1, *corner(x1, y1))
+        unit2, unit3, unit4 = hidden_units
+        unit2 = after(unit2, x1, y1)
+        x2, y2 = straight(unit2)
+        cot = to_rows(order.gate(cotangent), routes)
+        q, nt_, w_q, w_o = order.call(
+            q_kernel, "q", [act, flip, ((width, width), bf16), ((width, width), bf16)],
+            [vm((2, width, width), bf16), vm((width, tokens), bf16), dma((2, 3, 4)), dma((2,))],
+            mm, 2 * width * width, n, vec, pieces=p1, meets=True, far_outs=2)
         sc = 2 * tokens * 2 * tokens * WIN * HEADS
-        q, x1, y1 = lax.optimization_barrier((q, x1, y1))
-        da1, db1, cx1, cy1 = swap(y1[0], 2, size), swap(x1[1], 4, size), swap(x1, 1, size), swap(y1, 1, size)
-        unit2 = after(unit2, q, x1, y1)
-        x2, y2, c2 = swap(unit2, 2, size), swap(unit2, 4, size), swap(unit2, 1, size)
-        att, lse = call(
+        att, lse = order.call(
             attention_forward_kernel, "attention_forward", [act, ((HEADS, tokens), f32)],
             [vm((tokens, 2 * tokens), f32), vm((tokens, width), f32), vm((tokens, 128), f32)],
             3 * sc, 8 * tokens * width, q, kv, far_kv, qid_col, kid_row)
-        da1, db1, att = lax.optimization_barrier((da1, db1, att))
-        p1 = (unit1, c1, x1, cx1, y1, cy1, da1, db1, swap(da1, 1, size), swap(db1, 1, size))
-        mid, n2, n2t, cott, attt = call(
-            middle_kernel, "middle", [((tokens, width), f32), act, flip, flip, flip],
-            [vm((width, width), bf16), vm((width, tokens), bf16), dma8], mm, 2 * width * width, att, x, cot, vec, pieces=p0)
-        n2, x2, y2 = lax.optimization_barrier((n2, x2, y2))
-        da2, db2, cx2, cy2 = swap(y2[0], 2, size), swap(x2[1], 4, size), swap(x2, 1, size), swap(y2, 1, size)
-        acc, gn, keep1, send1, gb1a = mlp_call(True, False, n2, cot, n2t, cott, b1[:, :cut], vec, mid, mid, p1)
-        acc, da2, db2 = lax.optimization_barrier((acc, da2, db2))
-        p2 = (unit2, c2, x2, cx2, y2, cy2, da2, db2, swap(da2, 1, size), swap(db2, 1, size))
-        got1 = swap(send1.reshape(2, width // 2, -1), 1, size)
-        out, gn, keep2, send2, gb1b = mlp_call(False, True, n2, cot, n2t, cott, b1[:, cut:], vec, acc, gn, p2)
-        keep1, got1, gn = lax.optimization_barrier((keep1, got1, gn))
-        ax1, by1 = unit_first("first1", keep1, got1, size)
-        got2 = swap(send2, 1, size)
+        x2, y2 = order.gate(x2), order.gate(y2)
+        p2 = (unit2, x2, y2, *corner(x2, y2))
+        unit3 = after(unit3, x2, y2)
+        x3, y3 = straight(unit3)
+        mid, n2, n2t, cott, attt = order.call(
+            middle_kernel, "middle", [act32, act, flip, flip, flip],
+            [vm((width, tokens), bf16)], mm, 2 * width * width, att, x, cot, vec, w_o)
+
+        args = (cot, n2t, cott)
+        acc, gn, *grads1, gb1 = order.mlp("mlp0", True, False, n2, *args, b1, vec, mid, mid, p2, 0, ends[1])
+        x3, y3 = order.gate(x3), order.gate(y3)
+        p3 = (unit3, x3, y3, *corner(x3, y3))
+        unit4 = after(unit4, x3, y3)
+        x4, y4 = straight(unit4)
+        rest_cols = ends[3] - ends[1]
+        acc, gn, *grads2, gb2 = order.mlp("mlp1", False, False, n2, *args, b1, vec, acc, gn, p3, ends[1], rest_cols)
+        x4, y4 = order.gate(x4), order.gate(y4)
+        p4 = (unit4, x4, y4, *corner(x4, y4))
+        r1 = Reduction("1", order, size, *grads1)
+        out, gn, *grads2, gb3 = order.mlp(
+            "mlp2", False, True, n2, *args, b1, vec, acc, gn, p4, ends[2], rest_cols, into=grads2)
         layer_out = from_rows(out, routes)
 
         part_o = (width // 256 + 1) * 128
-        stacked = ((2, width // 2, part_o), bf16)
-        gm, ga, keepo, sendo, sums2, inner = call(
-            branch_kernel, "branch", [((tokens, width), f32), act, stacked, stacked, ((8, width), f32), ((HEADS, tokens), f32)],
-            [vm((width, width), bf16), vm((tokens, width), bf16), dma8], 2 * mm, 4 * width * width,
-            cot, gn, mid, vec, att, attt, pieces=p0)
-        keep2, got2, ga = lax.optimization_barrier((keep2, got2, ga))
-        ax2, by2 = unit_first("first2", keep2, got2, size)
-        goto = swap(sendo, 1, size)
-
-        def attention_backward(near, kv_half, ids_half, dqp):
-            return call(
-                functools.partial(attention_backward_kernel, near), "attention_backward_near" if near else "attention_backward_far",
-                [((tokens, width), bf16 if near else f32), ((tokens, 2 * width), f32 if near else bf16)],
-                [vm((tokens, tokens), f32), vm((tokens, width), f32), vm((tokens, 2 * width), f32)],
-                3 * sc, 16 * tokens * width, q, kv_half, ga, lse, inner, ids_half, qid_row, dqp)
-
-        dqp, dkx = attention_backward(False, far_kv, kid_col[tokens:], gm)
-        dkr = swap(dkx, 1, size)
-        dqp, ax1, by1, goto = lax.optimization_barrier((dqp, ax1, by1, goto))
-        ay1, bx1 = unit_second("second1", keep1, got1, ax1, by1, size)
-        axo, byo = unit_first("firsto", keepo, goto, size)
-        dq, dko = attention_backward(True, kv, kid_col[:tokens], dqp)
-        dq, ax2, by2, ay1, bx1 = lax.optimization_barrier((dq, ax2, by2, ay1, bx1))
-        ay2, bx2 = unit_second("second2", keep2, got2, ax2, by2, size)
-        own1 = unit_third("third1", keep1, got1, ax1, by1, ay1, bx1)
-        in1 = fold_in(own1)
-        part_q = (3 * width // 256 + 1) * 128
-        stacked = ((2, width // 2, part_q), bf16)
-        keepq, sendq, dkv = call(
-            qkv_grad_kernel, "qkv_grad", [stacked, stacked, ((tokens, 2 * width), bf16)], [vm((tokens, 3 * width), bf16)],
-            3 * mm, 8 * width * width, nt_, dq, dko, dkr)
-        gotq = swap(sendq, 1, size)
-        dkv, axo, byo = lax.optimization_barrier((dkv, axo, byo))
-        ayo, bxo = unit_second("secondo", keepo, goto, axo, byo, size)
-        gx, sums1 = call(
-            input_grad_kernel, "input_grad", [act, ((8, width), f32)],
-            [vm((width, width), bf16), vm((width, 2 * width), bf16), vm((tokens, width), f32), pltpu.SemaphoreType.DMA((2, 8))],
-            3 * mm, 6 * width * width, dq, dkv, x, gm, vec, pieces=p0)
-        keepq, gotq, gx = lax.optimization_barrier((keepq, gotq, gx))
-        axq, byq = unit_first("firstq", keepq, gotq, size)
-        grad_patches = from_rows(gx, routes)
-
-        gb1 = jnp.concatenate([gb1a, gb1b], axis=1)[:, :ff].reshape(size, ff // size)
-        vecs = jnp.concatenate([sums1[:4], sums2[:4]]).reshape(8, size, part)
-        small = reduce_small(jnp.concatenate([jnp.moveaxis(vecs, 0, 1).reshape(size, 8 * part), gb1], axis=1), size)
-        mine, grad_b_fc1 = small[: 8 * part].reshape(8, part), small[8 * part :]
-
-        own2 = unit_third("third2", keep2, got2, ax2, by2, ay2, bx2)
-        owno = unit_third("thirdo", keepo, goto, axo, byo, ayo, bxo)
-        in2, ino = fold_in(own2), fold_in(owno)
-        mid1 = pair_sum("inner1", own1, in1)
-        tot1 = pair_sum("total1", mid1, across(mid1))
-        mid2, mido = pair_sum("inner2", own2, in2), pair_sum("innero", owno, ino)
-        tot2, toto = pair_sum("total2", mid2, across(mid2)), pair_sum("totalo", mido, across(mido))
-        ayq, bxq = unit_second("secondq", keepq, gotq, axq, byq, size)
-        ownq = unit_third("thirdq", keepq, gotq, axq, byq, ayq, bxq)
-        midq = pair_sum("innerq", ownq, fold_in(ownq))
-        totq = pair_sum("totalq", midq, across(midq))
-        inside = (z == 1) | (z == 2)
-        g1, g2, go, gq = [jnp.where(inside, t, fold_out(t)).astype(f32) for t in (tot1, tot2, toto, totq)]
-        n1, nk = cut, ff - cut
-        w1g = jnp.concatenate([g1[0], g2[0][:, :nk]], axis=1)
-        w2g = jnp.concatenate([g1[1], g2[1][:, :nk]], axis=1).T
+
+        def gradient(columns):
+            return [((2, part, columns), bf16)] * 4
+
+        def exchanged(columns):
+            return [vm((2, width // 2, columns), bf16)] * 3 + [dma((3, 2))]
+
+        gm, ga, sums2, inner, *gradso = order.call(
+            branch_kernel, "branch", [act32, act, ((8, width), f32), ((HEADS, tokens), f32), *gradient(part_o)],
+            [vm((tokens, width), bf16), *exchanged(part_o)], 2 * mm, 4 * width * width,
+            cot, gn, mid, vec, att, attt, w_o, meets=True)
+        cut_head = (HEADS + 2) // 2
+        cut_col = cut_head * HD // 128 * 128
+
+        def attention_backward(name, h0, h1, base, done, span, carry):
+            share = 3 * sc * (h1 - h0) // HEADS * 2
+            return order.call(
+                functools.partial(attention_backward_kernel, h0, h1, base, done), name,
+                [((tokens, done), bf16), ((tokens, 2 * done), f32), ((tokens, 2 * done), bf16),
+                 ((5, tokens if span > done else 8, 128), f32)],
+                [vm((2 * tokens, tokens), f32), vm((5, tokens, span), f32)],
+                share, 16 * tokens * width, q, kv, far_kv, ga, lse, inner, kid_col, qid_row, carry)
+
+        def qkv_grad(name, dq, dkn, dkr):
+            columns = 3 * dq.shape[1]
+            share = (columns + 511) // 512 * 256
+            got, *grads = order.call(
+                qkv_grad_kernel, name, [((tokens, columns), bf16), *gradient(share)], exchanged(share),
+                mm * columns // width, 4 * width * columns, nt_, dq, dkn, dkr, meets=True)
+            return got, grads
+
+        dqa, dna, dfa, carry = attention_backward("attention_backward_a", 0, cut_head, 0, cut_col, cut_col + 128, inner)
+        dra = swap(dfa, 1, size)
+        r1.second()
+        r2 = Reduction("2", order, size, *grads2)
+        gra, gradsa = qkv_grad("qkv_grad_a", dqa, dna, dra)
+        dqb, dnb, dfb, _ = attention_backward(
+            "attention_backward_b", cut_head, HEADS, cut_col, width - cut_col, width - cut_col, carry)
+        drb = swap(dfb, 1, size)
+        r1.third()
+        r2.second()
+        ro = Reduction("o", order, size, *gradso)
+        qa = Reduction("qa", order, size, *gradsa)
+        grb, gradsb = qkv_grad("qkv_grad_b", dqb, dnb, drb)
+        qb = Reduction("qb", order, size, *gradsb)
+        gnq, sums0 = order.call(
+            normed_grad_kernel, "normed_grad", [act32, ((8, width), f32)],
+            [vm((3, width, width), bf16), dma((2,))], 3 * mm, 6 * width * width, gra, grb, pieces=(w_q, w_kv))
+        r1.fourth()
+        r2.third()
+        gx, sums1 = order.call(input_grad_kernel, "input_grad", [act, ((8, width), f32)], [], 10**7, 12 * tokens * width,
+                               gnq, x, gm, vec)
+        gx_rows = (gx, routes)
+        ro.second()
+        qa.second()
+        r1.fifth()
+        r2.fourth()
+        qb.second()
+        ro.third()
+        qa.third()
+        grad_patches = from_rows(*gx_rows)
+        bias_grads = jnp.concatenate([gb1, gb2, gb3], axis=1)[:, :ff].reshape(size, ff // size)
+        vecs = jnp.concatenate([sums1[:2], sums0[:2], sums2[:4]]).reshape(8, size, part)
+        tiny = reduce_small(jnp.concatenate([jnp.moveaxis(vecs, 0, 1).reshape(size, 8 * part), bias_grads], axis=1), size)
+        mine, grad_b_fc1 = tiny[: 8 * part].reshape(8, part), tiny[8 * part :]
+        r2.fifth()
+        qb.third()
+        ro.fourth()
+        qa.fourth()
+        ro.fifth()
+        qa.fifth()
+        qb.fourth()
+        qb.fifth()
+        g1, g2, go, ga_, gb_ = [r.result() for r in (r1, r2, ro, qa, qb)]
+        left = ff - ends[1]
+        w1g = jnp.concatenate([g1[0], g2[0][:, :left]], axis=1)
+        w2g = jnp.concatenate([g1[1], g2[1][:, :left]], axis=1).T
         wog = jnp.concatenate([go[0], go[1][:, 2 * part_o - width :]], axis=1)
-        wqg = jnp.concatenate([gq[0], gq[1][:, 2 * part_q - 3 * width :]], axis=1)
+
+        def joined(g, columns):
+            return jnp.concatenate([g[0], g[1][:, 2 * g.shape[2] - columns :]], axis=1).reshape(part, 3, columns // 3)
+
+        wqg = jnp.concatenate([joined(ga_, 3 * cut_col), joined(gb_, 3 * (width - cut_col))], axis=2).reshape(part, 3 * width)
         return (layer_out, grad_patches, mine[0], mine[1], wqg, mine[2:4], wog, mine[6], mine[4], mine[5], w1g, grad_b_fc1, w2g, mine[7])
 
     return step

time: 644 us -> 668 us (1.037)
  waiting for transfers between devices: 205 us -> 117 us
  starting transfers between devices: 96.9 us -> 146 us
  Pallas kernels: 273 us -> 319 us
  local copies, waits for them, and re-layouts: 31.7 us -> 41.1 us
    ppermute x12 -> x15, waiting for transfers between devices: 109 us -> 57.8 us  [the longest x5 37.9 us: fifth(): self.outer = lax.ppermute(self.total, 'seq', [(1, 0), (2, 3)])]
    ppermute x12 -> x15, starting transfers between devices: 19 us -> 53.3 us  [the longest x5 41.7 us: third(): self.inner = lax.ppermute(self.own, 'seq', [(0, 1), (3, 2)])]
    ppermute x56 -> x47, waiting for transfers between devices: 90.2 us -> 58.9 us  [swap(): return lax.ppermute(v, 'dp', [(i, i ^ mask) for i in range(size)])]
    pallas_call x2 -> x3, Pallas kernels: 60.4 us -> 91.5 us  [mlp_call(): pl.pallas_call(functools.partial(mlp_kernel, first, last, into is not Non...]
    pallas_call x9 -> x11, Pallas kernels: 150 us -> 176 us  [call(): pl.pallas_call(body, out_shape=tuple((sds(s, t) for s, t in outs)), in_sp...]
    pallas_call x20, Pallas kernels: 62.4 us -> 51.9 us  [add_blocks(): pl.pallas_call(functools.partial(sums_kernel, [[len(terms) for terms in o...]
    ppermute x56 -> x47, starting transfers between devices: 38.6 us -> 48.7 us  [swap(): return lax.ppermute(v, 'dp', [(i, i ^ mask) for i in range(size)])]
    unnamed x113 -> x136, local copies, waits for them, and re-layouts: 9.28 us -> 14.8 us
  transfers between devices with their start and end apart: 78 -> 72, of which waited for: 24 -> 19; matrix products, arithmetic and copies ran while one was open for 8% -> 8% of each run, Pallas kernels for 42% -> 39%
where the time goes in v2:
time: 668 us; the launch traced here: 660 us
  Pallas kernels  319 us (48%)
  starting transfers between devices  146 us (22%)
  waiting for transfers between devices  117 us (18%)
  local copies, waits for them, and re-layouts  41.1 us (6%)
  other arithmetic  34.3 us (5%)
    pallas_call x11, Pallas kernels, call(): pl.pallas_call(body, out_shape=tuple((sds(s, t) for s, t in outs)), in_sp...  176 us
    pallas_call x3, Pallas kernels, mlp_call(): pl.pallas_call(functools.partial(mlp_kernel, first, last, into is not Non...  91.5 us
    ppermute x47, waiting for transfers between devices, swap(): return lax.ppermute(v, 'dp', [(i, i ^ mask) for i in range(size)])  58.9 us
    pallas_call x20, Pallas kernels, add_blocks(): pl.pallas_call(functools.partial(sums_kernel, [[len(terms) for terms in o...  51.9 us
    ppermute x47, starting transfers between devices, swap(): return lax.ppermute(v, 'dp', [(i, i ^ mask) for i in range(size)])  48.7 us
    ppermute x5, starting transfers between devices, third(): self.inner = lax.ppermute(self.own, 'seq', [(0, 1), (3, 2)])  41.7 us
    ppermute x5, waiting for transfers between devices, fifth(): self.outer = lax.ppermute(self.total, 'seq', [(1, 0), (2, 3)])  37.9 us
    ppermute x5, waiting for transfers between devices, third(): self.inner = lax.ppermute(self.own, 'seq', [(0, 1), (3, 2)])  19.9 us
  transfers between devices with their start and end apart: 72, of which 19 were waited for; matrix products, arithmetic and copies ran while one was open for 8% of the time, Pallas kernels for 39%

profile of v2, /device:TPU:0, one launch (start us, length us, event | category | flops | bytes accessed | tf_op | source)
XLA Modules:
  0.0 659.8 jit_solution(7927658825104680211)
XLA Ops:
  11.7 5.9 collective-permute-start.1
  36.2 23.0 %kv.1 = (bf16[512,1152]{1,0:T(8,128)(2,1)}, bf16[512,2304]{1,0:T(8,128)(2,1)}, f32[16,1152]{1,0:T(8,128)}, f32[16,4352]{1,0:T(8,128)}, bf16[2,1152,1152]{2,1,0:T(8,128)(2,1)}) custom-call(bf16[512,1152]{1,0:T(8,128)(2,1)} %pad_maximum_fusion.2.x_ref, bf16[2,160,1152]{2,1,0:T(8,128)(2,1)} %pad_maximum_fusion.10.rest_0_, ...), custom_call_target="tpu_custom_call" | custom-call | flops 2717908992 | bytes 5308416 | tf_op jit(solution)/shard_map/kv/pallas_call | solution.py:1046
  65.9 6.1 collective-permute-start.13
  73.7 11.1 %q.1 = (bf16[512,1152]{1,0:T(8,128)(2,1)}, bf16[1152,512]{1,0:T(8,128)(2,1)}, bf16[1152,1152]{1,0:T(8,128)(2,1)}, bf16[1152,1152]{1,0:T(8,128)(2,1)}) custom-call(bf16[512,1152]{1,0:T(8,128)(2,1)} %get-tuple-element.146.n_ref, f32[16,1152]{1,0:T(8,128)} %get-tuple-element.147.vec_ref, bf16[2,144,1152]{2,1,0:T(8,128)(2,1)} %pad_maximum_fusion.11.rest_0_, ...), custom_call_target="tpu_custom_call" | custom-call | flops 1358954496 | bytes 2654208 | tf_op jit(solution)/shard_map/q/pallas_call | solution.py:1046
  86.3 25.6 %attention_forward.1 = (bf16[512,1152]{1,0:T(8,128)(2,1)}, f32[16,512]{1,0:T(8,128)}) custom-call(bf16[512,1152]{1,0:T(8,128)(2,1)} %get-tuple-element.205.q_ref, bf16[512,2304]{1,0:T(8,128)(2,1)} %get-tuple-element.153.ko_ref.kn_ref, bf16[512,2304]{1,0:T(8,128)(2,1)} %collective-permute-done.10.kx_ref.kf_ref, s32[512,128]{1,0:T(8,128)} %broadcast_in_dim.34.qid_ref, ...), custom_call_target="tpu_custom_call" | custom-call | flops 12884901888 | bytes 4718592 | tf_op jit(solution)/shard_map/attention_forward/pallas_call | solution.py:1046
  122.4 12.7 %middle.1 = (f32[512,1152]{1,0:T(8,128)}, bf16[512,1152]{1,0:T(8,128)(2,1)}, bf16[1152,512]{1,0:T(8,128)(2,1)}, bf16[1152,512]{1,0:T(8,128)(2,1)}, bf16[1152,512]{1,0:T(8,128)(2,1)}) custom-call(bf16[512,1152]{1,0:T(8,128)(2,1)} %get-tuple-element.155.att_ref, bf16[512,1152]{1,0:T(8,128)(2,1)} %pad_maximum_fusion.2.x_ref, ...), custom_call_target="tpu_custom_call" | custom-call | flops 1358954496 | bytes 2654208 | tf_op jit(solution)/shard_map/middle/pallas_call | solution.py:1046
  135.1 39.4 %mlp0.1 = (f32[512,1152]{1,0:T(8,128)}, f32[512,1152]{1,0:T(8,128)}, bf16[2,144,2048]{2,1,0:T(8,128)(2,1)}, bf16[2,144,2048]{2,1,0:T(8,128)(2,1)}, bf16[2,144,20...) custom-call(bf16[512,1152]{1,0:T(8,128)(2,1)} %get-tuple-element.175.n2_ref, ...), custom_call_target="tpu_custom_call" | custom-call | flops 14495514624 | bytes 25952256 | tf_op jit(solution)/shard_map/mlp0/pallas_call | solution.py:871
  180.9 7.7 %collective-permute-done.20.rest_3_ = bf16[144,1536]{1,0:T(8,128)(2,1)S(1)} collective-permute-done((bf16[144,1536]{1,0:T(8,128)(2,1)S(1)}, bf16[144,1536]{1,0:T(8,128)(2,1)S(1)}, u32[]{:S(2)}, u32[]{:S(2)}) %collective-permute-start.20) | collective-permute-done | bytes 442400 | tf_op jit(solution)/shard_map/ppermute | solution.py:1059
  191.7 32.1 %mlp1.1 = (f32[512,1152]{1,0:T(8,128)}, f32[512,1152]{1,0:T(8,128)}, bf16[2,144,2304]{2,1,0:T(8,128)(2,1)}, bf16[2,144,2304]{2,1,0:T(8,128)(2,1)}, bf16[2,144,23...) custom-call(bf16[512,1152]{1,0:T(8,128)(2,1)} %get-tuple-element.175.n2_ref, ...), custom_call_target="tpu_custom_call" | custom-call | flops 10871635968 | bytes 21233664 | tf_op jit(solution)/shard_map/mlp1/pallas_call | solution.py:871
  226.3 5.2 collective-permute-done.24.rest_3_
  232.8 20.1 %mlp2.1 = (bf16[512,1152]{1,0:T(8,128)(2,1)}, f32[512,1152]{1,0:T(8,128)}, bf16[2,144,2304]{2,1,0:T(8,128)(2,1)}, bf16[2,144,2304]{2,1,0:T(8,128)(2,1)}, bf16[2,...) custom-call(bf16[512,1152]{1,0:T(8,128)(2,1)} %get-tuple-element.175, ...), custom_call_target="tpu_custom_call", output_to_operand_aliasing={{2}: (13, {}), {3}: (14, {}), {4}: (15, {}), {5}: (16, {})} | custom-call | flops 5435817984 | bytes 14155776 | tf_op jit(solution)/shard_map/mlp2/pallas_call | solution.py:871
  252.9 19.4 %branch.1 = (f32[512,1152]{1,0:T(8,128)}, bf16[512,1152]{1,0:T(8,128)(2,1)}, f32[8,1152]{1,0:T(8,128)}, f32[16,512]{1,0:T(8,128)}, bf16[2,144,640]{2,1,0:T(8,128...) custom-call(bf16[512,1152]{1,0:T(8,128)(2,1)} %pad_maximum_fusion.3.cot_ref, ...), custom_call_target="tpu_custom_call" | custom-call | flops 2717908992 | bytes 5308416 | tf_op jit(solution)/shard_map/branch/pallas_call | solution.py:1046
  273.9 23.6 %attention_backward_a.1 = (bf16[512,640]{1,0:T(8,128)(2,1)}, f32[512,1280]{1,0:T(8,128)}, bf16[512,1280]{1,0:T(8,128)(2,1)}, f32[5,512,128]{2,1,0:T(8,128)}) custom-call(bf16[512,1152]{1,0:T(8,128)(2,1)} %get-tuple-element.205.q_ref, bf16[512,2304]{1,0:T(8,128)(2,1)} %get-tuple-element.153.ko_ref.kn_ref, ...), custom_call_target="tpu_custom_call" | custom-call | flops 14495514624 | bytes 9437184 | tf_op jit(solution)/shard_map/attention_backward_a/pallas_call | solution.py:1046
  301.8 25.1 %collective-permute-done.28.refs_1_ = bf16[2,144,2048]{2,1,0:T(8,128)(2,1)} collective-permute-done((bf16[2,144,2048]{2,1,0:T(8,128)(2,1)}, bf16[2,144,2048]{2,1,0:T(8,128)(2,1)}, u32[]{:S(2)}, u32[]{:S(2)}) %collective-permute-start.28) | collective-permute-done | bytes 1179680 | tf_op jit(solution)/shard_map/ppermute | solution.py:1059
  332.9 12.0 %qkv_grad_a.1 = (bf16[512,1920]{1,0:T(8,128)(2,1)}, bf16[2,144,1024]{2,1,0:T(8,128)(2,1)}, bf16[2,144,1024]{2,1,0:T(8,128)(2,1)}, bf16[2,144,1024]{2,1,0:T(8,128)(2,1)}, bf16[2,144,1024]{2,1,0:T(8,128)(2,1)}) custom-call(bf16[1152,512]{1,0:T(8,128)(2,1)} %get-tuple-element.215.nt_ref, bf16[512,640]{1,0:T(8,128)(2,1)} %get-tuple-element.195.dq_ref, ...), custom_call_target="tpu_custom_call" | custom-call | flops 2264924160 | bytes 8847360 | tf_op jit(solution)/shard_map/qkv_grad_a/pallas_call | solution.py:1046
  344.9 19.4 %attention_backward_b.1 = (bf16[512,512]{1,0:T(8,128)(2,1)}, f32[512,1024]{1,0:T(8,128)}, bf16[512,1024]{1,0:T(8,128)(2,1)}, f32[5,8,128]{2,1,0:T(8,128)}) custom-call(bf16[512,1152]{1,0:T(8,128)(2,1)} %get-tuple-element.205.q_ref, bf16[512,2304]{1,0:T(8,128)(2,1)} %get-tuple-element.153.ko_ref.kn_ref, ...), custom_call_target="tpu_custom_call" | custom-call | flops 11274289152 | bytes 9437184 | tf_op jit(solution)/shard_map/attention_backward_b/pallas_call | solution.py:1046
  371.9 4.8 collective-permute-start.36
  388.7 9.9 %qkv_grad_b.1 = (bf16[512,1536]{1,0:T(8,128)(2,1)}, bf16[2,144,768]{2,1,0:T(8,128)(2,1)}, bf16[2,144,768]{2,1,0:T(8,128)(2,1)}, bf16[2,144,768]{2,1,0:T(8,128)(2,1)}, bf16[2,144,768]{2,1,0:T(8,128)(2,1)}) custom-call(bf16[1152,512]{1,0:T(8,128)(2,1)} %get-tuple-element.215.nt_ref, bf16[512,512]{1,0:T(8,128)(2,1)} %get-tuple-element.207.dq_ref, ...), custom_call_target="tpu_custom_call" | custom-call | flops 1811939328 | bytes 7077888 | tf_op jit(solution)/shard_map/qkv_grad_b/pallas_call | solution.py:1046
  398.7 12.6 %normed_grad.1 = (f32[512,1152]{1,0:T(8,128)}, f32[8,1152]{1,0:T(8,128)}) custom-call(bf16[512,1920]{1,0:T(8,128)(2,1)} %get-tuple-element.219.g1_ref, bf16[512,1536]{1,0:T(8,128)(2,1)} %get-tuple-element.218.g2_ref, bf16[1152,1152]{1,0:T(8,128)(2,1)} %get-tuple-element.220.wq_ref, bf16[2,1152,1152]{2,1,0:T(8,128)(2,1)} %get-tuple-element.221.wkv_ref), custom_call_target="tpu_custom_call" | custom-call | flops 4076863488 | bytes 7962624 | tf_op jit(solution)/shard_map/normed_grad/pallas_call | solution.py:1046
  417.6 4.2 third2.1.refs_0_.refs_2_
  421.8 6.4 input_grad.1
  432.6 6.0 collective-permute-start.27
  442.3 5.2 collective-permute-start.51
  458.2 17.8 %collective-permute-done.51.refs_1_.refs_3_ = bf16[2,144,2304]{2,1,0:T(8,128)(2,1)} collective-permute-done((bf16[2,144,2304]{2,1,0:T(8,128)(2,1)S(1)}, bf16[2,144,2304]{2,1,0:T(8,128)(2,1)}, u32[]{:S(2)}, u32[]{:S(2)}) %collective-permute-start.51) | collective-permute-done | bytes 1327136 | tf_op jit(solution)/shard_map/ppermute | solution.py:1191
  476.0 3.8 inner2.1.refs_0_.refs_2_
  486.4 4.5 collective-permute-done.52.refs_1_
  492.5 18.4 %collective-permute-start.44 = (bf16[1,1690]{1,0:T(2,128)(2,1)S(1)}, bf16[1,1690]{1,0:T(2,128)(2,1)S(1)}, u32[]{:S(2)}, u32[]{:S(2)}) collective-permute-start(bf16[1,1690]{1,0:T(2,128)(2,1)S(1)} %fusion.16), channel_id=1, source_target_pairs={{0,1},{1,0},{2,3},{3,2},{4,5},{5,4},{6,7},{7,6},{8,9},{9,8},{10,11... | collective-permute-start | bytes 10148 | tf_op jit(solution)/shard_map/ppermute | solution.py:1111
  521.0 6.4 collective-permute-start.62
  535.8 3.8 total2.1
  539.7 5.9 collective-permute-start.40
  558.1 21.7 %collective-permute-start.66 = (bf16[2,144,768]{2,1,0:T(8,128)(2,1)S(1)}, bf16[2,144,768]{2,1,0:T(8,128)(2,1)S(1)}, u32[]{:S(2)}, u32[]{:S(2)}) collective-permute-start(bf16[2,144,768]{2,1,0:T(8,128)(2,1)S(1)} %copy-done.11), channel_id=1, source_target_pairs={{0,1},{3,2},{4,5},{7,6},{8,9},{11,10},{12,13},{15,14},{16,17},{19,... | collective-permute-start | bytes 1327112 | tf_op jit(solution)/shard_map/ppermute | solution.py:1191
  606.7 37.8 %collective-permute-done.65 = bf16[2,144,1024]{2,1,0:T(8,128)(2,1)} collective-permute-done((bf16[2,144,1024]{2,1,0:T(8,128)(2,1)S(1)}, bf16[2,144,1024]{2,1,0:T(8,128)(2,1)}, u32[]{:S(2)}, u32[]{:S(2)}) %collective-permute-start.65) | collective-permute-done | bytes 589856 | tf_op jit(solution)/shard_map/ppermute | solution.py:1202
  (380 shorter events, 199.9 us)
Async XLA Ops:
  65.9 52.7 %collective-permute-start.12 = (bf16[256,1152]{1,0:T(8,128)(2,1)}, bf16[256,1152]{1,0:T(8,128)(2,1)}, u32[]{:S(2)}, u32[]{:S(2)}) collective-permute-start(bf16[256,1152]{1,0:T(8,128)(2,1)} %get-tuple-element.288), channel_id=1, source_target_pairs={{0,1},{1,0},{2,5},{3,4},{4,3},{5,2},{6,7},{7,6},{8,9},{9,8},{10,13... | collective-permute-start | bytes 1769480 | tf_op jit(solution)/shard_map/ppermute | solution.py:1133
  65.9 52.7 %collective-permute-start.13 = (bf16[256,1152]{1,0:T(8,128)(2,1)}, bf16[256,1152]{1,0:T(8,128)(2,1)}, u32[]{:S(2)}, u32[]{:S(2)}) collective-permute-start(bf16[256,1152]{1,0:T(8,128)(2,1)} %get-tuple-element.289), channel_id=1, source_target_pairs={{0,0},{1,1},{2,4},{3,5},{4,2},{5,3},{6,6},{7,7},{8,8},{9,9},{10,12... | collective-permute-start | bytes 1769480 | tf_op jit(solution)/shard_map/ppermute | solution.py:1132
  72.1 39.9 %collective-permute-start.15 = (bf16[2,144,2048]{2,1,0:T(8,128)(2,1)}, bf16[2,144,2048]{2,1,0:T(8,128)(2,1)}, u32[]{:S(2)}, u32[]{:S(2)}) collective-permute-start(bf16[2,144,2048]{2,1,0:T(8,128)(2,1)} %pad_maximum_fusion.4.rest_0_), channel_id=1, source_target_pairs={{0,16},{4,20},{8,24},{12,28},{16,0},{20,4},{24,8},{28,12},{1,17},{... | collective-permute-start | bytes 3538952 | tf_op jit(solution)/shard_map/ppermute | solution.py:1059
  72.9 40.9 %collective-permute-start.14 = (bf16[2,144,2048]{2,1,0:T(8,128)(2,1)}, bf16[2,144,2048]{2,1,0:T(8,128)(2,1)}, u32[]{:S(2)}, u32[]{:S(2)}) collective-permute-start(bf16[2,144,2048]{2,1,0:T(8,128)(2,1)} %pad_maximum_fusion.4.rest_0_), channel_id=1, source_target_pairs={{0,8},{4,12},{8,0},{12,4},{16,24},{20,28},{24,16},{28,20},{1,9},{5... | collective-permute-start | bytes 3538952 | tf_op jit(solution)/shard_map/ppermute | solution.py:1059
  121.0 53.4 %collective-permute-start.19 = (bf16[2,144,1536]{2,1,0:T(8,128)(2,1)S(1)}, bf16[2,144,1536]{2,1,0:T(8,128)(2,1)}, u32[]{:S(2)}, u32[]{:S(2)}) collective-permute-start(bf16[2,144,1536]{2,1,0:T(8,128)(2,1)S(1)} %pad_maximum_fusion.8.rest_0_), channel_id=1, source_target_pairs={{0,16},{4,20},{8,24},{12,28},{16,0},{20,4},{24,8},{28,12},{1,17},{... | collective-permute-start | bytes 2654216 | tf_op jit(solution)/shard_map/ppermute | solution.py:1059
  121.6 52.9 %collective-permute-start.18 = (bf16[2,144,1536]{2,1,0:T(8,128)(2,1)S(1)}, bf16[2,144,1536]{2,1,0:T(8,128)(2,1)}, u32[]{:S(2)}, u32[]{:S(2)}) collective-permute-start(bf16[2,144,1536]{2,1,0:T(8,128)(2,1)S(1)} %pad_maximum_fusion.8.rest_0_), channel_id=1, source_target_pairs={{0,8},{4,12},{8,0},{12,4},{16,24},{20,28},{24,16},{28,20},{1,9},{5... | collective-permute-start | bytes 2654216 | tf_op jit(solution)/shard_map/ppermute | solution.py:1059
  179.5 44.3 %collective-permute-start.23 = (bf16[2,144,768]{2,1,0:T(8,128)(2,1)S(1)}, bf16[2,144,768]{2,1,0:T(8,128)(2,1)S(1)}, u32[]{:S(2)}, u32[]{:S(2)}) collective-permute-start(bf16[2,144,768]{2,1,0:T(8,128)(2,1)S(1)} %pad_maximum_fusion.13.rest_0_), channel_id=1, source_target_pairs={{0,16},{4,20},{8,24},{12,28},{16,0},{20,4},{24,8},{28,12},{1,17},{... | collective-permute-start | bytes 1327112 | tf_op jit(solution)/shard_map/ppermute | solution.py:1059
  180.1 44.6 %collective-permute-start.22 = (bf16[2,144,768]{2,1,0:T(8,128)(2,1)S(1)}, bf16[2,144,768]{2,1,0:T(8,128)(2,1)S(1)}, u32[]{:S(2)}, u32[]{:S(2)}) collective-permute-start(bf16[2,144,768]{2,1,0:T(8,128)(2,1)S(1)} %pad_maximum_fusion.13.rest_0_), channel_id=1, source_target_pairs={{0,8},{4,12},{8,0},{12,4},{16,24},{20,28},{24,16},{28,20},{1,9},{5... | collective-permute-start | bytes 1327112 | tf_op jit(solution)/shard_map/ppermute | solution.py:1059
  297.5 35.3 %collective-permute-start.30 = (bf16[512,1280]{1,0:T(8,128)(2,1)}, bf16[512,1280]{1,0:T(8,128)(2,1)}, u32[]{:S(2)}, u32[]{:S(2)}) collective-permute-start(bf16[512,1280]{1,0:T(8,128)(2,1)} %get-tuple-element.203), channel_id=1, source_target_pairs={{0,4},{4,0},{8,12},{12,8},{16,20},{20,16},{24,28},{28,24},{1,5},{5... | collective-permute-start | bytes 3932168 | tf_op jit(solution)/shard_map/ppermute | solution.py:1059
  300.5 77.0 %collective-permute-start.33 = (bf16[2,144,2304]{2,1,0:T(8,128)(2,1)}, bf16[2,144,2304]{2,1,0:T(8,128)(2,1)S(1)}, u32[]{:S(2)}, u32[]{:S(2)}) collective-permute-start(bf16[2,144,2304]{2,1,0:T(8,128)(2,1)} %get-tuple-element.211), channel_id=1, source_target_pairs={{0,8},{4,12},{8,0},{12,4},{16,24},{20,28},{24,16},{28,20},{1,9},{5... | collective-permute-start | bytes 3981320 | tf_op jit(solution)/shard_map/ppermute | solution.py:1059
  301.2 76.3 %collective-permute-start.34 = (bf16[2,144,2304]{2,1,0:T(8,128)(2,1)}, bf16[2,144,2304]{2,1,0:T(8,128)(2,1)S(1)}, u32[]{:S(2)}, u32[]{:S(2)}) collective-permute-start(bf16[2,144,2304]{2,1,0:T(8,128)(2,1)} %get-tuple-element.213), channel_id=1, source_target_pairs={{0,16},{4,20},{8,24},{12,28},{16,0},{20,4},{24,8},{28,12},{1,17},{... | collective-permute-start | bytes 3981320 | tf_op jit(solution)/shard_map/ppermute | solution.py:1059
  330.6 37.5 %collective-permute-start.31 = (bf16[1,144,2048]{2,1,0:T(8,128)(2,1)}, bf16[1,144,2048]{2,1,0:T(8,128)(2,1)S(1)}, u32[]{:S(2)}, u32[]{:S(2)}) collective-permute-start(bf16[1,144,2048]{2,1,0:T(8,128)(2,1)} %get-tuple-element.200), channel_id=1, source_target_pairs={{0,16},{4,20},{8,24},{12,28},{16,0},{20,4},{24,8},{28,12},{1,17},{... | collective-permute-start | bytes 1769480 | tf_op jit(solution)/shard_map/ppermute | solution.py:1059
  332.1 36.0 %collective-permute-start.32 = (bf16[1,144,2048]{2,1,0:T(8,128)(2,1)}, bf16[1,144,2048]{2,1,0:T(8,128)(2,1)}, u32[]{:S(2)}, u32[]{:S(2)}) collective-permute-start(bf16[1,144,2048]{2,1,0:T(8,128)(2,1)} %get-tuple-element.209), channel_id=1, source_target_pairs={{0,8},{4,12},{8,0},{12,4},{16,24},{20,28},{24,16},{28,20},{1,9},{5... | collective-permute-start | bytes 1769480 | tf_op jit(solution)/shard_map/ppermute | solution.py:1059
  371.9 40.1 %collective-permute-start.36 = (bf16[2,144,2048]{2,1,0:T(8,128)(2,1)}, bf16[2,144,2048]{2,1,0:T(8,128)(2,1)}, u32[]{:S(2)}, u32[]{:S(2)}) collective-permute-start(bf16[2,144,2048]{2,1,0:T(8,128)(2,1)} %third1.1.refs_0_.refs_2_), channel_id=1, source_target_pairs={{0,1},{3,2},{4,5},{7,6},{8,9},{11,10},{12,13},{15,14},{16,17},{19,... | collective-permute-start | bytes 3538952 | tf_op jit(solution)/shard_map/ppermute | solution.py:1191
  376.8 55.7 %collective-permute-start.46 = (bf16[2,144,640]{2,1,0:T(8,128)(2,1)}, bf16[2,144,640]{2,1,0:T(8,128)(2,1)S(1)}, u32[]{:S(2)}, u32[]{:S(2)}) collective-permute-start(bf16[2,144,640]{2,1,0:T(8,128)(2,1)} %get-tuple-element.238), channel_id=1, source_target_pairs={{0,8},{4,12},{8,0},{12,4},{16,24},{20,28},{24,16},{28,20},{1,9},{5... | collective-permute-start | bytes 1105928 | tf_op jit(solution)/shard_map/ppermute | solution.py:1059
  382.7 32.6 %collective-permute-start.37 = (bf16[1,144,2304]{2,1,0:T(8,128)(2,1)}, bf16[1,144,2304]{2,1,0:T(8,128)(2,1)S(1)}, u32[]{:S(2)}, u32[]{:S(2)}) collective-permute-start(bf16[1,144,2304]{2,1,0:T(8,128)(2,1)} %get-tuple-element.214), channel_id=1, source_target_pairs={{0,16},{4,20},{8,24},{12,28},{16,0},{20,4},{24,8},{28,12},{1,17},{... | collective-permute-start | bytes 1990664 | tf_op jit(solution)/shard_map/ppermute | solution.py:1059
  384.1 32.6 %collective-permute-start.38 = (bf16[1,144,2304]{2,1,0:T(8,128)(2,1)}, bf16[1,144,2304]{2,1,0:T(8,128)(2,1)S(1)}, u32[]{:S(2)}, u32[]{:S(2)}) collective-permute-start(bf16[1,144,2304]{2,1,0:T(8,128)(2,1)} %get-tuple-element.225), channel_id=1, source_target_pairs={{0,8},{4,12},{8,0},{12,4},{16,24},{20,28},{24,16},{28,20},{1,9},{5... | collective-permute-start | bytes 1990664 | tf_op jit(solution)/shard_map/ppermute | solution.py:1059
  388.1 44.5 %collective-permute-start.47 = (bf16[2,144,640]{2,1,0:T(8,128)(2,1)}, bf16[2,144,640]{2,1,0:T(8,128)(2,1)}, u32[]{:S(2)}, u32[]{:S(2)}) collective-permute-start(bf16[2,144,640]{2,1,0:T(8,128)(2,1)} %get-tuple-element.240), channel_id=1, source_target_pairs={{0,16},{4,20},{8,24},{12,28},{16,0},{20,4},{24,8},{28,12},{1,17},{... | collective-permute-start | bytes 1105928 | tf_op jit(solution)/shard_map/ppermute | solution.py:1059
  432.5 48.4 %collective-permute-start.26 = (bf16[256,1152]{1,0:T(8,128)(2,1)}, bf16[256,1152]{1,0:T(8,128)(2,1)}, u32[]{:S(2)}, u32[]{:S(2)}) collective-permute-start(bf16[256,1152]{1,0:T(8,128)(2,1)} %get-tuple-element.284), channel_id=1, source_target_pairs={{1,0},{0,1},{5,2},{4,3},{3,4},{2,5},{7,6},{6,7},{9,8},{8,9},{13,10... | collective-permute-start | bytes 1769480 | tf_op jit(solution)/shard_map/ppermute | solution.py:1143
  432.6 48.3 %collective-permute-start.27 = (bf16[256,1152]{1,0:T(8,128)(2,1)}, bf16[256,1152]{1,0:T(8,128)(2,1)}, u32[]{:S(2)}, u32[]{:S(2)}) collective-permute-start(bf16[256,1152]{1,0:T(8,128)(2,1)} %get-tuple-element.285), channel_id=1, source_target_pairs={{0,0},{1,1},{4,2},{5,3},{2,4},{3,5},{6,6},{7,7},{8,8},{9,9},{12,10... | collective-permute-start | bytes 1769480 | tf_op jit(solution)/shard_map/ppermute | solution.py:1142
  442.3 33.7 %collective-permute-start.51 = (bf16[2,144,2304]{2,1,0:T(8,128)(2,1)S(1)}, bf16[2,144,2304]{2,1,0:T(8,128)(2,1)}, u32[]{:S(2)}, u32[]{:S(2)}) collective-permute-start(bf16[2,144,2304]{2,1,0:T(8,128)(2,1)S(1)} %copy-done), channel_id=1, source_target_pairs={{0,1},{3,2},{4,5},{7,6},{8,9},{11,10},{12,13},{15,14},{16,17},{19,... | collective-permute-start | bytes 3981320 | tf_op jit(solution)/shard_map/ppermute | solution.py:1191
  453.5 32.3 %collective-permute-start.54 = (bf16[1,144,640]{2,1,0:T(8,128)(2,1)}, bf16[1,144,640]{2,1,0:T(8,128)(2,1)S(1)}, u32[]{:S(2)}, u32[]{:S(2)}) collective-permute-start(bf16[1,144,640]{2,1,0:T(8,128)(2,1)} %get-tuple-element.241), channel_id=1, source_target_pairs={{0,16},{4,20},{8,24},{12,28},{16,0},{20,4},{24,8},{28,12},{1,17},{... | collective-permute-start | bytes 552968 | tf_op jit(solution)/shard_map/ppermute | solution.py:1059
  479.7 52.6 %collective-permute-start.58 = (bf16[2,144,2304]{2,1,0:T(8,128)(2,1)}, bf16[2,144,2304]{2,1,0:T(8,128)(2,1)S(1)}, u32[]{:S(2)}, u32[]{:S(2)}) collective-permute-start(bf16[2,144,2304]{2,1,0:T(8,128)(2,1)} %inner2.1.refs_0_.refs_2_), channel_id=1, source_target_pairs={{1,2},{2,1},{5,6},{6,5},{9,10},{10,9},{13,14},{14,13},{17,18},{18,... | collective-permute-start | bytes 3981320 | tf_op jit(solution)/shard_map/ppermute | solution.py:1198
  484.5 32.6 %collective-permute-start.56 = (bf16[1,144,1024]{2,1,0:T(8,128)(2,1)}, bf16[1,144,1024]{2,1,0:T(8,128)(2,1)S(1)}, u32[]{:S(2)}, u32[]{:S(2)}) collective-permute-start(bf16[1,144,1024]{2,1,0:T(8,128)(2,1)} %get-tuple-element.246), channel_id=1, source_target_pairs={{0,16},{4,20},{8,24},{12,28},{16,0},{20,4},{24,8},{28,12},{1,17},{... | collective-permute-start | bytes 884744 | tf_op jit(solution)/shard_map/ppermute | solution.py:1059
  492.5 34.9 %collective-permute-start.44 = (bf16[1,1690]{1,0:T(2,128)(2,1)S(1)}, bf16[1,1690]{1,0:T(2,128)(2,1)S(1)}, u32[]{:S(2)}, u32[]{:S(2)}) collective-permute-start(bf16[1,1690]{1,0:T(2,128)(2,1)S(1)} %fusion.16), channel_id=1, source_target_pairs={{0,1},{1,0},{2,3},{3,2},{4,5},{5,4},{6,7},{7,6},{8,9},{9,8},{10,11... | collective-permute-start | bytes 10148 | tf_op jit(solution)/shard_map/ppermute | solution.py:1111
  521.0 32.0 %collective-permute-start.62 = (bf16[2,144,1024]{2,1,0:T(8,128)(2,1)}, bf16[2,144,1024]{2,1,0:T(8,128)(2,1)S(1)}, u32[]{:S(2)}, u32[]{:S(2)}) collective-permute-start(bf16[2,144,1024]{2,1,0:T(8,128)(2,1)} %thirdqa.1.refs_0_.refs_2_), channel_id=1, source_target_pairs={{0,1},{3,2},{4,5},{7,6},{8,9},{11,10},{12,13},{15,14},{16,17},{19,... | collective-permute-start | bytes 1769480 | tf_op jit(solution)/shard_map/ppermute | solution.py:1191
  539.6 51.9 %collective-permute-start.39 = (bf16[256,1152]{1,0:T(8,128)(2,1)}, bf16[256,1152]{1,0:T(8,128)(2,1)}, u32[]{:S(2)}, u32[]{:S(2)}) collective-permute-start(bf16[256,1152]{1,0:T(8,128)(2,1)} %get-tuple-element.280), channel_id=1, source_target_pairs={{1,0},{0,1},{5,2},{4,3},{3,4},{2,5},{7,6},{6,7},{9,8},{8,9},{13,10... | collective-permute-start | bytes 1769480 | tf_op jit(solution)/shard_map/ppermute | solution.py:1143
  539.7 51.8 %collective-permute-start.40 = (bf16[256,1152]{1,0:T(8,128)(2,1)}, bf16[256,1152]{1,0:T(8,128)(2,1)}, u32[]{:S(2)}, u32[]{:S(2)}) collective-permute-start(bf16[256,1152]{1,0:T(8,128)(2,1)} %get-tuple-element.281), channel_id=1, source_target_pairs={{0,0},{1,1},{4,2},{5,3},{2,4},{3,5},{6,6},{7,7},{8,8},{9,9},{12,10... | collective-permute-start | bytes 1769480 | tf_op jit(solution)/shard_map/ppermute | solution.py:1142
  556.7 44.9 %collective-permute-start.70 = (bf16[2,144,2048]{2,1,0:T(8,128)(2,1)S(1)}, bf16[2,144,2048]{2,1,0:T(8,128)(2,1)}, u32[]{:S(2)}, u32[]{:S(2)}) collective-permute-start(bf16[2,144,2048]{2,1,0:T(8,128)(2,1)S(1)} %copy-done.6), channel_id=1, source_target_pairs={{1,0},{2,3},{5,4},{6,7},{9,8},{10,11},{13,12},{14,15},{17,16},{18,... | collective-permute-start | bytes 3538952 | tf_op jit(solution)/shard_map/ppermute | solution.py:1202
  594.7 53.8 %collective-permute-start.71 = (bf16[2,144,2304]{2,1,0:T(8,128)(2,1)S(1)}, bf16[2,144,2304]{2,1,0:T(8,128)(2,1)}, u32[]{:S(2)}, u32[]{:S(2)}) collective-permute-start(bf16[2,144,2304]{2,1,0:T(8,128)(2,1)S(1)} %copy-done.3), channel_id=1, source_target_pairs={{1,0},{2,3},{5,4},{6,7},{9,8},{10,11},{13,12},{14,15},{17,16},{18,... | collective-permute-start | bytes 3981320 | tf_op jit(solution)/shard_map/ppermute | solution.py:1202
  596.0 48.6 %collective-permute-start.65 = (bf16[2,144,1024]{2,1,0:T(8,128)(2,1)S(1)}, bf16[2,144,1024]{2,1,0:T(8,128)(2,1)}, u32[]{:S(2)}, u32[]{:S(2)}) collective-permute-start(bf16[2,144,1024]{2,1,0:T(8,128)(2,1)S(1)} %copy-done.14), channel_id=1, source_target_pairs={{1,0},{2,3},{5,4},{6,7},{9,8},{10,11},{13,12},{14,15},{17,16},{18,... | collective-permute-start | bytes 1769480 | tf_op jit(solution)/shard_map/ppermute | solution.py:1202
  600.2 54.4 %collective-permute-start.68 = (bf16[2,144,768]{2,1,0:T(8,128)(2,1)}, bf16[2,144,768]{2,1,0:T(8,128)(2,1)S(1)}, u32[]{:S(2)}, u32[]{:S(2)}) collective-permute-start(bf16[2,144,768]{2,1,0:T(8,128)(2,1)} %totalqb.1), channel_id=1, source_target_pairs={{1,0},{2,3},{5,4},{6,7},{9,8},{10,11},{13,12},{14,15},{17,16},{18,... | collective-permute-start | bytes 1327112 | tf_op jit(solution)/shard_map/ppermute | solution.py:1202
  (106 other events, 1209.9 us)

commit v3 on v2

--- a/solution.py
+++ b/solution.py
@@ -458,6 +458,7 @@
 ROWBLK = 64
 LOG2E = 1.4426950408889634
 ORDER = (0, 2, 4, 6, 1, 3, 5, 7)
+ORDER_SMALL = (0, 4, 2, 6, 1, 5, 3, 7)
 bf16 = jnp.bfloat16
 f32 = jnp.float32
 
@@ -498,19 +499,339 @@
     return d
 
 
-def sibling():
-    return flipped_index(lax.axis_index("dp"), 1), lax.axis_index("seq")
-
-
-def meet_sibling():
+def here():
+    return lax.axis_index("dp"), lax.axis_index("seq")
+
+
+def across_links(mask):
+    d, z = here()
+    return flipped_index(d, mask), z
+
+
+def row_partner(s):
+    d, z = here()
+    core, odd = lax.rem(d, 2), lax.rem(z, 2)
+    return d - core + lax.div(z, 2), 2 * core + odd + s - 2 * s * odd
+
+
+def row_stays():
+    d, z = here()
+    return lax.rem(d, 2) == lax.div(z, 2)
+
+
+def greet(relations):
+    if not relations:
+        return
     barrier = pltpu.get_barrier_semaphore()
-    pl.semaphore_signal(barrier, inc=1, device_id=sibling(), device_id_type=MESH)
-    pl.semaphore_wait(barrier, 1)
+    d, z = here()
+
+    def signal(device):
+        pl.semaphore_signal(barrier, inc=1, device_id=device, device_id_type=MESH)
+
+    count = 0
+    for mask in (1, 2, 4):
+        if mask in relations:
+            signal(across_links(mask))
+            count += 1
+    conditions = []
+    if "z" in relations:
+        conditions += [(z > 0, (d, z - 1)), (z < 3, (d, z + 1))]
+        count = count + lax.div(z + 2, 3) + lax.div(5 - z, 3)
+    if "rows" in relations:
+        signal(row_partner(1))
+        count += 1
+        conditions.append((jnp.logical_not(row_stays()), row_partner(0)))
+        away = lax.rem(d, 2) - lax.div(z, 2)
+        count = count + away * away
+    for condition, device in conditions:
+        pl.when(condition)(functools.partial(signal, device))
+    pl.semaphore_wait(barrier, count)
+
+
+def remote(src, dst, sem, device):
+    return pltpu.make_async_remote_copy(
+        src_ref=src, dst_ref=dst, send_sem=sem.at[0], recv_sem=sem.at[1], device_id=device, device_id_type=MESH
+    )
+
+
+def start_all(copies):
+    for c in copies:
+        c.start()
+
+
+def wait_all(copies):
+    for c in copies:
+        c.wait()
+
+
+class Hop:
+    relations = ()
+    ins, outs, scratch = (), (), ()
+
+    def start(self, ins, outs, scratch):
+        pass
+
+    def halfway(self, ins, outs, scratch):
+        pass
+
+    def finish(self, ins, outs, scratch):
+        pass
+
+
+class Straight(Hop):
+    relations = (2, 4)
+
+    def __init__(self, unit):
+        self.ins = (unit,)
+        self.outs = ((unit.shape, bf16),) * 2
+        self.scratch = (pltpu.SemaphoreType.DMA((2, 2)),)
+
+    def copies(self, ins, outs, scratch):
+        return [remote(ins[0], outs[i], scratch[0].at[i], across_links(mask)) for i, mask in ((0, 2), (1, 4))]
+
+    def start(self, *refs):
+        start_all(self.copies(*refs))
+
+    def finish(self, *refs):
+        wait_all(self.copies(*refs))
+
+
+class Corner(Straight):
+    def __init__(self, x, y):
+        super().__init__(x)
+        self.ins = (x, y)
+        self.outs = ((x.shape[1:], bf16),) * 2
+
+    def copies(self, ins, outs, scratch):
+        x, y = ins
+        return [
+            remote(y.at[0], outs[0], scratch[0].at[0], across_links(2)),
+            remote(x.at[1], outs[1], scratch[0].at[1], across_links(4)),
+        ]
+
+
+class Chain(Straight):
+    def __init__(self, unit, following):
+        self.ins = (unit, following)
+        self.outs = ((unit.shape, bf16),) * 2 + ((unit.shape[1:], bf16),) * 2 + ((following.shape, bf16),) * 2
+        self.scratch = (pltpu.SemaphoreType.DMA((6, 2)),)
+
+    def stages(self, ins, outs, scratch):
+        sem = scratch[0]
+        x, y, da, db, x2, y2 = outs
+        on_x, on_y = across_links(2), across_links(4)
+        first = [remote(ins[0], x, sem.at[0], on_x), remote(ins[0], y, sem.at[1], on_y)]
+        second = [remote(y.at[0], da, sem.at[2], on_x), remote(x.at[1], db, sem.at[3], on_y),
+                  remote(ins[1], x2, sem.at[4], on_x), remote(ins[1], y2, sem.at[5], on_y)]
+        return first, second
+
+    def start(self, *refs):
+        start_all(self.stages(*refs)[0])
+
+    def halfway(self, *refs):
+        first, second = self.stages(*refs)
+        wait_all(first)
+        start_all(second)
+
+    def finish(self, *refs):
+        wait_all(self.stages(*refs)[1])
+
+
+class Rows(Hop):
+    relations = ("rows",)
+
+    def __init__(self, v):
+        self.ins = (v,)
+        self.outs = ((v.shape, v.dtype),)
+        self.scratch = (pltpu.SemaphoreType.DMA((2, 2)), pltpu.SemaphoreType.DMA)
+
+    def each(self, ins, outs, scratch, act):
+        odd = lax.rem(lax.axis_index("seq"), 2)
+        stays = row_stays()
+
+        @pl.when(stays)
+        def _():
+            act(pltpu.make_async_copy(ins[0].at[odd], outs[0].at[odd], scratch[1]))
+
+        @pl.when(jnp.logical_not(stays))
+        def _():
+            act(remote(ins[0].at[odd], outs[0].at[odd], scratch[0].at[0], row_partner(0)))
+
+        act(remote(ins[0].at[1 - odd], outs[0].at[odd], scratch[0].at[1], row_partner(1)))
+
+    def start(self, *refs):
+        self.each(*refs, lambda c: c.start())
+
+    def finish(self, *refs):
+        self.each(*refs, lambda c: c.wait())
+
+
+def add_into(total, other):
+    @pl.loop(0, total.shape[-1] // 128)
+    def _(t):
+        cols = pl.ds(pl.multiple_of(t * 128, 128), 128)
+        total[..., cols] = (total[..., cols].astype(f32) + other[..., cols].astype(f32)).astype(bf16)
+
+
+class First(Hop):
+    relations = (2, 4)
+
+    def __init__(self, keep_a, send_a, keep_b, send_b):
+        self.ins = (keep_a, send_a, keep_b, send_b)
+        shape = (2, *keep_a.shape)
+        self.outs = ((shape, bf16),)
+        self.scratch = (pltpu.VMEM(shape, bf16), pltpu.VMEM(shape, bf16), pltpu.SemaphoreType.DMA((2, 2)),
+                        pltpu.SemaphoreType.DMA((3,)))
+
+    def copies(self, ins, outs, scratch):
+        kept, got, sem, own = scratch
+        return [
+            remote(ins[1], got.at[0], sem.at[0], across_links(2)),
+            remote(ins[3], got.at[1], sem.at[1], across_links(4)),
+            pltpu.make_async_copy(ins[0], kept.at[0], own.at[0]),
+            pltpu.make_async_copy(ins[2], kept.at[1], own.at[1]),
+        ]
+
+    def start(self, *refs):
+        start_all(self.copies(*refs))
+
+    def finish(self, ins, outs, scratch):
+        wait_all(self.copies(ins, outs, scratch))
+        for i in range(2):
+            add_into(scratch[0].at[i], scratch[1].at[i])
+        done = pltpu.make_async_copy(scratch[0], outs[0], scratch[3].at[2])
+        done.start()
+        done.wait()
+
+
+class Second(Hop):
+    relations = (2, 4)
+
+    def __init__(self, sums):
+        self.ins = (sums,)
+        shape = (2, *sums.shape[2:])
+        self.outs = ((shape, bf16),)
+        self.scratch = (pltpu.VMEM(shape, bf16), pltpu.VMEM(shape, bf16), pltpu.SemaphoreType.DMA((2, 2)),
+                        pltpu.SemaphoreType.DMA((3,)))
+
+    def copies(self, ins, outs, scratch):
+        kept, got, sem, own = scratch
+        return [
+            remote(ins[0].at[0, 1], got.at[0], sem.at[0], across_links(4)),
+            remote(ins[0].at[1, 1], got.at[1], sem.at[1], across_links(2)),
+            pltpu.make_async_copy(ins[0].at[0, 0], kept.at[0], own.at[0]),
+            pltpu.make_async_copy(ins[0].at[1, 0], kept.at[1], own.at[1]),
+        ]
+
+    def start(self, *refs):
+        start_all(self.copies(*refs))
+
+    def finish(self, ins, outs, scratch):
+        wait_all(self.copies(ins, outs, scratch))
+        add_into(scratch[0], scratch[1])
+        done = pltpu.make_async_copy(scratch[0], outs[0], scratch[3].at[2])
+        done.start()
+        done.wait()
+
+
+INWARD, MIDDLE, OUTWARD = range(3)
+
+
+def seq_step(stage):
+    d, z = here()
+    inner = (z == 1) | (z == 2)
+    outer = jnp.logical_not(inner)
+    side = z + 1 - 2 * lax.rem(z, 2)
+    if stage == INWARD:
+        return outer, inner, (d, side)
+    if stage == MIDDLE:
+        return inner, inner, (d, 3 - z)
+    return inner, outer, (d, side)
+
+
+class Seq(Hop):
+    relations = ("z",)
+
+    def __init__(self, stage, v, half=None):
+        self.stage, self.half = stage, half
+        self.ins = (v,)
+        shape = v.shape if half is None else v.shape[1:]
+        self.outs = ((shape, bf16),)
+        self.scratch = (pltpu.VMEM(shape, bf16), pltpu.VMEM(shape, bf16), pltpu.SemaphoreType.DMA((2,)),
+                        pltpu.SemaphoreType.DMA((2,)))
+
+    def source(self, ins):
+        return ins[0] if self.half is None else ins[0].at[self.half]
+
+    def start(self, ins, outs, scratch):
+        kept, got, sem, own = scratch
+        sends, _, partner = seq_step(self.stage)
+        src = self.source(ins)
+        pltpu.make_async_copy(src, kept, own.at[0]).start()
+
+        @pl.when(sends)
+        def _():
+            remote(src, got, sem, partner).start()
+
+    def finish(self, ins, outs, scratch):
+        kept, got, sem, own = scratch
+        sends, receives, partner = seq_step(self.stage)
+        src = self.source(ins)
+        pltpu.make_async_copy(src, kept, own.at[0]).wait()
+
+        @pl.when(sends)
+        def _():
+            remote(src, got, sem, partner).wait_send()
+
+        def store(ref):
+            done = pltpu.make_async_copy(ref, outs[0], own.at[1])
+            done.start()
+            done.wait()
+
+        @pl.when(receives)
+        def _():
+            remote(src, got, sem, partner).wait_recv()
+            if self.stage != OUTWARD:
+                add_into(kept, got)
+            store(kept if self.stage != OUTWARD else got)
+
+        @pl.when(jnp.logical_not(receives))
+        def _():
+            store(kept)
+
+
+def hop_parts(hops):
+    relations = set()
+    for h in hops:
+        relations |= set(h.relations)
+    return (
+        [a for h in hops for a in h.ins],
+        [sds(s, t) for h in hops for s, t in h.outs],
+        [s for h in hops for s in h.scratch],
+        relations,
+    )
+
+
+def hop_refs(hops, ins, outs, scratch):
+    ins, outs, scratch = list(ins), list(outs), list(scratch)
+    parts = []
+    for h in hops:
+        parts.append(tuple([refs.pop(0) for _ in range(n)] for refs, n in (
+            (ins, len(h.ins)), (outs, len(h.outs)), (scratch, len(h.scratch)))))
+    return parts
+
+
+def hop_results(hops, results):
+    results, parts = list(results), []
+    for h in hops:
+        got = tuple(results.pop(0) for _ in h.outs)
+        parts.append(got if len(got) > 1 else got[0])
+    return parts
 
 
 def to_sibling(src, dst, sem, i):
     return pltpu.make_async_remote_copy(
-        src_ref=src, dst_ref=dst, send_sem=sem.at[1, i], recv_sem=sem.at[2, i], device_id=sibling(), device_id_type=MESH
+        src_ref=src, dst_ref=dst, send_sem=sem.at[1, i], recv_sem=sem.at[2, i], device_id=across_links(1), device_id_type=MESH
     )
 
 
@@ -530,16 +851,6 @@
     return lambda j: ref.at[pl.ds(pl.multiple_of(j * count, count), count), :]
 
 
-def start_all(copies):
-    for c in copies:
-        c.start()
-
-
-def wait_all(copies):
-    for c in copies:
-        c.wait()
-
-
 def norm_rows(v, gain, offset):
     center = v - jnp.mean(v, axis=-1, keepdims=True)
     spread = jnp.mean(center * center, axis=-1, keepdims=True)
@@ -561,56 +872,16 @@
         dst[i * part : (i + 1) * part, :] = flipped[where, :]
 
 
-def spread(buf, out_ref, part, span):
+def spread(piece, out_ref, part, span):
     inside = (part + 127) // 128 * 128
 
     @pl.loop(0, 8)
     def _(j):
-        at = pl.multiple_of(jnp.minimum(j * part // 128, (out_ref.shape[1] - span) // 128) * 128, 128)
+        at = pl.multiple_of(lax.div(j * ((out_ref.shape[1] - span) // 128), 7) * 128, 128)
         r = lax.broadcasted_iota(jnp.int32, (inside, span), 0)
         c = lax.broadcasted_iota(jnp.int32, (inside, span), 1)
         place = jnp.where((c == r + (j * part - at)) & (r < part), 1.0, 0.0).astype(bf16)
-        out_ref[0:16, pl.ds(at, span)] += nn(buf[j][:, 0:inside], place)
-
-
-def kv_kernel(ff, x_ref, *rest):
-    pieces, (n_ref, kv_ref, vec_ref, b1_ref, wkv_ref, w, buf, sem, out_sem) = rest[:5], rest[5:]
-    width = x_ref.shape[1]
-    part = width // 8
-    every = pl.ds(0, width)
-    meet_sibling()
-    vectors, weights = [], []
-    for half in range(2):
-        vectors += unit_copies(pieces, half, pl.ds(part, 16), every, lambda j, half=half: buf.at[half, j], sem.at[2 + half])
-    for half in range(2):
-        weights += unit_copies(pieces, half, pl.ds(0, part), every, shard_rows(w.at[half], part), sem.at[half])
-    start_all(vectors + weights)
-    vec_ref[...] = jnp.zeros(vec_ref.shape, f32)
-    b1_ref[...] = jnp.zeros(b1_ref.shape, f32)
-    wait_all(vectors)
-    spread(buf.at[0], vec_ref, part, 512)
-
-    def body(rows):
-        v = x_ref[rows, :].astype(f32)
-        n_ref[rows, :] = norm_rows(v, vec_ref[0:1, :], vec_ref[1:2, :]).astype(bf16)
-
-    row_loop(x_ref.shape[0], body)
-    wait_all(weights)
-    store = pltpu.make_async_copy(w, wkv_ref, out_sem)
-    store.start()
-
-    def keys(cols):
-        kv_ref[:, cols] = nn(n_ref[...], w[0, :, cols]).astype(bf16)
-
-    column_tiles(width, keys)
-
-    def values(cols):
-        total = nn(n_ref[...], w[1, :, cols]) + vec_ref[3:4, cols]
-        kv_ref[:, pl.ds(pl.multiple_of(cols.start + width, 128), cols.size)] = total.astype(bf16)
-
-    column_tiles(width, values)
-    spread(buf.at[1], b1_ref, ff // 8, 768)
-    store.wait()
+        out_ref[0:16, pl.ds(at, span)] += nn(piece(j)[:, 0:inside], place)
 
 
 def column_tiles(width, body):
@@ -624,30 +895,123 @@
         body(pl.ds(full * 256, width % 256))
 
 
-def q_kernel(n_ref, vec_ref, *rest):
-    pieces, (q_ref, nt_ref, wq_ref, wo_ref, w, flipped, sem, out_sem) = rest[:5], rest[5:]
-    width = n_ref.shape[1]
-    part = width // 8
-    meet_sibling()
-    halves = [
-        unit_copies(pieces, half, pl.ds(0, part), pl.ds(0, width), shard_rows(w.at[half], part), sem.at[half]) for half in range(2)
-    ]
-    start_all(halves[0] + halves[1])
-    transpose_ordered(n_ref, flipped, nt_ref)
-    wait_all(halves[0])
-
-    def body(cols):
-        q_ref[:, cols] = (nn(n_ref[...], w[0, :, cols]) + vec_ref[2:3, cols]).astype(bf16)
-
-    column_tiles(width, body)
-    wait_all(halves[1])
-    stores = [pltpu.make_async_copy(w.at[i], out, out_sem.at[i]) for i, out in ((0, wq_ref), (1, wo_ref))]
-    start_all(stores)
-    wait_all(stores)
+class Gather:
+    def __init__(self, unit, place, sem, local, halves=2):
+        self.unit, self.place, self.sem, self.local, self.halves = unit, place, sem, local, halves
+        self.d = lax.axis_index("dp")
+
+    def own(self, kind, mask):
+        return [remote(self.unit.at[h], self.place(h, self.d), self.sem.at[kind, h], across_links(mask)) for h in range(self.halves)]
+
+    def forward(self, kind, h, shard_mask, mask):
+        ref = self.place(h, flipped_index(self.d, shard_mask))
+        return remote(ref, ref, self.sem.at[kind, h], across_links(mask))
+
+    def here(self):
+        return [pltpu.make_async_copy(self.unit.at[h], self.place(h, self.d), self.local.at[h]) for h in range(self.halves)]
+
+    def both(self, kind, shard_mask):
+        return [self.forward(kind, h, shard_mask, 1) for h in range(self.halves)]
+
+    def corners(self):
+        if self.halves == 1:
+            return [self.forward(3, 0, 2, 4)]
+        return [self.forward(3, 0, 4, 2), self.forward(3, 1, 2, 4)]
+
+    def begin(self):
+        start_all(self.own(0, 2) + self.own(1, 4) + self.own(2, 1) + self.here())
+
+    def turn(self):
+        for c in self.own(0, 2) + self.own(1, 4):
+            c.wait_recv()
+        start_all(self.corners() + self.both(4, 2) + self.both(5, 4))
+
+    def last(self):
+        for c in self.corners():
+            c.wait_recv()
+        start_all(self.both(6, 6))
+
+    def arrived(self):
+        for c in self.own(2, 1) + self.both(4, 2) + self.both(5, 4) + self.both(6, 6):
+            c.wait_recv()
+        wait_all(self.here())
+
+    def sent(self):
+        for c in (self.own(0, 2) + self.own(1, 4) + self.own(2, 1) + self.corners() + self.both(4, 2) + self.both(5, 4)
+                  + self.both(6, 6)):
+            c.wait_send()
+
+
+def entry_kernel(ff, unit0, small, unit1, patches, x_ref, nt_ref, q_ref, kv_ref, vec_ref, b1_ref, far_ref, w_ref,
+                 w, buf, xbuf, n, flipped, sem, small_sem, local, rows_sem, rows_local, far_sem, out_sem):
+    width = unit0.shape[2]
+    part, tokens = width // 8, n.shape[0]
+
+    def matrix_rows(first):
+        return lambda h, j: w.at[first + h, pl.ds(pl.multiple_of(j * part, part), part), :]
+
+    vectors = Gather(small, lambda h, j: buf.at[j], small_sem, local.at[2], halves=1)
+    keys, queries = Gather(unit0, matrix_rows(0), sem.at[0], local.at[0]), Gather(unit1, matrix_rows(2), sem.at[1], local.at[1])
+    rows = Rows(x_ref)
+    row_refs = ([patches], [xbuf], [rows_sem, rows_local])
+    far = [remote(kv_ref.at[:, pl.ds(i * width, width)], far_ref.at[:, pl.ds(i * width, width)], far_sem.at[i], across_links(1))
+           for i in range(2)]
+    vectors.begin()
+    keys.begin()
+    rows.start(*row_refs)
+    vec_ref[...] = jnp.zeros(vec_ref.shape, f32)
+    b1_ref[...] = jnp.zeros(b1_ref.shape, f32)
+    vectors.turn()
+    keys.turn()
+    vectors.last()
+    queries.begin()
+    vectors.arrived()
+    spread(lambda j: buf[j, 0], vec_ref, part, 512)
+    rows.finish(*row_refs)
+    half = tokens // 2
+    for i in range(2):
+
+        @pl.loop(0, half // ROWBLK)
+        def _(r):
+            at = pl.ds(pl.multiple_of(r * ROWBLK, ROWBLK), ROWBLK)
+            to = pl.ds(pl.multiple_of(r * ROWBLK + i * half, ROWBLK), ROWBLK)
+            v = xbuf[i, at, :]
+            x_ref[to, :] = v
+            n[to, :] = norm_rows(v.astype(f32), vec_ref[0:1, :], vec_ref[1:2, :]).astype(bf16)
+
+    keys.last()
+    keys.arrived()
+
+    def project(i, bias, out, offset):
+        def body(cols):
+            total = nn(n[...], w[i, :, cols])
+            if bias is not None:
+                total = total + vec_ref[bias : bias + 1, cols]
+            out[:, pl.ds(pl.multiple_of(cols.start + offset, 128), cols.size)] = total.astype(bf16)
+
+        column_tiles(width, body)
+
+    project(0, None, kv_ref, 0)
+    far[0].start()
+    queries.turn()
+    project(1, 3, kv_ref, width)
+    far[1].start()
+    stores = [pltpu.make_async_copy(w.at[pl.ds(2 * i, 2)], w_ref.at[pl.ds(2 * i, 2)], out_sem.at[i]) for i in range(2)]
+    stores[0].start()
+    transpose_ordered(n, flipped, nt_ref)
+    spread(lambda j: buf[j, 1], b1_ref, ff // 8, 768)
+    queries.last()
+    queries.arrived()
+    stores[1].start()
+    project(2, 2, q_ref, 0)
+    for g in (vectors, keys, queries):
+        g.sent()
+    wait_all(far + stores)
 
 
 def head_window(h, width):
-    w0 = pl.multiple_of(jnp.minimum((h * HD) // 128, (width - WIN) // 128) * 128, 128)
+    tile = lax.div(h * HD, 128)
+    w0 = pl.multiple_of((tile - lax.div(tile, (width - WIN) // 128 + 1)) * 128, 128)
     lane = lax.broadcasted_iota(jnp.int32, (1, WIN), 1)
     off = h * HD - w0
     return w0, (lane >= off) & (lane < off + HD)
@@ -697,7 +1061,7 @@
 
 def attention_backward_kernel(
     h0, h1, base, done, q_ref, kn_ref, kf_ref, go_ref, lse_ref, del_ref, kid_ref, qid_ref, cin_ref,
-    dq_ref, dkn_ref, dkf_ref, cout_ref, bias, acc
+    dq_ref, dkn_ref, cout_ref, dkr_ref, bias, acc, dkf_ref, far_sem
 ):
     tokens, width = q_ref.shape
     span = acc.shape[2]
@@ -755,11 +1119,18 @@
             if span > done:
                 cout_ref[i, rows, :] = acc[i, rows, done : done + 128]
 
-
-def middle_kernel(att_ref, x_ref, cot_ref, vec_ref, w, mid_ref, n2_ref, n2t_ref, cott_ref, attt_ref, flipped):
+    far = remote(dkf_ref, dkr_ref, far_sem, across_links(1))
+    far.start()
+    far.wait()
+
+
+def middle_kernel(att_ref, x_ref, cot_ref, vec_ref, w_ref, mid_ref, n2_ref, n2t_ref, cott_ref, attt_ref, flipped, w, sem):
     tokens, width = x_ref.shape
+    load = pltpu.make_async_copy(w_ref.at[3], w, sem)
+    load.start()
     transpose_ordered(cot_ref, flipped, cott_ref)
     transpose_ordered(att_ref, flipped, attt_ref)
+    load.wait()
 
     def body(cols):
         mid_ref[:, cols] = nn(att_ref[...], w[:, cols]) + vec_ref[4:5, cols] + x_ref[:, cols].astype(f32)
@@ -781,10 +1152,12 @@
         send[i, :, cols] = total[sent[i] * part : (sent[i] + 1) * part]
 
 
-def mlp_kernel(first, last, aliased, n2_ref, cot_ref, n2t_ref, cott_ref, b1_ref, vec_ref, outp_ref, gnp_ref, *rest):
-    pieces = rest[:5]
-    out_ref, gn_ref, ka_ref, sa_ref, kb_ref, sb_ref, gb1_ref, wbuf, acc, gacc, mine, theirs, came, sem, gsem, credit = (
-        rest[9 if aliased else 5 :])
+def mlp_kernel(first, last, hops, n2_ref, cot_ref, n2t_ref, cott_ref, b1_ref, vec_ref, outp_ref, gnp_ref, *rest):
+    counts = [sum(len(part) for part in parts) for parts in zip(*((h.ins, h.outs, h.scratch) for h in hops))] or [0, 0, 0]
+    pieces, hop_ins, rest = rest[:5], rest[5 : 5 + counts[0]], rest[5 + counts[0] :]
+    (out_ref, gn_ref, ka_ref, sa_ref, kb_ref, sb_ref, gb1_ref), hop_outs, rest = rest[:7], rest[7 : 7 + counts[1]], rest[7 + counts[1] :]
+    (wbuf, acc, gacc, mine, theirs, came, sem, gsem, credit), hop_scratch = rest[:9], rest[9:]
+    carried = list(zip(hops, hop_refs(hops, hop_ins, hop_outs, hop_scratch)))
     t, steps = pl.program_id(0), pl.num_programs(0) - 1
     width = n2_ref.shape[1]
     tile, part = wbuf.shape[-1], width // 8
@@ -804,7 +1177,9 @@
 
     @pl.when(t == 0)
     def _():
-        meet_sibling()
+        greet(hop_parts(hops)[3] | {1})
+        for h, refs in carried:
+            h.start(*refs)
         start_all(copies(0, 0))
 
         def init(rows):
@@ -850,29 +1225,35 @@
 
     @pl.when(t < steps - 1)
     def _():
-        pl.semaphore_signal(credit, inc=1, device_id=sibling(), device_id_type=MESH)
+        pl.semaphore_signal(credit, inc=1, device_id=across_links(1), device_id_type=MESH)
 
     @pl.when(t == steps)
     def _():
         out_ref[...] = acc[...].astype(out_ref.dtype)
         gn_ref[...] = gacc[...]
-
-
-def mlp_call(name, first, last, n2, cot, n2t, cott, b1, vec, outp, gnp, pieces, begin, total, into=None, collective=0):
+        for h, refs in carried:
+            h.finish(*refs)
+
+    @pl.when(t == steps * 5 // 8)
+    def _():
+        for h, refs in carried:
+            h.halfway(*refs)
+
+
+def mlp_call(name, first, last, n2, cot, n2t, cott, b1, vec, outp, gnp, pieces, begin, collective=0, hops=()):
     tokens, width = n2.shape
     cols, tile = pieces[0].shape[2], 256
     steps = cols // tile
     const = lambda a: pl.BlockSpec(a.shape, lambda t: (0,) * a.ndim, pipeline_mode=pl.Buffered(1))
-    skip = 0 if into is None else (total - cols) // tile
-    grads = pl.BlockSpec((2, width // 8, tile), lambda t: (0, 0, jnp.maximum(t - 1, 0) + skip))
+    grads = pl.BlockSpec((2, width // 8, tile), lambda t: (0, 0, jnp.maximum(t - 1, 0)))
     hidden = lambda t: jnp.minimum(t, steps - 1)
-    args = (n2, cot, n2t, cott, b1, vec, outp, gnp, *pieces)
-    grad = sds((2, width // 8, total), bf16)
-    return pl.pallas_call(
-        functools.partial(mlp_kernel, first, last, into is not None),
+    hop_ins, hop_outs, hop_scratch, _ = hop_parts(hops)
+    grad = sds((2, width // 8, cols), bf16)
+    got = pl.pallas_call(
+        functools.partial(mlp_kernel, first, last, hops),
         grid=(steps + 1,),
         in_specs=[const(n2), const(cot), const(n2t), const(cott), pl.BlockSpec((8, tile), lambda t: (0, hidden(t) + begin // tile)),
-                  const(vec), const(outp), const(gnp)] + [ANY] * (5 if into is None else 9),
+                  const(vec), const(outp), const(gnp)] + [ANY] * (5 + len(hop_ins)),
         out_specs=(
             pl.BlockSpec((tokens, width), lambda t: (0, 0)),
             pl.BlockSpec((tokens, width), lambda t: (0, 0)),
@@ -881,6 +1262,7 @@
             grads,
             grads,
             pl.BlockSpec((1, tile), lambda t: (0, hidden(t))),
+            *[ANY] * len(hop_outs),
         ),
         out_shape=(
             sds((tokens, width), bf16 if last else f32),
@@ -890,8 +1272,8 @@
             grad,
             grad,
             sds((1, cols), f32),
+            *hop_outs,
         ),
-        input_output_aliases={} if into is None else {len(args) + i: 2 + i for i in range(4)},
         scratch_shapes=[
             pltpu.VMEM((2, 2, width, tile), bf16),
             pltpu.VMEM((tokens, width), f32),
@@ -902,13 +1284,15 @@
             pltpu.SemaphoreType.DMA((2, 2, 3, 4)),
             pltpu.SemaphoreType.DMA((2, 3, 2)),
             pltpu.SemaphoreType.REGULAR,
+            *hop_scratch,
         ],
         compiler_params=pltpu.CompilerParams(collective_id=collective, has_side_effects=True),
         cost_estimate=pl.CostEstimate(
             flops=12 * tokens * width * cols, bytes_accessed=8 * width * cols + 12 * tokens * width, transcendentals=tokens * cols
         ),
         name=name,
-    )(*args, *(() if into is None else into))
+    )(n2, cot, n2t, cott, b1, vec, outp, gnp, *pieces, *hop_ins)
+    return got[:7], hop_results(hops, got[7:])
 
 
 def norm_back(v, g, gain):
@@ -920,10 +1304,11 @@
     return grad, g * n
 
 
-def branch_kernel(cot_ref, gn_ref, mid_ref, vec_ref, att_ref, attt_ref, w, gm_ref, ga_ref, sums_ref, del_ref,
-                  ka_ref, sa_ref, kb_ref, sb_ref, gb, mine, theirs, came, sem):
+def branch_kernel(cot_ref, gn_ref, mid_ref, vec_ref, att_ref, attt_ref, w_ref, gm_ref, ga_ref, sums_ref, del_ref,
+                  ka_ref, sa_ref, kb_ref, sb_ref, gb, mine, theirs, came, sem, w, load_sem):
     tokens, width = cot_ref.shape
-    meet_sibling()
+    load = pltpu.make_async_copy(w_ref.at[3], w, load_sem)
+    load.start()
     sums_ref[...] = jnp.zeros(sums_ref.shape, f32)
 
     def body(rows):
@@ -947,6 +1332,7 @@
         g = nn(attt_ref[...], gb[:, at : at + part]).astype(bf16)
         mine[i], theirs[i] = g[:half], g[half:]
         exchanges[i].start()
+    load.wait()
     column = lax.broadcasted_iota(jnp.int32, (HEADS, 128), 1)
     first = lax.broadcasted_iota(jnp.int32, (HEADS, 128), 0) * HD
     del_ref[...] = jnp.zeros(del_ref.shape, f32)
@@ -971,7 +1357,6 @@
 def qkv_grad_kernel(nt_ref, dq_ref, dko_ref, dkr_ref, all_ref, ka_ref, sa_ref, kb_ref, sb_ref, mine, theirs, came, sem):
     tokens, width = dq_ref.shape
     half, part = nt_ref.shape[0] // 2, mine.shape[-1]
-    meet_sibling()
 
     def join(rows):
         all_ref[rows, 0:width] = dq_ref[rows, :]
@@ -1000,10 +1385,10 @@
             store_blocks(i, total, half // 4, keep, send, cols)
 
 
-def normed_grad_kernel(g1_ref, g2_ref, wq_ref, wkv_ref, gn_ref, sums_ref, w, sem):
+def normed_grad_kernel(g1_ref, g2_ref, w_ref, gn_ref, sums_ref, w, sem):
     tokens, width = gn_ref.shape
     a, b = g1_ref.shape[1] // 3, g2_ref.shape[1] // 3
-    copies = [pltpu.make_async_copy(wq_ref, w.at[0], sem.at[0]), pltpu.make_async_copy(wkv_ref, w.at[pl.ds(1, 2)], sem.at[1])]
+    copies = [pltpu.make_async_copy(w_ref.at[2], w.at[0], sem.at[0]), pltpu.make_async_copy(w_ref.at[pl.ds(0, 2)], w.at[pl.ds(1, 2)], sem.at[1])]
     start_all(copies)
     sums_ref[...] = jnp.zeros(sums_ref.shape, f32)
 
@@ -1041,18 +1426,35 @@
     row_loop(tokens, body)
 
 
-def call(body, name, outs, scratch, flops, moved, *args, pieces=(), collective=None, far_outs=0):
-    params = {} if collective is None else {"collective_id": collective, "has_side_effects": True}
-    return pl.pallas_call(
-        body,
-        out_shape=tuple(sds(s, t) for s, t in outs),
-        in_specs=[VM] * len(args) + [ANY] * len(pieces),
-        out_specs=(VM,) * (len(outs) - far_outs) + (ANY,) * far_outs,
-        compiler_params=pltpu.CompilerParams(**params),
-        scratch_shapes=scratch,
+def carrying(body, counts, hops, relations, *refs):
+    refs, parts = list(refs), []
+    for n in counts:
+        parts.append([refs.pop(0) for _ in range(n)])
+    ins, hop_ins, outs, hop_outs, scratch, hop_scratch = parts
+    carried = list(zip(hops, hop_refs(hops, hop_ins, hop_outs, hop_scratch)))
+    greet(relations)
+    for h, r in carried:
+        h.start(*r)
+    body(*ins, *outs, *scratch)
+    for h, r in carried:
+        h.finish(*r)
+
+
+def call(body, name, outs, scratch, flops, moved, *args, pieces=(), far_outs=0, hops=(), relations=(), collective=0):
+    hop_ins, hop_outs, hop_scratch, hop_relations = hop_parts(hops)
+    relations = hop_relations | set(relations)
+    counts = (len(args) + len(pieces), len(hop_ins), len(outs), len(hop_outs), len(scratch), len(hop_scratch))
+    got = pl.pallas_call(
+        functools.partial(carrying, body, counts, hops, relations),
+        out_shape=tuple(sds(s, t) for s, t in outs) + tuple(hop_outs),
+        in_specs=[VM] * len(args) + [ANY] * (len(pieces) + len(hop_ins)),
+        out_specs=(VM,) * (len(outs) - far_outs) + (ANY,) * (far_outs + len(hop_outs)),
+        scratch_shapes=list(scratch) + hop_scratch,
+        compiler_params=pltpu.CompilerParams(**({"collective_id": collective, "has_side_effects": True} if relations else {})),
         cost_estimate=pl.CostEstimate(flops=flops, bytes_accessed=moved, transcendentals=0),
         name=name,
-    )(*args, *pieces)
+    )(*args, *pieces, *hop_ins)
+    return got[: len(outs)], hop_results(hops, got[len(outs) :])
 
 
 def swap(v, mask, size):
@@ -1063,147 +1465,55 @@
     return lax.optimization_barrier((v, *others))[0]
 
 
-def sums_kernel(shape, *refs):
-    terms, outs, at = refs[: sum(map(sum, shape))], refs[sum(map(sum, shape)) :], 0
-    for out, counts in zip(outs, shape):
-        for k, count in enumerate(counts):
-            total = terms[at][...].astype(f32)
-            for r in terms[at + 1 : at + count]:
-                total = total + r[...].astype(f32)
-            out[k] = total.astype(bf16)
-            at += count
-
-
-def add_blocks(name, *outs):
-    first = outs[0][0][0][0]
-    rows, cols = first.shape[-2:]
-    tile = max(t for t in range(128, 1025, 128) if cols % t == 0)
-    specs, args = [], []
-    for out in outs:
-        for terms in out:
-            for array, index in terms:
-                specs.append(pl.BlockSpec((None,) * len(index) + (rows, tile), lambda t, index=index: (*index, 0, t)))
-                args.append(array)
-    count = sum(len(out) for out in outs)
-    return pl.pallas_call(
-        functools.partial(sums_kernel, [[len(terms) for terms in out] for out in outs]),
-        grid=(cols // tile,),
-        in_specs=specs,
-        out_specs=tuple(pl.BlockSpec((len(out), rows, tile), lambda t: (0, 0, t)) for out in outs),
-        out_shape=tuple(sds((len(out), rows, cols), bf16) for out in outs),
-        cost_estimate=pl.CostEstimate(flops=len(args) * rows * cols, bytes_accessed=2 * (len(args) + count) * rows * cols, transcendentals=0),
-        name=name,
-    )(*args)
-
-
-def reduce_small(rows, size):
-    d = lax.axis_index("dp")
-    bit, left = 1, rows
-    while bit < size:
-        pairs = left.reshape(left.shape[0] // 2, 2, -1)
-        up = (d // bit) % 2 == 1
-        mine = jnp.where(up, pairs[:, 1], pairs[:, 0])
-        other = jnp.where(up, pairs[:, 0], pairs[:, 1])
-        left = mine + swap(other.astype(bf16), bit, size).astype(f32)
-        bit *= 2
-    for mask in (1, 2):
-        low = left.astype(bf16)
-        left = low.astype(f32) + lax.ppermute(low, "seq", [(i, i ^ mask) for i in range(4)]).astype(f32)
-    return left[0]
-
-
-def token_routes(size, depth):
-    routes = []
-    for s in range(2):
-        perm = []
-        for d in range(size):
-            for z in range(depth):
-                j = (z & 1) ^ s
-                to_d, to_z = (d & ~1) | (z >> 1), 2 * (d & 1) + j
-                perm.append((d * depth + z, to_d * depth + to_z))
-        routes.append(perm)
-    return routes
-
-
-def to_rows(v, routes):
-    odd = lax.axis_index("seq") % 2 == 1
-    first = jnp.where(odd, v[1], v[0])
-    second = jnp.where(odd, v[0], v[1])
-    r0 = lax.ppermute(first, ("dp", "seq"), routes[0])
-    r1 = lax.ppermute(second, ("dp", "seq"), routes[1])
-    return jnp.concatenate([jnp.where(odd, r1, r0), jnp.where(odd, r0, r1)], axis=0)
-
-
-def from_rows(v, routes):
-    odd = lax.axis_index("seq") % 2 == 1
-    half = v.shape[0] // 2
-    t0, t1 = v[:half], v[half:]
-    back = [[(b, a) for a, b in perm] for perm in routes]
-    r0 = lax.ppermute(jnp.where(odd, t1, t0), ("dp", "seq"), back[0])
-    r1 = lax.ppermute(jnp.where(odd, t0, t1), ("dp", "seq"), back[1])
-    return jnp.stack([jnp.where(odd, r1, r0), jnp.where(odd, r0, r1)])
-
-
 class Order:
     def __init__(self):
-        self.tail, self.meetings = None, 0
+        self.tail, self.count = None, 0
 
     def gate(self, v):
         return v if self.tail is None else after(v, self.tail)
 
-    def call(self, body, name, outs, scratch, flops, moved, first, *args, pieces=(), meets=False, far_outs=0):
-        self.meetings += meets
-        got = call(body, name, outs, scratch, flops, moved, self.gate(first), *args, pieces=pieces,
-                   collective=self.meetings if meets else None, far_outs=far_outs)
+    def call(self, body, name, outs, scratch, flops, moved, *args, **named):
+        self.count += 1
+        if args:
+            args = (self.gate(args[0]), *args[1:])
+        got, carried = call(body, name, outs, scratch, flops, moved, *args, collective=self.count, **named)
         self.tail = got[0]
-        return got
+        return (*got, *carried)
 
     def mlp(self, name, first, last, n2, *args, **named):
-        self.meetings += 1
-        got = mlp_call(name, first, last, self.gate(n2), *args, collective=self.meetings, **named)
+        self.count += 1
+        got, carried = mlp_call(name, first, last, self.gate(n2), *args, collective=self.count, **named)
         self.tail = got[2]
-        return got
-
-    def add(self, name, *outs):
-        (array, index), *terms = outs[0][0]
-        outs = ([[(self.gate(array), index), *terms], *outs[0][1:]], *outs[1:])
-        got = add_blocks(name, *outs)
-        self.tail = got[0]
-        return got
-
-
-class Reduction:
-    def __init__(self, name, order, size, keep_a, send_a, keep_b, send_b):
-        self.name, self.order, self.size = name, order, size
-        self.a, self.b = keep_a, keep_b
-        self.ax, self.by = swap(send_a, 2, size), swap(send_b, 4, size)
-
-    def second(self):
-        ta, tb = self.order.add(
-            "second" + self.name, [[(self.a, (1,)), (self.ax, (1,))]], [[(self.b, (1,)), (self.by, (1,))]]
-        )
-        self.ay, self.bx = swap(ta, 4, self.size), swap(tb, 2, self.size)
-
-    def third(self):
-        a = [(self.a, (0,)), (self.ax, (0,)), (self.ay, (0,))]
-        b = [(self.b, (0,)), (self.by, (0,)), (self.bx, (0,))]
-        self.own = self.order.add("third" + self.name, [a, b])[0]
-        self.inner = lax.ppermute(self.own, "seq", [(0, 1), (3, 2)])
-
-    def add_pair(self, name, a, b):
-        return self.order.add(name + self.name, [[(a, (i,)), (b, (i,))] for i in range(2)])[0]
-
-    def fourth(self):
-        self.half = self.add_pair("inner", self.own, self.inner)
-        self.across = lax.ppermute(self.half, "seq", [(1, 2), (2, 1)])
-
-    def fifth(self):
-        self.total = self.add_pair("total", self.half, self.across)
-        self.outer = lax.ppermute(self.total, "seq", [(1, 0), (2, 3)])
-
-    def result(self):
-        z = lax.axis_index("seq")
-        return jnp.where((z == 1) | (z == 2), self.total, self.order.gate(self.outer)).astype(f32)
+        return (*got, *carried)
+
+
+def small_kernel(rows_ref, out_ref, held, came, core_sem, x_sem, y_sem, z_sem):
+    d, z = here()
+    for i, m in enumerate(ORDER_SMALL):
+        held[i] = rows_ref[flipped_index(d, m)]
+    for sem, mask, count in ((core_sem, 1, 4), (x_sem, 2, 2), (y_sem, 4, 1)):
+        hop = remote(held.at[pl.ds(count, count)], came.at[pl.ds(count, count)], sem, across_links(mask))
+        hop.start()
+        hop.wait()
+        held[0:count] = held[0:count] + came[count : 2 * count]
+    sends, receives, partner = seq_step(INWARD)
+    hop = remote(held.at[0], came.at[0], z_sem, partner)
+
+    @pl.when(sends)
+    def _():
+        hop.start()
+        hop.wait_send()
+
+    out_ref[...] = held[0].astype(bf16)
+
+    @pl.when(receives)
+    def _():
+        hop.wait_recv()
+        out_ref[...] = (held[0] + came[0]).astype(bf16)
+
+
+def nothing_kernel(first_ref, out_ref):
+    out_ref[...] = jnp.zeros(out_ref.shape, f32)
 
 
 def by_rows(size, depth):
@@ -1214,7 +1524,6 @@
         tokens = patches.shape[0] * patches.shape[1]
         part = width // size
         z, core = lax.axis_index("seq"), lax.axis_index("dp") % 2
-        routes = token_routes(size, depth)
         order = Order()
         vm = pltpu.VMEM
         act, flip = ((tokens, width), bf16), ((width, tokens), bf16)
@@ -1223,9 +1532,8 @@
 
         small = jnp.stack([ln1_gain, ln1_bias, bias_qv[0], bias_qv[1], b_out, ln2_gain, ln2_bias, b_fc2])
         small = jnp.pad(small, ((0, 8), (0, width - part)))
-        bias = jnp.pad(b_fc1[None], ((0, 15), (0, width - ff // size)))
-        unit0 = jnp.stack([
-            jnp.concatenate([w_qkv[:, width : 2 * width], small]), jnp.concatenate([w_qkv[:, 2 * width :], bias])])
+        small = jnp.stack([small, jnp.pad(b_fc1[None], ((0, 15), (0, width - ff // size)))])[None]
+        unit0 = jnp.stack([w_qkv[:, width : 2 * width], w_qkv[:, 2 * width :]])
         unit1 = jnp.stack([w_qkv[:, :width], w_out])
         extra = -ff % 256
         tiles = (ff + extra) // 256
@@ -1233,18 +1541,6 @@
         w1 = jnp.pad(w_fc1, ((0, 0), (0, extra)))
         w2 = jnp.pad(w_fc2.T, ((0, 0), (0, extra)))
         hidden_units = [jnp.stack([w1[:, a:b], w2[:, a:b]]) for a, b in zip(ends, ends[1:])]
-
-        def straight(unit):
-            return swap(unit, 2, size), swap(unit, 4, size)
-
-        def corner(x, y):
-            return swap(y[0], 2, size), swap(x[1], 4, size)
-
-        x0, y0 = straight(unit0)
-        x = to_rows(patches, routes)
-        unit1, y0a, x0b = lax.optimization_barrier((unit1, y0[0], x0[1]))
-        p0 = (unit0, x0, y0, swap(y0a, 2, size), swap(x0b, 4, size))
-        x1, y1 = straight(unit1)
 
         ids = jnp.stack([picture_ids, jnp.where(valid_mask == 1, picture_ids, -1)])
         far_ids = swap(ids, 1, size)
@@ -1257,49 +1553,35 @@
         kid_row, kid_col = jnp.broadcast_to(keys[None], (8, 2 * tokens)), jnp.broadcast_to(keys[:, None], (2 * tokens, 128))
 
         dma = pltpu.SemaphoreType.DMA
-        n, kv, vec, b1, w_kv = order.call(
-            functools.partial(kv_kernel, ff), "kv",
-            [act, ((tokens, 2 * width), bf16), ((16, width), f32), ((16, ff + extra), f32), ((2, width, width), bf16)],
-            [vm((2, width, width), bf16), vm((2, 8, 16, width), bf16), dma((4, 3, 4)), dma],
-            2 * mm, 4 * width * width, x, pieces=p0, meets=True, far_outs=1)
-        far_kv = swap(kv, 1, size)
-        x1, y1 = order.gate(x1), order.gate(y1)
-        p1 = (unit1, x1, y1, *corner(x1, y1))
+        half_rows = (2, tokens // 2, width)
+        x, nt_, q, kv, vec, b1, far_kv, w_all = order.call(
+            functools.partial(entry_kernel, ff), "entry",
+            [act, flip, act, ((tokens, 2 * width), bf16), ((16, width), f32), ((16, ff + extra), f32),
+             ((tokens, 2 * width), bf16), ((4, width, width), bf16)],
+            [vm((4, width, width), bf16), vm((8, 2, 16, width), bf16), vm(half_rows, bf16), vm((tokens, width), bf16),
+             vm((width, tokens), bf16), dma((2, 7, 2, 2)), dma((7, 1, 2)), dma((3, 2)), dma((2, 2)), dma, dma((2, 2)), dma((2,))],
+            3 * mm, 8 * width * width, pieces=(unit0, small, unit1, patches), relations=(1, 2, 4, "rows"), far_outs=2)
         unit2, unit3, unit4 = hidden_units
-        unit2 = after(unit2, x1, y1)
-        x2, y2 = straight(unit2)
-        cot = to_rows(order.gate(cotangent), routes)
-        q, nt_, w_q, w_o = order.call(
-            q_kernel, "q", [act, flip, ((width, width), bf16), ((width, width), bf16)],
-            [vm((2, width, width), bf16), vm((width, tokens), bf16), dma((2, 3, 4)), dma((2,))],
-            mm, 2 * width * width, n, vec, pieces=p1, meets=True, far_outs=2)
         sc = 2 * tokens * 2 * tokens * WIN * HEADS
-        att, lse = order.call(
+        att, lse, (x2, y2), cot = order.call(
             attention_forward_kernel, "attention_forward", [act, ((HEADS, tokens), f32)],
             [vm((tokens, 2 * tokens), f32), vm((tokens, width), f32), vm((tokens, 128), f32)],
-            3 * sc, 8 * tokens * width, q, kv, far_kv, qid_col, kid_row)
-        x2, y2 = order.gate(x2), order.gate(y2)
-        p2 = (unit2, x2, y2, *corner(x2, y2))
-        unit3 = after(unit3, x2, y2)
-        x3, y3 = straight(unit3)
-        mid, n2, n2t, cott, attt = order.call(
+            3 * sc, 8 * tokens * width, q, kv, far_kv, qid_col, kid_row, hops=(Straight(unit2), Rows(cotangent)))
+        cot = cot.reshape(tokens, width)
+        mid, n2, n2t, cott, attt, (da2, db2) = order.call(
             middle_kernel, "middle", [act32, act, flip, flip, flip],
-            [vm((width, tokens), bf16)], mm, 2 * width * width, att, x, cot, vec, w_o)
+            [vm((width, tokens), bf16), vm((width, width), bf16), dma], mm, 2 * width * width, att, x, cot, vec,
+            pieces=(w_all,), hops=(Corner(x2, y2),))
 
         args = (cot, n2t, cott)
-        acc, gn, *grads1, gb1 = order.mlp("mlp0", True, False, n2, *args, b1, vec, mid, mid, p2, 0, ends[1])
-        x3, y3 = order.gate(x3), order.gate(y3)
-        p3 = (unit3, x3, y3, *corner(x3, y3))
-        unit4 = after(unit4, x3, y3)
-        x4, y4 = straight(unit4)
-        rest_cols = ends[3] - ends[1]
-        acc, gn, *grads2, gb2 = order.mlp("mlp1", False, False, n2, *args, b1, vec, acc, gn, p3, ends[1], rest_cols)
-        x4, y4 = order.gate(x4), order.gate(y4)
-        p4 = (unit4, x4, y4, *corner(x4, y4))
-        r1 = Reduction("1", order, size, *grads1)
-        out, gn, *grads2, gb3 = order.mlp(
-            "mlp2", False, True, n2, *args, b1, vec, acc, gn, p4, ends[2], rest_cols, into=grads2)
-        layer_out = from_rows(out, routes)
+        acc, gn, *grads1, gb1, chain = order.mlp(
+            "mlp0", True, False, n2, *args, b1, vec, mid, mid, (unit2, x2, y2, da2, db2), 0, hops=(Chain(unit3, unit4),))
+        x3, y3, da3, db3, x4, y4 = chain
+        acc, gn, *grads2, gb2, (da4, db4), p1 = order.mlp(
+            "mlp1", False, False, n2, *args, b1, vec, acc, gn, (unit3, x3, y3, da3, db3), ends[1],
+            hops=(Corner(x4, y4), First(*grads1)))
+        out, gn, *grads3, gb3, own1 = order.mlp(
+            "mlp2", False, True, n2, *args, b1, vec, acc, gn, (unit4, x4, y4, da4, db4), ends[2], hops=(Second(p1),))
 
         part_o = (width // 256 + 1) * 128
 
@@ -1309,82 +1591,76 @@
         def exchanged(columns):
             return [vm((2, width // 2, columns), bf16)] * 3 + [dma((3, 2))]
 
-        gm, ga, sums2, inner, *gradso = order.call(
+        gm, ga, sums2, inner, *gradso, p2, layer_out = order.call(
             branch_kernel, "branch", [act32, act, ((8, width), f32), ((HEADS, tokens), f32), *gradient(part_o)],
-            [vm((tokens, width), bf16), *exchanged(part_o)], 2 * mm, 4 * width * width,
-            cot, gn, mid, vec, att, attt, w_o, meets=True)
+            [vm((tokens, width), bf16), *exchanged(part_o), vm((width, width), bf16), dma], 2 * mm, 4 * width * width,
+            cot, gn, mid, vec, att, attt, pieces=(w_all,), relations=(1,),
+            hops=(First(*grads2), Rows(out.reshape(half_rows))))
         cut_head = (HEADS + 2) // 2
         cut_col = cut_head * HD // 128 * 128
 
-        def attention_backward(name, h0, h1, base, done, span, carry):
+        def attention_backward(name, h0, h1, base, done, span, carry, hops):
             share = 3 * sc * (h1 - h0) // HEADS * 2
             return order.call(
                 functools.partial(attention_backward_kernel, h0, h1, base, done), name,
-                [((tokens, done), bf16), ((tokens, 2 * done), f32), ((tokens, 2 * done), bf16),
-                 ((5, tokens if span > done else 8, 128), f32)],
-                [vm((2 * tokens, tokens), f32), vm((5, tokens, span), f32)],
-                share, 16 * tokens * width, q, kv, far_kv, ga, lse, inner, kid_col, qid_row, carry)
-
-        def qkv_grad(name, dq, dkn, dkr):
+                [((tokens, done), bf16), ((tokens, 2 * done), f32), ((5, tokens if span > done else 8, 128), f32),
+                 ((tokens, 2 * done), bf16)],
+                [vm((2 * tokens, tokens), f32), vm((5, tokens, span), f32), vm((tokens, 2 * done), bf16), dma((2,))],
+                share, 16 * tokens * width, q, kv, far_kv, ga, lse, inner, kid_col, qid_row, carry,
+                relations=(1,), far_outs=1, hops=hops)
+
+        def qkv_grad(name, dq, dkn, dkr, hops):
             columns = 3 * dq.shape[1]
             share = (columns + 511) // 512 * 256
-            got, *grads = order.call(
+            got, *rest = order.call(
                 qkv_grad_kernel, name, [((tokens, columns), bf16), *gradient(share)], exchanged(share),
-                mm * columns // width, 4 * width * columns, nt_, dq, dkn, dkr, meets=True)
-            return got, grads
-
-        dqa, dna, dfa, carry = attention_backward("attention_backward_a", 0, cut_head, 0, cut_col, cut_col + 128, inner)
-        dra = swap(dfa, 1, size)
-        r1.second()
-        r2 = Reduction("2", order, size, *grads2)
-        gra, gradsa = qkv_grad("qkv_grad_a", dqa, dna, dra)
-        dqb, dnb, dfb, _ = attention_backward(
-            "attention_backward_b", cut_head, HEADS, cut_col, width - cut_col, width - cut_col, carry)
-        drb = swap(dfb, 1, size)
-        r1.third()
-        r2.second()
-        ro = Reduction("o", order, size, *gradso)
-        qa = Reduction("qa", order, size, *gradsa)
-        grb, gradsb = qkv_grad("qkv_grad_b", dqb, dnb, drb)
-        qb = Reduction("qb", order, size, *gradsb)
-        gnq, sums0 = order.call(
+                mm * columns // width, 4 * width * columns, nt_, dq, dkn, dkr, relations=(1,), hops=hops)
+            return got, rest[:4], *rest[4:]
+
+        dqa, dna, carry, dra, own2, p3, in1 = attention_backward(
+            "attention_backward_a", 0, cut_head, 0, cut_col, cut_col + 128, inner, (Second(p2), First(*grads3), Seq(INWARD, own1)))
+        gra, gradsa, own3, po, mid1a, in2a = qkv_grad(
+            "qkv_grad_a", dqa, dna, dra, (Second(p3), First(*gradso), Seq(MIDDLE, in1, 0), Seq(INWARD, own2, 0)))
+        dqb, dnb, _, drb, owno, pa, mid1b, in2b, in3 = attention_backward(
+            "attention_backward_b", cut_head, HEADS, cut_col, width - cut_col, width - cut_col, carry,
+            (Second(po), First(*gradsa), Seq(MIDDLE, in1, 1), Seq(INWARD, own2, 1), Seq(INWARD, own3)))
+        grb, gradsb, owna, mid2a, out1a, ino = qkv_grad(
+            "qkv_grad_b", dqb, dnb, drb, (Second(pa), Seq(MIDDLE, in2a), Seq(OUTWARD, mid1a), Seq(INWARD, owno)))
+        gnq, sums0, pb, mid2b, out1b, ina = order.call(
             normed_grad_kernel, "normed_grad", [act32, ((8, width), f32)],
-            [vm((3, width, width), bf16), dma((2,))], 3 * mm, 6 * width * width, gra, grb, pieces=(w_q, w_kv))
-        r1.fourth()
-        r2.third()
-        gx, sums1 = order.call(input_grad_kernel, "input_grad", [act, ((8, width), f32)], [], 10**7, 12 * tokens * width,
-                               gnq, x, gm, vec)
-        gx_rows = (gx, routes)
-        ro.second()
-        qa.second()
-        r1.fifth()
-        r2.fourth()
-        qb.second()
-        ro.third()
-        qa.third()
-        grad_patches = from_rows(*gx_rows)
+            [vm((3, width, width), bf16), dma((2,))], 3 * mm, 6 * width * width, gra, grb, pieces=(w_all,),
+            hops=(First(*gradsb), Seq(MIDDLE, in2b), Seq(OUTWARD, mid1b), Seq(INWARD, owna)))
+        gx, sums1, ownb, mid3, out2a = order.call(
+            input_grad_kernel, "input_grad", [act, ((8, width), f32)], [], 10**7, 12 * tokens * width, gnq, x, gm, vec,
+            hops=(Second(pb), Seq(MIDDLE, in3), Seq(OUTWARD, mid2a)))
+
         bias_grads = jnp.concatenate([gb1, gb2, gb3], axis=1)[:, :ff].reshape(size, ff // size)
         vecs = jnp.concatenate([sums1[:2], sums0[:2], sums2[:4]]).reshape(8, size, part)
-        tiny = reduce_small(jnp.concatenate([jnp.moveaxis(vecs, 0, 1).reshape(size, 8 * part), bias_grads], axis=1), size)
+        rows = jnp.concatenate([jnp.moveaxis(vecs, 0, 1).reshape(size, 8 * part), bias_grads], axis=1)
+        lanes = rows.shape[1]
+        rows = jnp.pad(rows, ((0, 0), (0, -lanes % 2048))).reshape(size, -1, 128)
+        few = rows.shape[1:]
+        tiny, grad_patches, inb, mido, mida, out2b, out3 = order.call(
+            small_kernel, "small", [(few, bf16)], [vm((8, *few), f32), vm((8, *few), f32)] + [dma((2,))] * 4, 10**6, 10**6, rows,
+            relations=(1, 2, 4, "z"),
+            hops=(Rows(gx.reshape(half_rows)), Seq(INWARD, ownb), Seq(MIDDLE, ino), Seq(MIDDLE, ina), Seq(OUTWARD, mid2b), Seq(OUTWARD, mid3)))
+        _, tiny, midb, outo, outa = order.call(
+            nothing_kernel, "middle_sums", [((8, 128), f32)], [], 10**6, 10**6, tiny,
+            hops=(Seq(MIDDLE, tiny), Seq(MIDDLE, inb), Seq(OUTWARD, mido), Seq(OUTWARD, mida)))
+        _, tiny, outb = order.call(
+            nothing_kernel, "outer_sums", [((8, 128), f32)], [], 10**6, 10**6, _, hops=(Seq(OUTWARD, tiny), Seq(OUTWARD, midb)))
+        tiny = tiny.reshape(-1)[:lanes].astype(f32)
         mine, grad_b_fc1 = tiny[: 8 * part].reshape(8, part), tiny[8 * part :]
-        r2.fifth()
-        qb.third()
-        ro.fourth()
-        qa.fourth()
-        ro.fifth()
-        qa.fifth()
-        qb.fourth()
-        qb.fifth()
-        g1, g2, go, ga_, gb_ = [r.result() for r in (r1, r2, ro, qa, qb)]
-        left = ff - ends[1]
-        w1g = jnp.concatenate([g1[0], g2[0][:, :left]], axis=1)
-        w2g = jnp.concatenate([g1[1], g2[1][:, :left]], axis=1).T
-        wog = jnp.concatenate([go[0], go[1][:, 2 * part_o - width :]], axis=1)
+        left = ff - ends[2]
+        w1g = jnp.concatenate([out1a, out2a, out3[0][:, :left]], axis=1).astype(f32)
+        w2g = jnp.concatenate([out1b, out2b, out3[1][:, :left]], axis=1).T.astype(f32)
+        wog = jnp.concatenate([outo[0], outo[1][:, 2 * part_o - width :]], axis=1).astype(f32)
 
         def joined(g, columns):
             return jnp.concatenate([g[0], g[1][:, 2 * g.shape[2] - columns :]], axis=1).reshape(part, 3, columns // 3)
 
-        wqg = jnp.concatenate([joined(ga_, 3 * cut_col), joined(gb_, 3 * (width - cut_col))], axis=2).reshape(part, 3 * width)
+        wqg = jnp.concatenate([joined(outa, 3 * cut_col), joined(outb, 3 * (width - cut_col))], axis=2)
+        wqg = wqg.reshape(part, 3 * width).astype(f32)
         return (layer_out, grad_patches, mine[0], mine[1], wqg, mine[2:4], wog, mine[6], mine[4], mine[5], w1g, grad_b_fc1, w2g, mine[7])
 
     return step

time: 668 us -> 542 us (0.81); the launches traced: 660 us -> 541 us
  Pallas kernels: 319 us -> 506 us
  starting transfers between devices: 146 us -> 0.45 us
  waiting for transfers between devices: 117 us -> 0.01 us
  other arithmetic: 34.3 us -> 11.9 us
  local copies, waits for them, and re-layouts: 41.1 us -> 21.9 us
    pallas_call x34 -> x16, Pallas kernels: 319 us -> 506 us  [the longest x13 386 us: call(): pl.pallas_call(functools.partial(carrying, body, counts, hops, relations)...]
    ppermute x25 -> x0, starting transfers between devices: 97.5 us -> none  [the longest x5 41.7 us: third(): self.inner = lax.ppermute(self.own, 'seq', [(0, 1), (3, 2)])]
    ppermute x47 -> x1, waiting for transfers between devices: 58.9 us -> 0.01 us  [swap(): return lax.ppermute(v, 'dp', [(i, i ^ mask) for i in range(size)])]
    ppermute x25 -> x0, waiting for transfers between devices: 57.8 us -> none  [the longest x5 37.9 us: fifth(): self.outer = lax.ppermute(self.total, 'seq', [(1, 0), (2, 3)])]
    ppermute x47 -> x1, starting transfers between devices: 48.7 us -> 0.45 us  [swap(): return lax.ppermute(v, 'dp', [(i, i ^ mask) for i in range(size)])]
    squeeze x13 -> x2, local copies, waits for them, and re-layouts: 11.8 us -> 0.06 us  [the longest x1 0.03 us: step(): outo[0]]
    select_n x9 -> x0, other arithmetic: 11 us -> none  [the longest x2 4.74 us: from_rows(): r1 = lax.ppermute(jnp.where(odd, t0, t1), ('dp', 'seq'), back[1])]
    unnamed x136 -> x58, local copies, waits for them, and re-layouts: 14.8 us -> 7.6 us
  transfers between devices with their start and end apart: 72 -> 1, of which waited for: 19 -> 0; matrix products, arithmetic and copies ran while one was open for 8% -> 2% of each run, Pallas kernels for 39% -> 11%
where the time goes in v3:
time: 542 us; the launch traced here: 541 us
  Pallas kernels  506 us (93%)
  local copies, waits for them, and re-layouts  21.9 us (4%)
  other arithmetic  11.9 us (2%)
    pallas_call x13, Pallas kernels, call(): pl.pallas_call(functools.partial(carrying, body, counts, hops, relations)...  386 us
    pallas_call x3, Pallas kernels, mlp_call(): pl.pallas_call(functools.partial(mlp_kernel, first, last, hops), grid=(st...  120 us
  transfers between devices with their start and end apart: 1, of which 0 were waited for; matrix products, arithmetic and copies ran while one was open for 2% of the time, Pallas kernels for 11%

profile of v3, /device:TPU:0, one launch (start us, length us, event | category | flops | bytes accessed | tf_op | source)
XLA Modules:
  0.0 541.3 jit_solution(14590851531932865078)
XLA Ops:
  0.7 0.8 fusion.5
  2.6 1.4 slice_bitcast_fusion
  4.0 1.2 slice_bitcast_fusion.2
  5.5 1.2 copy-done.4
  12.2 1.1 pad_maximum_fusion.refs_5_.rest_0_
  13.3 1.0 pad_maximum_fusion.1.rest_5_.rest_0_
  14.3 1.2 pad_maximum_fusion.2
  15.5 61.3 %entry.1 = (bf16[512,1152]{1,0:T(8,128)(2,1)}, bf16[1152,512]{1,0:T(8,128)(2,1)}, bf16[512,1152]{1,0:T(8,128)(2,1)}, bf16[512,2304]{1,0:T(8,128)(2,1)}, f32[16,1...) custom-call(bf16[2,144,1152]{2,1,0:T(8,128)(2,1)} %get-tuple-element.300.refs_0_, ...), custom_call_target="tpu_custom_call" | custom-call | flops 4076863488 | bytes 10616832 | tf_op jit(solution)/shard_map/entry/pallas_call | solution.py:1447
  76.8 0.8 pad_maximum_fusion.5.rest_6_.rest_0_
  78.4 0.8 broadcast_in_dim.38.refs_3_
  79.2 32.9 %attention_forward.1 = (bf16[512,1152]{1,0:T(8,128)(2,1)}, f32[16,512]{1,0:T(8,128)}, bf16[2,144,2048]{2,1,0:T(8,128)(2,1)}, bf16[2,144,2048]{2,1,0:T(8,128)(2,1)}, bf16[2,256,1152]{2,1,0:T(8,128)(2,1)}) custom-call(bf16[512,1152]{1,0:T(8,128)(2,1)} %get-tuple-element.218.refs_0_, bf16[512,2304]{1,0:T(8,128)(2,1)} %get-tuple-element.149.refs_1_, ...), custom_call_target="tpu_custom_call" | custom-call | flops 12884901888 | bytes 4718592 | tf_op jit(solution)/shard_map/attention_forward/pallas_call | solution.py:1447
  112.1 20.6 %middle.1 = (f32[512,1152]{1,0:T(8,128)}, bf16[512,1152]{1,0:T(8,128)(2,1)}, bf16[1152,512]{1,0:T(8,128)(2,1)}, bf16[1152,512]{1,0:T(8,128)(2,1)}, bf16[1152,512...) custom-call(bf16[512,1152]{1,0:T(8,128)(2,1)} %get-tuple-element.153.refs_0_.refs_4_, ...), custom_call_target="tpu_custom_call" | custom-call | flops 1358954496 | bytes 2654208 | tf_op jit(solution)/shard_map/middle/pallas_call | solution.py:1447
  132.7 53.5 %mlp0.1 = (f32[512,1152]{1,0:T(8,128)}, f32[512,1152]{1,0:T(8,128)}, bf16[2,144,2048]{2,1,0:T(8,128)(2,1)}, bf16[2,144,2048]{2,1,0:T(8,128)(2,1)}, bf16[2,144,20...) custom-call(bf16[512,1152]{1,0:T(8,128)(2,1)} %get-tuple-element.180, ...), custom_call_target="tpu_custom_call" | custom-call | flops 14495514624 | bytes 25952256 | tf_op jit(solution)/shard_map/mlp0/pallas_call | solution.py:1252
  186.2 42.7 %mlp1.1 = (f32[512,1152]{1,0:T(8,128)}, f32[512,1152]{1,0:T(8,128)}, bf16[2,144,1536]{2,1,0:T(8,128)(2,1)}, bf16[2,144,1536]{2,1,0:T(8,128)(2,1)}, bf16[2,144,15...) custom-call(bf16[512,1152]{1,0:T(8,128)(2,1)} %get-tuple-element.180, ...), custom_call_target="tpu_custom_call" | custom-call | flops 10871635968 | bytes 21233664 | tf_op jit(solution)/shard_map/mlp1/pallas_call | solution.py:1252
  228.9 23.9 %mlp2.1 = (bf16[512,1152]{1,0:T(8,128)(2,1)}, f32[512,1152]{1,0:T(8,128)}, bf16[2,144,768]{2,1,0:T(8,128)(2,1)}, bf16[2,144,768]{2,1,0:T(8,128)(2,1)}, bf16[2,14...) custom-call(bf16[512,1152]{1,0:T(8,128)(2,1)} %get-tuple-element.180.n2_re, ...), custom_call_target="tpu_custom_call" | custom-call | flops 5435817984 | bytes 14155776 | tf_op jit(solution)/shard_map/mlp2/pallas_call | solution.py:1252
  252.8 31.1 %branch.1 = (f32[512,1152]{1,0:T(8,128)}, bf16[512,1152]{1,0:T(8,128)(2,1)}, f32[8,1152]{1,0:T(8,128)}, f32[16,512]{1,0:T(8,128)}, bf16[2,144,640]{2,1,0:T(8,128...) custom-call(bf16[512,1152]{1,0:T(8,128)(2,1)} %bitcast.69, ...), custom_call_target="tpu_custom_call" | custom-call | flops 2717908992 | bytes 5308416 | tf_op jit(solution)/shard_map/branch/pallas_call | solution.py:1447
  283.9 1.0 broadcast_in_dim.40.refs_6_
  285.5 34.3 %attention_backward_a.1 = (bf16[512,640]{1,0:T(8,128)(2,1)}, f32[512,1280]{1,0:T(8,128)}, f32[5,512,128]{2,1,0:T(8,128)}, bf16[512,1280]{1,0:T(8,128)(2,1)}, bf1...) custom-call(bf16[512,1152]{1,0:T(8,128)(2,1)} %get-tuple-element.218.refs_0_, ...), custom_call_target="tpu_custom_call" | custom-call | flops 14495514624 | bytes 9437184 | tf_op jit(solution)/shard_map/attention_backward_a/pallas_call | solution.py:1447
  319.8 25.2 %qkv_grad_a.1 = (bf16[512,1920]{1,0:T(8,128)(2,1)}, bf16[2,144,1024]{2,1,0:T(8,128)(2,1)}, bf16[2,144,1024]{2,1,0:T(8,128)(2,1)}, bf16[2,144,1024]{2,1,0:T(8,128...) custom-call(bf16[1152,512]{1,0:T(8,128)(2,1)} %get-tuple-element.227, ...), custom_call_target="tpu_custom_call" | custom-call | flops 2264924160 | bytes 8847360 | tf_op jit(solution)/shard_map/qkv_grad_a/pallas_call | solution.py:1447
  345.1 29.5 %attention_backward_b.1 = (bf16[512,512]{1,0:T(8,128)(2,1)}, f32[512,1024]{1,0:T(8,128)}, f32[5,8,128]{2,1,0:T(8,128)}, bf16[512,1024]{1,0:T(8,128)(2,1)}, bf16[...) custom-call(bf16[512,1152]{1,0:T(8,128)(2,1)} %get-tuple-element.218, ...), custom_call_target="tpu_custom_call" | custom-call | flops 11274289152 | bytes 9437184 | tf_op jit(solution)/shard_map/attention_backward_b/pallas_call | solution.py:1447
  374.6 21.9 %qkv_grad_b.1 = (bf16[512,1536]{1,0:T(8,128)(2,1)}, bf16[2,144,768]{2,1,0:T(8,128)(2,1)}, bf16[2,144,768]{2,1,0:T(8,128)(2,1)}, bf16[2,144,768]{2,1,0:T(8,128)(2...) custom-call(bf16[1152,512]{1,0:T(8,128)(2,1)} %get-tuple-element.227, ...), custom_call_target="tpu_custom_call" | custom-call | flops 1811939328 | bytes 7077888 | tf_op jit(solution)/shard_map/qkv_grad_b/pallas_call | solution.py:1447
  396.5 19.8 %normed_grad.1 = (f32[512,1152]{1,0:T(8,128)}, f32[8,1152]{1,0:T(8,128)}, bf16[2,2,144,768]{3,2,1,0:T(8,128)(2,1)}, bf16[144,1536]{1,0:T(8,128)(2,1)}, bf16[144,...) custom-call(bf16[512,1920]{1,0:T(8,128)(2,1)} %get-tuple-element.235.refs_0_, ...), custom_call_target="tpu_custom_call" | custom-call | flops 4076863488 | bytes 7962624 | tf_op jit(solution)/shard_map/normed_grad/pallas_call | solution.py:1447
  416.4 15.1 %input_grad.1 = (bf16[512,1152]{1,0:T(8,128)(2,1)}, f32[8,1152]{1,0:T(8,128)}, bf16[2,144,768]{2,1,0:T(8,128)(2,1)}, bf16[2,144,768]{2,1,0:T(8,128)(2,1)}, bf16[144,1536]{1,0:T(8,128)(2,1)}) custom-call(f32[512,1152]{1,0:T(8,128)} %get-tuple-element.243.refs_0_, bf16[512,1152]{1,0:T(8,128)(2,1)} %get-tuple-element.147.refs_1_, ...), custom_call_target="tpu_custom_call" | custom-call | flops 10000000 | bytes 7077888 | tf_op jit(solution)/shard_map/input_grad/pallas_call | solution.py:1447
  434.2 44.5 %small.1 = (bf16[16,128]{1,0:T(8,128)(2,1)}, bf16[2,256,1152]{2,1,0:T(8,128)(2,1)}, bf16[2,144,768]{2,1,0:T(8,128)(2,1)}, bf16[2,144,640]{2,1,0:T(8,128)(2,1)}, ...) custom-call(f32[8,16,128]{2,1,0:T(8,128)} %bitcast.79, ...), custom_call_target="tpu_custom_call" | custom-call | flops 1000000 | bytes 1000000 | tf_op jit(solution)/shard_map/small/pallas_call | solution.py:1447
  478.7 34.6 %middle_sums.1 = (f32[8,128]{1,0:T(8,128)}, bf16[16,128]{1,0:T(8,128)(2,1)}, bf16[2,144,768]{2,1,0:T(8,128)(2,1)}, bf16[2,144,640]{2,1,0:T(8,128)(2,1)}, bf16[2,144,1024]{2,1,0:T(8,128)(2,1)}) custom-call(bf16[16,128]{1,0:T(8,128)(2,1)} %get-tuple-element.262.refs_0_.refs_1_, bf16[16,128]{1,0:T(8,128)(2,1)} %get-tuple-element.262.refs_0_.refs_1_, ...), custom_call_target="tpu_custom_call" | custom-call | flops 1000000 | bytes 1000000 | tf_op jit(solution)/shard_map/middle_sums/pallas_call | solution.py:1447
  513.4 14.8 %outer_sums.1 = (f32[8,128]{1,0:T(8,128)}, bf16[16,128]{1,0:T(8,128)(2,1)}, bf16[2,144,768]{2,1,0:T(8,128)(2,1)}) custom-call(f32[8,128]{1,0:T(8,128)} %get-tuple-element.266.refs_0_, bf16[16,128]{1,0:T(8,128)(2,1)} %get-tuple-element.267.refs_1_, bf16[2,144,768]{2,1,0:T(8,128)(2,1)} %get-tuple-element.268.refs_2_), custom_call_target="tpu_custom_call" | custom-call | flops 1000000 | bytes 1000000 | tf_op jit(solution)/shard_map/outer_sums/pallas_call | solution.py:1447
  532.4 1.4 copy.33
  534.5 0.9 maximum_convert_fusion.2
  535.4 1.6 convert_bitcast_fusion
  537.0 1.6 maximum_convert_fusion.1
  538.7 1.0 copy.38
  540.3 1.0 copy.39
  (103 shorter events, 16.2 us)
Async XLA Ops:
  0.6 3.4 copy-start
  2.2 75.4 %collective-permute-start = (s32[2,2,1024]{2,1,0:T(2,128)S(1)}, s32[2,2,1024]{2,1,0:T(2,128)S(1)}, u32[]{:S(2)}, u32[]{:S(2)}) collective-permute-start(s32[2,2,1024]{2,1,0:T(2,128)S(1)} %pad_add_fusion), channel_id=1, source_target_pairs={{0,4},{4,0},{8,12},{12,8},{16,20},{20,16},{24,28},{28,24},{1,5},{5... | collective-permute-start | bytes 49160 | tf_op jit(solution)/shard_map/ppermute | solution.py:1461
  4.0 1.4 copy-start.1
  5.4 1.2 copy-start.4
  6.6 0.7 copy-start.21
  6.6 1.2 copy-start.22
  6.7 1.8 copy-start.23
  6.7 2.4 copy-start.24
  6.7 2.9 copy-start.25
  6.7 3.5 copy-start.26
  6.7 4.0 copy-start.19
  6.7 4.0 copy-start.20
  13.3 1.0 copy-start.13
  15.5 62.1 %copy-start.14 = (s32[2,1024]{1,0:T(2,128)S(1)}, s32[2,1024]{1,0:T(2,128)}, u32[]{:S(2)}) copy-start(s32[2,1024]{1,0:T(2,128)} %param.17) | copy-start | bytes 24580
  416.4 16.7 %copy-start.15 = (f32[8,1152]{1,0:T(8,128)S(1)}, f32[8,1152]{1,0:T(8,128)}, u32[]{:S(2)}) copy-start(f32[8,1152]{1,0:T(8,128)} %get-tuple-element.249) | copy-start | bytes 110596
  416.4 17.0 %copy-start.16 = (f32[1,2048]{1,0:T(1,128)S(1)}, f32[1,2048]{1,0:T(1,128)}, u32[]{:S(2)}) copy-start(f32[1,2048]{1,0:T(1,128)} %get-tuple-element.250) | copy-start | bytes 24580
  416.4 17.0 %copy-start.17 = (f32[1,1536]{1,0:T(1,128)S(1)}, f32[1,1536]{1,0:T(1,128)}, u32[]{:S(2)}) copy-start(f32[1,1536]{1,0:T(1,128)} %get-tuple-element.251) | copy-start | bytes 18436
  416.4 17.0 %copy-start.18 = (f32[1,768]{1,0:T(1,128)S(1)}, f32[1,768]{1,0:T(1,128)}, u32[]{:S(2)}) copy-start(f32[1,768]{1,0:T(1,128)} %get-tuple-element.252) | copy-start | bytes 9220
  478.7 51.5 %copy-start.10 = (bf16[2,144,768]{2,1,0:T(8,128)(2,1)S(1)}, bf16[2,144,768]{2,1,0:T(8,128)(2,1)}, u32[]{:S(2)}) copy-start(bf16[2,144,768]{2,1,0:T(8,128)(2,1)} %get-tuple-element.275) | copy-start | bytes 1327108
  513.4 16.9 %copy-start.12 = (bf16[2,144,640]{2,1,0:T(8,128)(2,1)S(1)}, bf16[2,144,640]{2,1,0:T(8,128)(2,1)}, u32[]{:S(2)}) copy-start(bf16[2,144,640]{2,1,0:T(8,128)(2,1)} %get-tuple-element.272) | copy-start | bytes 1105924
  513.4 17.0 %copy-start.7 = (bf16[2,144,1024]{2,1,0:T(8,128)(2,1)S(1)}, bf16[2,144,1024]{2,1,0:T(8,128)(2,1)}, u32[]{:S(2)}) copy-start(bf16[2,144,1024]{2,1,0:T(8,128)(2,1)} %get-tuple-element.270) | copy-start | bytes 1769476
  530.4 1.0 copy-start.11
  532.4 3.0 copy-start.9
  533.8 1.5 copy-start.6
  535.4 1.6 copy-start.5
  535.4 1.6 copy-start.8
  537.0 1.7 copy-start.2
  538.6 1.7 copy-start.3
